TPU v7x, 32 devices: a whole 2x2x4 slice. The times are simulated.
32 devices in a mesh: seq: 2 (over x), shard: 16 (over z, y, core).
Axes of the slice: x: 2, y: 2, z: 4, core: 2. Of those that a mesh axis runs over, the one named last changes fastest.
Arguments:
- layer_input: bfloat16 [16, 256, 2048], P('shard', 'seq'), may hold values from -6 to 6
- seq_lengths: int32 [16, 3], P('shard'), may hold values from 1 to 192, 256 in all within a row
- seq_order: int32 [16, 3], P('shard'), may hold values from 0 to 2, each once within a row
- expert_ids: int32 [16, 256, 8], P('shard', 'seq'), may hold values from 0 to 15, all different within a row; in each aligned block of 128 rows (0 to 127, 128 to 255, ..., all dimensions but the last counted through in order) at most 96 rows name the same one
- expert_probs: float32 [16, 256, 8], P('shard', 'seq'), may hold values from 0.05 to 0.3
- weight_qkv: bfloat16 [2048, 6144], P('shard'), may hold values from -0.125 to 0.125
- weight_out: bfloat16 [2048, 2048], P('shard'), may hold values from -1.5 to 1.5
- norm_gains: bfloat16 [2048, 4], P('shard'), may hold values from 0.25 to 1.75
- weight_gate: bfloat16 [16, 2048, 1024], P('shard'), may hold values from -0.125 to 0.125
- weight_up: bfloat16 [16, 2048, 1024], P('shard'), may hold values from -0.125 to 0.125
- weight_down: bfloat16 [16, 1024, 2048], P('shard'), may hold values from -0.75 to 0.75
- out_cotangent: bfloat16 [16, 256, 2048], P('shard', 'seq'), may hold values from -6 to 6
Outputs:
- layer_output: bfloat16 [16, 256, 2048], P('shard', 'seq')
- input_grad: bfloat16 [16, 256, 2048], P('shard', 'seq')
- grad_qkv: float32 [2048, 6144], P('shard')
- grad_out: float32 [2048, 2048], P('shard')
- grad_gains: float32 [2048, 4], P('shard')
- grad_gate: float32 [16, 2048, 1024], P('shard', 'seq')
- grad_up: float32 [16, 2048, 1024], P('shard', 'seq')
- grad_down: float32 [16, 1024, 2048], P('shard', 'seq')
Inputs may be any that keep to these rules, and one draw needn't show every extreme that they name: `seq_lengths`: in each group the 3 lengths add up to 256, and the longest is exactly 192. `seq_order`: each group's row is a permutation of 0 to 2. `expert_ids`: each token names 8 different experts. Among the 128 tokens of one device (aligned blocks of 128 tokens in order of group and position) no expert is named more than 96 times, and in every draw some expert is named exactly 96 times within some block.
All inputs are finite; a program needn't handle non-finite values.
Results may differ from a plain program's by a relative error of at most 0.02.
Values may be sent and summed in bfloat16 or wider, within the bound.
A program may use at most 320 MiB of HBM per device.

v0:
```python
import jax
import jax.numpy as jnp
from jax import lax
from jax.sharding import PartitionSpec as P

HEADS = 16
HEAD_DIM = 128


norm_eps = 1e-05
rope_base = 10000.0


def rms_scale(values, gain_col):
    return (
        values * lax.rsqrt(jnp.mean(values * values, axis=-1, keepdims=True) + norm_eps) * gain_col
    )


def rotate(values, cosine, sine_part):
    half_dim = values.shape[-1] // 2
    first_half = values[..., :half_dim]
    second_half = values[..., half_dim:]
    return jnp.concatenate(
        [
            first_half * cosine - second_half * sine_part,
            second_half * cosine + first_half * sine_part,
        ],
        axis=-1,
    )


def rope_tables(position, head_size):
    half_dim = head_size // 2
    frequency = rope_base ** (-2.0 * jnp.arange(half_dim, dtype=jnp.float32) / head_size)
    angles = position.astype(jnp.float32)[:, None] * frequency[None, :]
    return (jnp.cos(angles)[:, None, :], jnp.sin(angles)[:, None, :])


def group_layout(lengths, seq_perm, group_tok):
    seq_count = lengths.shape[0]
    numbers = jnp.arange(seq_count, dtype=jnp.int32)
    packed = jnp.sum(jnp.where(seq_perm[:, None] == numbers[None, :], lengths[None, :], 0), axis=1)
    seq_ends = jnp.cumsum(packed)
    seq_starts = seq_ends - packed
    places = jnp.arange(group_tok, dtype=jnp.int32)
    segment = jnp.sum((places[:, None] >= seq_ends[None, :]).astype(jnp.int32), axis=1)
    begins = jnp.sum(
        jnp.where(segment[:, None] == numbers[None, :], seq_starts[None, :], 0), axis=1
    )
    return (segment, places - begins)


def slot_tables(expert_list, expert_count, capacity):
    rows_here, top_count = expert_list.shape
    flat_ids = expert_list.reshape(-1)
    onehot = (flat_ids[:, None] == jnp.arange(expert_count, dtype=jnp.int32)[None, :]).astype(
        jnp.int32
    )
    slot_rank = jnp.sum((jnp.cumsum(onehot, axis=0) - 1) * onehot, axis=1)
    slot_index = flat_ids * capacity + slot_rank
    owners = jnp.arange(rows_here * top_count, dtype=jnp.int32) // top_count
    sources = (
        jnp.full((expert_count * capacity,), rows_here, dtype=jnp.int32).at[slot_index].set(owners)
    )
    return (sources, slot_index)


def contract_rows(left_side, right_side):
    return lax.dot_general(
        left_side, right_side, (((0,), (0,)), ((), ())), preferred_element_type=jnp.float32
    )


def contract_cols(left_side, right_side):
    return lax.dot_general(
        left_side, right_side, (((1,), (1,)), ((), ())), preferred_element_type=jnp.float32
    )


def shards(
    layer_input,
    seq_lengths,
    seq_order,
    expert_ids,
    expert_probs,
    weight_qkv,
    weight_out,
    norm_gains,
    weight_gate,
    weight_up,
    weight_down,
    out_cotangent,
):
    model_width = layer_input.shape[-1]
    tok_rows = layer_input.shape[1]
    seq_groups = lax.axis_size("seq")
    group_tok = tok_rows * seq_groups
    expert_count = lax.axis_size("shard")
    top_count = expert_ids.shape[-1]
    capacity = min(tok_rows, 3 * tok_rows * top_count // (2 * expert_count))
    heads_local = HEADS // seq_groups
    local_width = heads_local * HEAD_DIM
    score_scale = HEAD_DIM ** (-0.5)
    segment, position = group_layout(seq_lengths[0], seq_order[0], group_tok)
    places = jnp.arange(group_tok, dtype=jnp.int32)
    allowed = (segment[:, None] == segment[None, :]) & (places[None, :] <= places[:, None])
    own_position = lax.dynamic_slice_in_dim(position, lax.axis_index("seq") * tok_rows, tok_rows)
    cosine, sine_part = rope_tables(own_position, HEAD_DIM)
    full_qkv, full_out, full_gains = (
        lax.all_gather(weight_qkv, "shard", axis=0, tiled=True),
        lax.all_gather(weight_out, "shard", axis=0, tiled=True),
        lax.all_gather(norm_gains, "shard", axis=0, tiled=True),
    )
    gain_cols = full_gains.astype(jnp.float32)

    def qk_piece(raw_part, gain_col):
        normed_part = rms_scale(raw_part, gain_col).reshape(tok_rows, HEADS, HEAD_DIM)
        return rotate(normed_part, cosine, sine_part).reshape(tok_rows, model_width)

    tokens_f32 = layer_input.reshape(tok_rows, model_width).astype(jnp.float32)
    attn_normed, attn_norm_back = jax.vjp(rms_scale, tokens_f32, gain_cols[:, 0])
    attn_in = attn_normed.astype(jnp.bfloat16)
    projected = jnp.dot(attn_in, full_qkv, preferred_element_type=jnp.float32)
    query_rot, query_back = jax.vjp(qk_piece, projected[:, :model_width], gain_cols[:, 1])
    key_rot, key_back = jax.vjp(
        qk_piece, projected[:, model_width : 2 * model_width], gain_cols[:, 2]
    )
    query_tok = query_rot.astype(jnp.bfloat16)
    key_tok = key_rot.astype(jnp.bfloat16)
    value_tok = projected[:, 2 * model_width :].astype(jnp.bfloat16)
    query_head, key_head, value_head = (
        lax.all_to_all(query_tok, "seq", split_axis=1, concat_axis=0, tiled=True),
        lax.all_to_all(key_tok, "seq", split_axis=1, concat_axis=0, tiled=True),
        lax.all_to_all(value_tok, "seq", split_axis=1, concat_axis=0, tiled=True),
    )
    query_head = query_head.reshape(group_tok, heads_local, HEAD_DIM)
    key_head = key_head.reshape(group_tok, heads_local, HEAD_DIM)
    value_head = value_head.reshape(group_tok, heads_local, HEAD_DIM)
    scores = (
        jnp.einsum("ihd,jhd->hij", query_head, key_head, preferred_element_type=jnp.float32)
        * score_scale
    )
    scores = jnp.where(allowed[None], scores, -1e30)
    score_peak = jnp.max(scores, axis=-1, keepdims=True)
    weights_exp = jnp.exp(scores - score_peak)
    row_total = jnp.sum(weights_exp, axis=-1, keepdims=True)
    attn_probs = weights_exp / row_total
    log_total = score_peak + jnp.log(row_total)
    mix_head = jnp.einsum(
        "hij,jhd->ihd",
        attn_probs.astype(jnp.bfloat16),
        value_head,
        preferred_element_type=jnp.float32,
    )
    mix_head = mix_head.astype(jnp.bfloat16).reshape(group_tok, local_width)
    attn_mix = lax.all_to_all(mix_head, "seq", split_axis=0, concat_axis=1, tiled=True)
    resid = tokens_f32 + jnp.dot(attn_mix, full_out, preferred_element_type=jnp.float32)
    ffn_normed, ffn_norm_back = jax.vjp(rms_scale, resid, gain_cols[:, 3])
    ffn_in = ffn_normed.astype(jnp.bfloat16)
    sources, slot_index = slot_tables(
        expert_ids.reshape(tok_rows, top_count), expert_count, capacity
    )
    pair_probs = expert_probs.reshape(tok_rows * top_count)
    slot_weight = jnp.zeros((expert_count * capacity,), jnp.float32).at[slot_index].set(pair_probs)
    padded = jnp.concatenate([ffn_in, jnp.zeros((1, model_width), jnp.bfloat16)], axis=0)
    outgoing = padded[sources].reshape(expert_count, capacity, model_width)
    gate_weight = weight_gate[0]
    up_weight = weight_up[0]
    down_weight = weight_down[0]
    arrived = lax.all_to_all(outgoing, "shard", split_axis=0, concat_axis=0, tiled=True)
    slot_count = arrived.shape[1]
    flat_rows = arrived.reshape(-1, model_width)
    gate_vals = jnp.dot(flat_rows, gate_weight, preferred_element_type=jnp.float32)
    up_vals = jnp.dot(flat_rows, up_weight, preferred_element_type=jnp.float32)
    hidden = (jax.nn.silu(gate_vals) * up_vals).astype(jnp.bfloat16)
    result = jnp.dot(hidden, down_weight, preferred_element_type=jnp.float32).astype(jnp.bfloat16)
    returned = lax.all_to_all(
        result.reshape(arrived.shape[0], slot_count, model_width),
        "shard",
        split_axis=0,
        concat_axis=0,
        tiled=True,
    )
    returned, arrived_kept, gate_kept, up_kept = (
        returned,
        arrived,
        gate_vals.reshape(arrived.shape[0], slot_count, -1),
        up_vals.reshape(arrived.shape[0], slot_count, -1),
    )
    picked = returned.reshape(expert_count * capacity, model_width)[slot_index].reshape(
        tok_rows, top_count, model_width
    )
    mixed_out = jnp.sum(
        picked.astype(jnp.float32) * expert_probs.reshape(tok_rows, top_count)[..., None], axis=1
    )
    layer_output = (resid + mixed_out).astype(jnp.bfloat16)
    grad_tokens = out_cotangent.reshape(tok_rows, model_width).astype(jnp.float32)
    padded_grad = jnp.concatenate([grad_tokens, jnp.zeros((1, model_width), jnp.float32)], axis=0)
    d_expert = (
        (padded_grad[sources] * slot_weight[:, None])
        .astype(jnp.bfloat16)
        .reshape(expert_count, capacity, model_width)
    )
    d_arrived = lax.all_to_all(d_expert, "shard", split_axis=0, concat_axis=0, tiled=True).reshape(
        -1, model_width
    )
    gate_vals = gate_kept.reshape(d_arrived.shape[0], -1)
    up_vals = up_kept.reshape(d_arrived.shape[0], -1)
    sigma_gate = jax.nn.sigmoid(gate_vals)
    silu_gate = gate_vals * sigma_gate
    hidden = (silu_gate * up_vals).astype(jnp.bfloat16)
    d_hidden = contract_cols(d_arrived, down_weight)
    d_gate = (d_hidden * up_vals * sigma_gate * (1.0 + gate_vals * (1.0 - sigma_gate))).astype(
        jnp.bfloat16
    )
    d_up = (d_hidden * silu_gate).astype(jnp.bfloat16)
    rows_in = arrived_kept.reshape(-1, model_width)
    part_down = contract_rows(hidden, d_arrived)
    part_gate = contract_rows(rows_in, d_gate)
    part_up = contract_rows(rows_in, d_up)
    d_pair = (contract_cols(d_gate, gate_weight) + contract_cols(d_up, up_weight)).astype(
        jnp.bfloat16
    )
    d_pair_back = lax.all_to_all(
        d_pair.reshape(expert_count, capacity, model_width),
        "shard",
        split_axis=0,
        concat_axis=0,
        tiled=True,
    )
    d_ffn_in = jnp.sum(
        d_pair_back.reshape(expert_count * capacity, model_width)[slot_index]
        .astype(jnp.float32)
        .reshape(tok_rows, top_count, model_width),
        axis=1,
    )
    sum_gate, sum_up, sum_down = (
        lax.psum_scatter(
            part_gate.astype(jnp.bfloat16), "seq", scatter_dimension=0, tiled=True
        ).astype(jnp.float32),
        lax.psum_scatter(
            part_up.astype(jnp.bfloat16), "seq", scatter_dimension=0, tiled=True
        ).astype(jnp.float32),
        lax.psum_scatter(
            part_down.astype(jnp.bfloat16), "seq", scatter_dimension=0, tiled=True
        ).astype(jnp.float32),
    )
    d_resid_norm, grad_g_ffn = ffn_norm_back(d_ffn_in)
    d_resid = grad_tokens + d_resid_norm
    d_branch = d_resid.astype(jnp.bfloat16)
    d_mix = contract_cols(d_branch, full_out).astype(jnp.bfloat16)
    d_mix_head = lax.all_to_all(d_mix, "seq", split_axis=1, concat_axis=0, tiled=True).reshape(
        group_tok, heads_local, HEAD_DIM
    )
    scores_again = (
        jnp.einsum("ihd,jhd->hij", query_head, key_head, preferred_element_type=jnp.float32)
        * score_scale
    )
    probs_back = jnp.where(allowed[None], jnp.exp(scores_again - log_total), 0.0)
    d_probs = jnp.einsum("ihd,jhd->hij", d_mix_head, value_head, preferred_element_type=jnp.float32)
    delta_rows = jnp.sum(probs_back * d_probs, axis=-1, keepdims=True)
    d_scores = (probs_back * (d_probs - delta_rows)).astype(jnp.bfloat16)
    d_query = (
        jnp.einsum("hij,jhd->ihd", d_scores, key_head, preferred_element_type=jnp.float32)
        * score_scale
    ).astype(jnp.bfloat16)
    d_key = (
        jnp.einsum("hij,ihd->jhd", d_scores, query_head, preferred_element_type=jnp.float32)
        * score_scale
    ).astype(jnp.bfloat16)
    d_value = jnp.einsum(
        "hij,ihd->jhd",
        probs_back.astype(jnp.bfloat16),
        d_mix_head,
        preferred_element_type=jnp.float32,
    ).astype(jnp.bfloat16)
    dq_tok, dk_tok, dv_tok = (
        lax.all_to_all(
            d_query.reshape(group_tok, local_width), "seq", split_axis=0, concat_axis=1, tiled=True
        ),
        lax.all_to_all(
            d_key.reshape(group_tok, local_width), "seq", split_axis=0, concat_axis=1, tiled=True
        ),
        lax.all_to_all(
            d_value.reshape(group_tok, local_width), "seq", split_axis=0, concat_axis=1, tiled=True
        ),
    )
    dq_raw, grad_g_q = query_back(dq_tok.astype(jnp.float32))
    dk_raw, grad_g_k = key_back(dk_tok.astype(jnp.float32))
    d_qkv = jnp.concatenate(
        [dq_raw.astype(jnp.bfloat16), dk_raw.astype(jnp.bfloat16), dv_tok], axis=1
    )
    d_attn_in = contract_cols(d_qkv, full_qkv)
    dx_norm, grad_g_attn = attn_norm_back(d_attn_in)
    input_grad = (d_resid + dx_norm).astype(jnp.bfloat16)
    gain_terms = jnp.stack([grad_g_attn, grad_g_q, grad_g_k, grad_g_ffn], axis=1)
    term_qkv = contract_rows(attn_in, d_qkv)
    term_out = contract_rows(attn_mix, d_branch)
    rows_qkv, rows_out, rows_gain = (
        lax.psum_scatter(
            term_qkv.astype(jnp.bfloat16), "shard", scatter_dimension=0, tiled=True
        ).astype(jnp.float32),
        lax.psum_scatter(
            term_out.astype(jnp.bfloat16), "shard", scatter_dimension=0, tiled=True
        ).astype(jnp.float32),
        lax.psum_scatter(
            gain_terms.astype(jnp.bfloat16), "shard", scatter_dimension=0, tiled=True
        ).astype(jnp.float32),
    )
    rows_qkv, rows_out, rows_gain = (
        lax.psum(rows_qkv.astype(jnp.bfloat16), "seq").astype(jnp.float32),
        lax.psum(rows_out.astype(jnp.bfloat16), "seq").astype(jnp.float32),
        lax.psum(rows_gain.astype(jnp.bfloat16), "seq").astype(jnp.float32),
    )
    return (
        layer_output.reshape(1, tok_rows, model_width),
        input_grad.reshape(1, tok_rows, model_width),
        rows_qkv,
        rows_out,
        rows_gain,
        sum_gate.reshape(1, sum_gate.shape[0], sum_gate.shape[1]),
        sum_up.reshape(1, sum_up.shape[0], sum_up.shape[1]),
        sum_down.reshape(1, sum_down.shape[0], sum_down.shape[1]),
    )


def solution(mesh):
    in_specs = (
        P("shard", "seq", None),
        P("shard", None),
        P("shard", None),
        P("shard", "seq", None),
        P("shard", "seq", None),
        P("shard", None),
        P("shard", None),
        P("shard", None),
        P("shard", None, None),
        P("shard", None, None),
        P("shard", None, None),
        P("shard", "seq", None),
    )
    out_specs = (
        P("shard", "seq", None),
        P("shard", "seq", None),
        P("shard", None),
        P("shard", None),
        P("shard", None),
        P("shard", "seq", None),
        P("shard", "seq", None),
        P("shard", "seq", None),
    )
    return jax.shard_map(shards, mesh=mesh, in_specs=in_specs, out_specs=out_specs, check_vma=False)
```

profile of v0, /device:TPU:0, one launch (start us, length us, event | category | flops | bytes accessed | tf_op | source)
XLA Modules:
  0.0 1513.1 jit_solution(13289953523183613215)
XLA Ops:
  11.6 4.5 reduce-window.18
  16.4 24.0 %all_gather.9 = bf16[2048,4]{0,1:T(4,128)(2,1)S(1)} all-gather(bf16[128,4]{0,1:T(4,128)(2,1)} %param.19), channel_id=1, replica_groups=mesh['seq'=2,'shard'=16] {'shard'}, dimensions={0}, use_global_device_ids=true | all-gather | bytes 17408 | tf_op jit(solution)/shard_map/all_gather | solution.py:113
  42.3 98.6 %all-gather.3.cloned.1.call-done = bf16[2048,6144]{1,0:T(8,128)(2,1)} async-done(((bf16[128,6144]{1,0:T(8,128)(2,1)}), bf16[2048,6144]{1,0:T(8,128)(2,1)}) %all-gather.3.cloned.1.call-update) | async-done | bytes 25165840 | tf_op jit(solution)/shard_map/all_gather | solution.py:111
  140.9 10.2 fusion.44
  152.3 4.2 all-to-all-start
  165.3 3.5 all-to-all-start.2
  169.6 6.9 all-to-all-done.2
  176.6 3.5 all-to-all-start.1
  180.1 4.3 scatter_custom_fusion
  192.2 4.0 all-to-all-start.3
  196.2 21.2 %all-gather.5.cloned.1.call-done = bf16[2048,2048]{1,0:T(8,128)(2,1)} async-done(((bf16[128,2048]{1,0:T(8,128)(2,1)}), bf16[2048,2048]{1,0:T(8,128)(2,1)}) %all-gather.5.cloned.1.call-update) | async-done | bytes 8388624 | tf_op jit(solution)/shard_map/all_gather | solution.py:112
  217.5 4.9 multiply_reduce_fusion.7
  223.6 7.1 gather_fusion
  230.7 4.8 all-to-all-start.4
  235.7 4.3 scatter_custom_fusion.1
  240.3 8.0 gather_fusion.2
  248.3 7.9 multiply_convert_fusion
  256.2 93.3 %all-to-all-done.4 = bf16[16,96,2048]{2,1,0:T(8,128)(2,1)} async-done(((bf16[16,96,2048]{2,1,0:T(8,128)(2,1)}), bf16[16,96,2048]{2,1,0:T(8,128)(2,1)}, u32[]{:S(2)}, u32[]{:S(2)}) %all-to-all-start.4) | async-done | bytes 6291488 | tf_op jit(solution)/shard_map/all_to_all | solution.py:171
  349.5 28.1 %all-to-all-start.6 = ((bf16[16,96,2048]{2,1,0:T(8,128)(2,1)}), bf16[16,96,2048]{2,1,0:T(8,128)(2,1)}, u32[]{:S(2)}, u32[]{:S(2)}) async-start(bf16[16,96,2048]{2,1,0:T(8,128)(2,1)} %multiply_convert_fusion), calls=%async_computation.6 | async-start | bytes 12582912 | tf_op jit(solution)/shard_map/all_to_all | solution.py:205
  377.6 11.8 fusion.6
  389.4 10.4 fusion.10
  399.8 91.8 %all-to-all-done.6 = bf16[16,96,2048]{2,1,0:T(8,128)(2,1)} async-done(((bf16[16,96,2048]{2,1,0:T(8,128)(2,1)}), bf16[16,96,2048]{2,1,0:T(8,128)(2,1)}, u32[]{:S(2)}, u32[]{:S(2)}) %all-to-all-start.6) | async-done | bytes 6291488 | tf_op jit(solution)/shard_map/all_to_all | solution.py:205
  491.7 17.7 %multiply_convert_fusion.1 = (bf16[1536,1024]{1,0:T(8,128)(2,1)}, bf16[1536,1024]{1,0:T(8,128)(2,1)}, bf16[1536,1024]{1,0:T(8,128)(2,1)S(1)}) fusion(f32[1536,1024]{1,0:T(8,128)} %fusion.10, f32[1536,1024]{1,0:T(8,128)} %fusion.6, bf16[1536,2048]{1,0:T(8,128)(2,1)} %bitcast.35, bf16[1,1024,2048]{2,1,0:T(8,128)(2,1)} %param.22), kind=kOutput, calls=%fused_computation.14 | convolution fusion | flops 6466043904 | bytes 32505856 | tf_op jit(solution)/shard_map/dot_general | solution.py:76
  509.3 8.7 convolution_convert_fusion.1
  518.1 28.1 %all-to-all-start.5 = ((bf16[16,96,2048]{2,1,0:T(8,128)(2,1)}), bf16[16,96,2048]{2,1,0:T(8,128)(2,1)}, u32[]{:S(2)}, u32[]{:S(2)}) async-start(bf16[16,96,2048]{2,1,0:T(8,128)(2,1)} %bitcast.177), calls=%async_computation.5 | async-start | bytes 12582912 | tf_op jit(solution)/shard_map/all_to_all | solution.py:178
  546.2 12.4 fusion.8
  558.7 11.5 add_convert_fusion
  570.2 90.1 %all-to-all-done.5 = bf16[16,96,2048]{2,1,0:T(8,128)(2,1)} async-done(((bf16[16,96,2048]{2,1,0:T(8,128)(2,1)}), bf16[16,96,2048]{2,1,0:T(8,128)(2,1)}, u32[]{:S(2)}, u32[]{:S(2)}) %all-to-all-start.5) | async-done | bytes 6291488 | tf_op jit(solution)/shard_map/all_to_all | solution.py:178
  660.3 28.1 %all-to-all-start.7 = ((bf16[16,96,2048]{2,1,0:T(8,128)(2,1)}), bf16[16,96,2048]{2,1,0:T(8,128)(2,1)}, u32[]{:S(2)}, u32[]{:S(2)}) async-start(bf16[16,96,2048]{2,1,0:T(8,128)(2,1)} %bitcast.176), calls=%async_computation.7 | async-start | bytes 12582912 | tf_op jit(solution)/shard_map/all_to_all | solution.py:225
  688.5 12.4 gather_fusion.1
  700.9 101.5 %all-to-all-done.7 = bf16[16,96,2048]{2,1,0:T(8,128)(2,1)} async-done(((bf16[16,96,2048]{2,1,0:T(8,128)(2,1)}), bf16[16,96,2048]{2,1,0:T(8,128)(2,1)}, u32[]{:S(2)}, u32[]{:S(2)}) %all-to-all-start.7) | async-done | bytes 6291488 | tf_op jit(solution)/shard_map/all_to_all | solution.py:225
  802.5 12.6 gather_fusion.3
  815.1 5.2 convert_reduce_fusion
  820.7 4.4 fusion
  826.2 5.6 convolution_convert_fusion.2
  831.9 6.7 convolution_convert_fusion.6
  839.4 3.5 all-to-all-start.8
  842.9 9.3 all-to-all-done.8
  855.3 4.2 all-to-all-start.11
  863.6 4.5 all-to-all-done.11
  868.2 3.5 all-to-all-start.9
  873.2 6.1 all-to-all-done.9
  879.3 3.5 all-to-all-start.10
  884.8 4.8 all-to-all-done.10
  892.0 2.8 copy.167
  894.8 2.3 pad_add_fusion
  897.1 2.5 copy.168
  899.7 2.3 multiply_reduce_fusion.3
  903.5 13.3 convolution_convert_fusion
  918.8 11.4 convolution_convert_fusion.4
  932.1 11.1 convolution_convert_fusion.5
  945.2 11.2 convolution_convert_fusion.3
  957.9 13.6 fusion.24
  972.8 233.2 %reduce-scatter.9.cloned.1.call-done = bf16[128,6144]{1,0:T(8,128)(2,1)} async-done(((bf16[2048,6144]{1,0:T(8,128)(2,1)}), bf16[128,6144]{1,0:T(8,128)(2,1)}) %reduce-scatter.9.cloned.1.call-update) | async-done | bytes 1572880 | tf_op jit(solution)/shard_map/reduce_scatter | solution.py:301
  1206.1 56.2 %reduce-scatter.15.cloned.1.call-done = bf16[1024,1024]{1,0:T(8,128)(2,1)} async-done(((bf16[2048,1024]{1,0:T(8,128)(2,1)}), bf16[1024,1024]{1,0:T(8,128)(2,1)}) %reduce-scatter.15.cloned.1.call-update) | async-done | bytes 2097168 | tf_op jit(solution)/shard_map/reduce_scatter | solution.py:242
  1262.2 4.1 bitcast_convert_fusion.1
  1266.3 53.1 %reduce-scatter.13.cloned.1.call-done = bf16[1024,1024]{1,0:T(8,128)(2,1)} async-done(((bf16[2048,1024]{1,0:T(8,128)(2,1)}), bf16[1024,1024]{1,0:T(8,128)(2,1)}) %reduce-scatter.13.cloned.1.call-update) | async-done | bytes 2097168 | tf_op jit(solution)/shard_map/reduce_scatter | solution.py:239
  1319.4 4.1 bitcast_convert_fusion.2
  1323.5 52.6 %reduce-scatter.17.cloned.1.call-done = bf16[512,2048]{1,0:T(8,128)(2,1)} async-done(((bf16[1024,2048]{1,0:T(8,128)(2,1)}), bf16[512,2048]{1,0:T(8,128)(2,1)}) %reduce-scatter.17.cloned.1.call-update) | async-done | bytes 2097168 | tf_op jit(solution)/shard_map/reduce_scatter | solution.py:245
  1376.1 4.1 bitcast_convert_fusion
  1381.4 55.1 %reduce-scatter.19.cloned.1.call-done = bf16[128,4]{1,0:T(8,128)(2,1)} async-done(((bf16[2048,4]{1,0:T(8,128)(2,1)}), bf16[128,4]{1,0:T(8,128)(2,1)}) %reduce-scatter.19.cloned.1.call-update) | async-done | bytes 1040
  1437.3 4.9 psum.23
  1442.8 58.0 %all-reduce.9.cloned.1.call-done = (bf16[128,6144]{1,0:T(8,128)(2,1)}, bf16[128,2048]{1,0:T(8,128)(2,1)}) async-done(((bf16[128,6144]{1,0:T(8,128)(2,1)}, bf16[128,2048]{1,0:T(8,128)(2,1)}), (bf16[128,6144]{1,0:T(8,128)(2,1)}, bf16[128,2048]{1,0:T(8,128)(2,1)})) %all-reduce.9.cloned.1.call-update) | async-done | bytes 2097168 | tf_op jit(solution)/shard_map/psum | solution.py:312
  1502.9 3.4 convert_element_type.227
  (259 shorter events, 56.4 us)
Async XLA Ops:
  7.2 133.8 %all-gather.3.cloned.1.call-start = ((), (), s32[]{:S(2)}) async-start(), calls=%async_computation.18 | async-start | bytes 26738688 | tf_op jit(solution)/shard_map/all_gather | solution.py:111
  7.9 209.6 %all-gather.5.cloned.1.call-start = ((), (), s32[]{:S(2)}) async-start(), calls=%async_computation.19 | async-start | bytes 8912896 | tf_op jit(solution)/shard_map/all_gather | solution.py:112
  42.0 98.9 %copy-start.59 = (f32[128]{0:T(128)}, f32[128]{0:T(128)S(1)}, u32[]{:S(2)}) copy-start(f32[128]{0:T(128)S(1)} %fusion.30) | copy-start | bytes 1540
  42.0 109.1 %copy-start.44 = (f32[128]{0:T(128)}, f32[128]{0:T(128)S(1)}, u32[]{:S(2)}) copy-start(f32[128]{0:T(128)S(1)} %fusion.56) | copy-start | bytes 1540
  42.3 119.8 %copy-start.30 = (f32[128,64]{0,1:T(8,128)}, f32[128,64]{0,1:T(8,128)S(1)}, u32[]{:S(2)}) copy-start(f32[128,64]{0,1:T(8,128)S(1)} %get-tuple-element.47) | copy-start | bytes 98308
  42.3 119.8 %copy-start.32 = (f32[128,64]{0,1:T(8,128)}, f32[128,64]{0,1:T(8,128)S(1)}, u32[]{:S(2)}) copy-start(f32[128,64]{0,1:T(8,128)S(1)} %get-tuple-element.48) | copy-start | bytes 98308
  42.3 108.9 %copy-start.28 = (f32[2048,1]{0,1:T(1,128)}, f32[2048,1]{0,1:T(1,128)S(1)}, u32[]{:S(2)}) copy-start(f32[2048,1]{0,1:T(1,128)S(1)} %get-tuple-element.46) | copy-start | bytes 24580
  42.3 114.9 %copy-start.34 = (f32[2048,1]{0,1:T(1,128)}, f32[2048,1]{0,1:T(1,128)S(1)}, u32[]{:S(2)}) copy-start(f32[2048,1]{0,1:T(1,128)S(1)} %get-tuple-element.44) | copy-start | bytes 24580
  42.3 114.9 %copy-start.36 = (f32[2048,1]{0,1:T(1,128)}, f32[2048,1]{0,1:T(1,128)S(1)}, u32[]{:S(2)}) copy-start(f32[2048,1]{0,1:T(1,128)S(1)} %get-tuple-element.45) | copy-start | bytes 24580
  42.3 180.1 %copy-start.38 = (f32[2048,1]{0,1:T(1,128)}, f32[2048,1]{0,1:T(1,128)S(1)}, u32[]{:S(2)}) copy-start(f32[2048,1]{0,1:T(1,128)S(1)} %get-tuple-element.43) | copy-start | bytes 24580
  151.2 7.6 copy-start
  152.3 13.0 all-to-all-start
  156.7 5.2 copy-start.55
  165.3 11.3 all-to-all-start.2
  176.6 10.5 all-to-all-start.1
  190.5 27.0 %copy-start.9 = (bf16[1,128,2048]{2,1,0:T(8,128)(2,1)S(1)}, bf16[1,128,2048]{2,1,0:T(8,128)(2,1)}, u32[]{:S(2)}) copy-start(bf16[1,128,2048]{2,1,0:T(8,128)(2,1)} %param.12) | copy-start | bytes 1572868
  192.2 25.2 %all-to-all-start.3 = ((bf16[2,128,1024]{1,2,0:T(8,128)(2,1)}), bf16[2,128,1024]{1,2,0:T(8,128)(2,1)S(1)}, u32[]{:S(2)}, u32[]{:S(2)}) async-start(bf16[2,128,1024]{1,2,0:T(8,128)(2,1)} %copy.136), calls=%async_computation.3 | async-start | bytes 1048576 | tf_op jit(solution)/shard_map/all_to_all | solution.py:157
  217.5 4.9 copy-start.11
  222.4 8.2 copy-start.57
  222.5 8.2 copy-start.47
  230.7 9.4 copy-start.22
  230.7 118.8 %all-to-all-start.4 = ((bf16[16,96,2048]{2,1,0:T(8,128)(2,1)}), bf16[16,96,2048]{2,1,0:T(8,128)(2,1)}, u32[]{:S(2)}, u32[]{:S(2)}) async-start(bf16[16,96,2048]{2,1,0:T(8,128)(2,1)} %bitcast.173), calls=%async_computation.4 | async-start | bytes 12582912 | tf_op jit(solution)/shard_map/all_to_all | solution.py:171
  349.5 142.2 %all-to-all-start.6 = ((bf16[16,96,2048]{2,1,0:T(8,128)(2,1)}), bf16[16,96,2048]{2,1,0:T(8,128)(2,1)}, u32[]{:S(2)}, u32[]{:S(2)}) async-start(bf16[16,96,2048]{2,1,0:T(8,128)(2,1)} %multiply_convert_fusion), calls=%async_computation.6 | async-start | bytes 12582912 | tf_op jit(solution)/shard_map/all_to_all | solution.py:205
  377.6 11.8 copy-start.62
  491.7 17.7 %copy-start.61 = (bf16[1,1024,2048]{2,1,0:T(8,128)(2,1)S(1)}, bf16[1,1024,2048]{2,1,0:T(8,128)(2,1)}, u32[]{:S(2)}) copy-start(bf16[1,1024,2048]{2,1,0:T(8,128)(2,1)} %param.22) | copy-start | bytes 12582916
  509.3 8.7 copy-start.64
  518.1 142.2 %all-to-all-start.5 = ((bf16[16,96,2048]{2,1,0:T(8,128)(2,1)}), bf16[16,96,2048]{2,1,0:T(8,128)(2,1)}, u32[]{:S(2)}, u32[]{:S(2)}) async-start(bf16[16,96,2048]{2,1,0:T(8,128)(2,1)} %bitcast.177), calls=%async_computation.5 | async-start | bytes 12582912 | tf_op jit(solution)/shard_map/all_to_all | solution.py:178
  546.2 12.5 copy-start.63
  546.2 12.5 copy-start.67
  660.3 142.2 %all-to-all-start.7 = ((bf16[16,96,2048]{2,1,0:T(8,128)(2,1)}), bf16[16,96,2048]{2,1,0:T(8,128)(2,1)}, u32[]{:S(2)}, u32[]{:S(2)}) async-start(bf16[16,96,2048]{2,1,0:T(8,128)(2,1)} %bitcast.176), calls=%async_computation.7 | async-start | bytes 12582912 | tf_op jit(solution)/shard_map/all_to_all | solution.py:225
  688.4 284.4 %reduce-scatter.11.cloned.1.call-start = ((), (), s32[]{:S(2)}) async-start(), calls=%async_computation.21 | async-start | bytes 8912896 | tf_op jit(solution)/shard_map/reduce_scatter | solution.py:304
  802.5 17.9 %copy-start.39 = (f32[2048,1]{0,1:T(1,128)S(1)}, f32[2048,1]{0,1:T(1,128)}, u32[]{:S(2)}) copy-start(f32[2048,1]{0,1:T(1,128)} %copy-done.38) | copy-start | bytes 24580
  802.5 17.9 %copy-start.48 = (f32[128]{0:T(128)S(1)}, f32[128]{0:T(128)}, u32[]{:S(2)}) copy-start(f32[128]{0:T(128)} %copy-done.47) | copy-start | bytes 1540
  815.1 5.3 copy-start.8
  815.1 5.5 copy-start.58
  815.1 5.5 copy-start.4
  820.7 5.6 copy-start.12
  826.2 5.6 copy-start.5
  831.9 11.0 copy-start.41
  831.9 11.0 copy-start.43
  838.5 15.0 copy-start.3
  838.5 14.9 copy-start.27
  839.4 12.9 all-to-all-start.8
  855.3 12.9 all-to-all-start.11
  862.3 9.4 copy-start.16
  868.2 11.2 all-to-all-start.9
  872.2 17.5 %copy-start.31 = (f32[128,64]{0,1:T(8,128)S(1)}, f32[128,64]{0,1:T(8,128)}, u32[]{:S(2)}) copy-start(f32[128,64]{0,1:T(8,128)} %copy-done.30) | copy-start | bytes 98308
  872.2 17.5 %copy-start.33 = (f32[128,64]{0,1:T(8,128)S(1)}, f32[128,64]{0,1:T(8,128)}, u32[]{:S(2)}) copy-start(f32[128,64]{0,1:T(8,128)} %copy-done.32) | copy-start | bytes 98308
  879.3 10.3 all-to-all-start.10
  882.8 323.2 %reduce-scatter.9.cloned.1.call-start = ((), (), s32[]{:S(2)}) async-start(), calls=%async_computation.20 | async-start | bytes 26738688 | tf_op jit(solution)/shard_map/reduce_scatter | solution.py:301
  890.9 8.7 copy-start.1
  890.9 8.7 copy-start.35
  891.0 8.7 copy-start.37
  891.0 8.7 copy-start.50
  891.0 8.7 copy-start.52
  894.8 7.2 copy-start.54
  894.8 7.2 copy-start.56
  916.9 345.3 %reduce-scatter.15.cloned.1.call-start = ((), (), s32[]{:S(2)}) async-start(), calls=%async_computation.23 | async-start | bytes 6291456 | tf_op jit(solution)/shard_map/reduce_scatter | solution.py:242
  930.2 389.2 %reduce-scatter.13.cloned.1.call-start = ((), (), s32[]{:S(2)}) async-start(), calls=%async_computation.22 | async-start | bytes 6291456 | tf_op jit(solution)/shard_map/reduce_scatter | solution.py:239
  943.3 432.8 %reduce-scatter.17.cloned.1.call-start = ((), (), s32[]{:S(2)}) async-start(), calls=%async_computation.24 | async-start | bytes 6291456 | tf_op jit(solution)/shard_map/reduce_scatter | solution.py:245
  956.4 480.1 %reduce-scatter.19.cloned.1.call-start = ((), (), s32[]{:S(2)}) async-start(), calls=%async_computation.25 | async-start | bytes 557056
  972.7 528.1 %all-reduce.9.cloned.1.call-start = ((), (), s32[]{:S(2)}) async-start(), calls=%async_computation.26 | async-start | bytes 4194304 | tf_op jit(solution)/shard_map/psum | solution.py:312
  1323.5 56.8 %copy-start.60 = (f32[128]{0:T(128)S(1)}, f32[128]{0:T(128)}, u32[]{:S(2)}) copy-start(f32[128]{0:T(128)} %copy-done.59) | copy-start | bytes 1540
  1323.5 56.8 %copy-start.6 = (f32[128,2048]{1,0:T(8,128)S(1)}, f32[128,2048]{1,0:T(8,128)}, u32[]{:S(2)}) copy-start(f32[128,2048]{1,0:T(8,128)} %copy-done.5) | copy-start | bytes 3145732
  (26 other events, 63.8 us)
Sparse Core Ops, SparseCore 0:
  9.6 131.3 all-gather.2
  143.1 74.3 all-gather.4
  832.0 126.8 reduce-scatter.10
  962.8 243.1 reduce-scatter.8
  1208.7 53.4 reduce-scatter.14
  1265.0 54.3 reduce-scatter.12
  1321.7 54.3 reduce-scatter.16
  1380.2 56.2 reduce-scatter.18
  1438.8 61.9 all-reduce.8
where the time goes:
time: 1520 us; the launch traced here: 1510 us
  waiting for transfers between devices  1040 us (68%)
  matrix products  165 us (11%)
  starting transfers between devices  119 us (8%)
  local copies, waits for them, and re-layouts  83.7 us (6%)
  other arithmetic  60.1 us (4%)
  blocking collectives  28.9 us (2%)
  between operations  15.3 us (1%)
    reduce_scatter x1, waiting for transfers between devices, shards(): lax.psum_scatter(term_qkv.astype(jnp.bfloat16), 'shard', scatter_dimensio...  233 us
    all_to_all x1, waiting for transfers between devices, shards(): lax.all_to_all(d_pair.reshape(expert_count, capacity, model_width), 'shar...  102 us
    all_gather x1, waiting for transfers between devices, shards(): lax.all_gather(weight_qkv, 'shard', axis=0, tiled=True)  98.6 us
    all_to_all x1, waiting for transfers between devices, shards(): lax.all_to_all(outgoing, 'shard', split_axis=0, concat_axis=0, tiled=True)  93.3 us
    all_to_all x1, waiting for transfers between devices, shards(): lax.all_to_all(d_expert, 'shard', split_axis=0, concat_axis=0, tiled=True)  91.8 us
    all_to_all x1, waiting for transfers between devices, shards(): lax.all_to_all(result.reshape(arrived.shape[0], slot_count, model_width),...  90.1 us
    dot_general x5, matrix products, contract_cols(): lax.dot_general(left_side, right_side, (((1,), (1,)), ((), ())), preferre...  61.9 us
    psum x1, waiting for transfers between devices, shards(): lax.psum(rows_qkv.astype(jnp.bfloat16), 'seq').astype(jnp.float32)  58 us
  transfers between devices with their start and end apart: 21, of which 19 were waited for; matrix products, arithmetic and copies ran while one was open for 15% of the time, Pallas kernels for 0%

commit v1 on v0

v1 whole, which is shorter than its diff:
```python
import functools

import jax
import jax.numpy as jnp
from jax import lax
from jax.experimental import pallas as pl
from jax.experimental.pallas import tpu as pltpu
from jax.sharding import PartitionSpec as P

HEADS = 16
HEAD_DIM = 128


norm_eps = 1e-05
rope_base = 10000.0


def rms_scale(values, gain_col):
    return (
        values * lax.rsqrt(jnp.mean(values * values, axis=-1, keepdims=True) + norm_eps) * gain_col
    )


def rotate(values, cosine, sine_part):
    half_dim = values.shape[-1] // 2
    first_half = values[..., :half_dim]
    second_half = values[..., half_dim:]
    return jnp.concatenate(
        [
            first_half * cosine - second_half * sine_part,
            second_half * cosine + first_half * sine_part,
        ],
        axis=-1,
    )


def rope_tables(position, head_size):
    half_dim = head_size // 2
    frequency = rope_base ** (-2.0 * jnp.arange(half_dim, dtype=jnp.float32) / head_size)
    angles = position.astype(jnp.float32)[:, None] * frequency[None, :]
    return (jnp.cos(angles)[:, None, :], jnp.sin(angles)[:, None, :])


def group_layout(lengths, seq_perm, group_tok):
    seq_count = lengths.shape[0]
    numbers = jnp.arange(seq_count, dtype=jnp.int32)
    packed = jnp.sum(jnp.where(seq_perm[:, None] == numbers[None, :], lengths[None, :], 0), axis=1)
    seq_ends = jnp.cumsum(packed)
    seq_starts = seq_ends - packed
    places = jnp.arange(group_tok, dtype=jnp.int32)
    segment = jnp.sum((places[:, None] >= seq_ends[None, :]).astype(jnp.int32), axis=1)
    begins = jnp.sum(
        jnp.where(segment[:, None] == numbers[None, :], seq_starts[None, :], 0), axis=1
    )
    return (segment, places - begins)


def contract_rows(left_side, right_side):
    return lax.dot_general(
        left_side, right_side, (((0,), (0,)), ((), ())), preferred_element_type=jnp.float32
    )


def contract_cols(left_side, right_side):
    return lax.dot_general(
        left_side, right_side, (((1,), (1,)), ((), ())), preferred_element_type=jnp.float32
    )


MESH_ID = pl.DeviceIdType.MESH
ROW_TILE = 16


def shard_stages(count):
    inner = 2 if count <= 16 else 4
    return (inner, 2, count // (2 * inner))


def scatter_kernel(stages, part_ref, total_ref, *scratch):
    in_one, sum_one, in_two, sum_two, in_three = scratch[:5]
    send_one, recv_one, send_two, recv_two, send_three, recv_three = scratch[5:]
    n1, n2, n3 = stages
    rows = total_ref.shape[0]
    me = lax.axis_index("shard")
    seq = lax.axis_index("seq")
    c = lax.rem(me, n1)
    y = lax.rem(me // n1, n2)
    z = me // (n1 * n2)

    def device(z_to, y_to, c_to):
        return (seq, (z_to * n2 + y_to) * n1 + c_to)

    barrier = pltpu.get_barrier_semaphore()
    for j in range(1, n1):
        pl.semaphore_signal(
            barrier, 1, device_id=device(z, y, lax.rem(c + j, n1)), device_id_type=MESH_ID
        )
    for j in range(1, n2):
        pl.semaphore_signal(
            barrier, 1, device_id=device(z, lax.rem(y + j, n2), c), device_id_type=MESH_ID
        )
    for j in range(1, n3):
        pl.semaphore_signal(
            barrier, 1, device_id=device(lax.rem(z + j, n3), y, c), device_id_type=MESH_ID
        )
    pl.semaphore_wait(barrier, n1 + n2 + n3 - 3)

    first, second, third = [], [], []
    for k in range(n3):
        z_to = lax.rem(z + k + 1, n3)
        copies = []
        for j in range(1, n1):
            c_to = lax.rem(c + j, n1)
            slot = n1 - 1 - j
            copy = pltpu.make_async_remote_copy(
                src_ref=part_ref.at[z_to, :, c_to],
                dst_ref=in_one.at[k, slot],
                send_sem=send_one.at[k, j - 1],
                recv_sem=recv_one.at[k, slot],
                device_id=device(z, y, c_to),
                device_id_type=MESH_ID,
            )
            copy.start()
            copies.append(copy)
        first.append(copies)

    def fold_one(k):
        z_to = lax.rem(z + k + 1, n3)
        for copy in first[k]:
            copy.wait_recv()

        def step(i, carry):
            at = pl.ds(pl.multiple_of(i * ROW_TILE, ROW_TILE), ROW_TILE)
            for y_to in range(n2):
                value = part_ref[z_to, y_to, c, at, :].astype(jnp.float32)
                for slot in range(n1 - 1):
                    value += in_one[k, slot, y_to, at, :].astype(jnp.float32)
                sum_one[k, y_to, at, :] = value.astype(sum_one.dtype)
            return carry

        lax.fori_loop(0, rows // ROW_TILE, step, 0)
        copies = []
        for j in range(1, n2):
            y_to = lax.rem(y + j, n2)
            slot = n2 - 1 - j
            copy = pltpu.make_async_remote_copy(
                src_ref=sum_one.at[k, y_to],
                dst_ref=in_two.at[k, slot],
                send_sem=send_two.at[k, j - 1],
                recv_sem=recv_two.at[k, slot],
                device_id=device(z, y_to, c),
                device_id_type=MESH_ID,
            )
            copy.start()
            copies.append(copy)
        second.append(copies)

    def fold_two(k):
        for copy in second[k]:
            copy.wait_recv()

        def step(i, carry):
            at = pl.ds(pl.multiple_of(i * ROW_TILE, ROW_TILE), ROW_TILE)
            value = sum_one[k, y, at, :].astype(jnp.float32)
            for slot in range(n2 - 1):
                value += in_two[k, slot, at, :].astype(jnp.float32)
            sum_two[k, at, :] = value.astype(sum_two.dtype)
            return carry

        lax.fori_loop(0, rows // ROW_TILE, step, 0)
        if k < n3 - 1:
            slot = n3 - 2 - k
            copy = pltpu.make_async_remote_copy(
                src_ref=sum_two.at[k],
                dst_ref=in_three.at[slot],
                send_sem=send_three.at[k],
                recv_sem=recv_three.at[slot],
                device_id=device(lax.rem(z + k + 1, n3), y, c),
                device_id_type=MESH_ID,
            )
            copy.start()
            third.append(copy)

    for k in range(n3 + 1):
        if k < n3:
            fold_one(k)
        if k > 0:
            fold_two(k - 1)
    for copy in third:
        copy.wait_recv()

    def finish(i, carry):
        at = pl.ds(pl.multiple_of(i * ROW_TILE, ROW_TILE), ROW_TILE)
        value = sum_two[n3 - 1, at, :].astype(jnp.float32)
        for slot in range(n3 - 1):
            value += in_three[slot, at, :].astype(jnp.float32)
        total_ref[at, :] = value.astype(total_ref.dtype)
        return carry

    lax.fori_loop(0, rows // ROW_TILE, finish, 0)
    for copies in first + second:
        for copy in copies:
            copy.wait_send()
    for copy in third:
        copy.wait_send()


def scatter_sum(part, collective_id, out_dtype):
    count, rows, cols = part.shape
    stages = shard_stages(count)
    n1, n2, n3 = stages
    low = part.dtype
    return pl.pallas_call(
        functools.partial(scatter_kernel, stages),
        out_shape=jax.ShapeDtypeStruct((rows, cols), out_dtype),
        in_specs=[pl.BlockSpec(memory_space=pltpu.VMEM)],
        out_specs=pl.BlockSpec(memory_space=pltpu.VMEM),
        scratch_shapes=[
            pltpu.VMEM((n3, n1 - 1, n2, rows, cols), low),
            pltpu.VMEM((n3, n2, rows, cols), low),
            pltpu.VMEM((n3, n2 - 1, rows, cols), low),
            pltpu.VMEM((n3, rows, cols), low),
            pltpu.VMEM((n3 - 1, rows, cols), low),
            pltpu.SemaphoreType.DMA((n3, n1 - 1)),
            pltpu.SemaphoreType.DMA((n3, n1 - 1)),
            pltpu.SemaphoreType.DMA((n3, n2 - 1)),
            pltpu.SemaphoreType.DMA((n3, n2 - 1)),
            pltpu.SemaphoreType.DMA((n3 - 1,)),
            pltpu.SemaphoreType.DMA((n3 - 1,)),
        ],
        compiler_params=pltpu.CompilerParams(
            collective_id=collective_id,
            has_side_effects=True,
            vmem_limit_bytes=60 * 1024 * 1024,
        ),
        name="scatter_sum_%d" % collective_id,
    )(part.reshape(n3, n2, n1, rows, cols))


def pair_tables(expert_list, prob_list, expert_count):
    numbers = jnp.arange(expert_count, dtype=jnp.int32)
    named = expert_list[None, :, :] == numbers[:, None, None]
    return jnp.sum(jnp.where(named, prob_list[None], 0.0), axis=2)


def shards(
    layer_input,
    seq_lengths,
    seq_order,
    expert_ids,
    expert_probs,
    weight_qkv,
    weight_out,
    norm_gains,
    weight_gate,
    weight_up,
    weight_down,
    out_cotangent,
):
    width = layer_input.shape[-1]
    tok_rows = layer_input.shape[1]
    seq_count = lax.axis_size("seq")
    seq_at = lax.axis_index("seq")
    group_tok = tok_rows * seq_count
    experts = lax.axis_size("shard")
    shard_at = lax.axis_index("shard")
    top_count = expert_ids.shape[-1]
    capacity = min(tok_rows, 3 * tok_rows * top_count // (2 * experts))
    weight_rows = weight_qkv.shape[0]
    heads_local = HEADS // seq_count
    local_width = heads_local * HEAD_DIM
    out_cols = width // seq_count
    score_scale = HEAD_DIM ** (-0.5)
    low = jnp.bfloat16
    f32 = jnp.float32

    def take_seq(array, axis):
        return lax.dynamic_index_in_dim(array, seq_at, axis, keepdims=False)

    own_cols = take_seq(weight_qkv.reshape(weight_rows, 3, seq_count, local_width), 2)
    qkv_cols = lax.all_gather(
        own_cols.reshape(weight_rows, 3 * local_width), "shard", axis=0, tiled=True
    )
    gain_cols = lax.all_gather(norm_gains, "shard", axis=0, tiled=True).astype(f32)
    group_in = lax.all_gather(layer_input[0], "seq", axis=0, tiled=True).astype(f32)
    table = pair_tables(expert_ids[0], expert_probs[0], experts)
    full_out = lax.all_gather(weight_out, "shard", axis=0, tiled=True)
    grad_all = lax.all_gather(out_cotangent[0], "shard", axis=0, tiled=False)
    tables_all = lax.all_gather(table, "shard", axis=0, tiled=False)
    pair_weight = lax.dynamic_index_in_dim(tables_all, shard_at, 1, keepdims=False)

    segment, position = group_layout(seq_lengths[0], seq_order[0], group_tok)
    places = jnp.arange(group_tok, dtype=jnp.int32)
    allowed = (segment[:, None] == segment[None, :]) & (places[None, :] <= places[:, None])
    cosine, sine_part = rope_tables(position, HEAD_DIM)

    def rope(values):
        return rotate(
            values.reshape(group_tok, heads_local, HEAD_DIM), cosine, sine_part
        ).reshape(group_tok, local_width)

    def rope_back(grads):
        return rotate(
            grads.reshape(group_tok, heads_local, HEAD_DIM), cosine, -sine_part
        ).reshape(group_tok, local_width)

    gain_q = lax.dynamic_slice_in_dim(gain_cols[:, 1], seq_at * local_width, local_width)
    gain_k = lax.dynamic_slice_in_dim(gain_cols[:, 2], seq_at * local_width, local_width)

    group_r = lax.rsqrt(jnp.mean(group_in * group_in, axis=-1, keepdims=True) + norm_eps)
    group_n = group_in * group_r
    attn_in = (group_n * gain_cols[:, 0]).astype(low)
    projected = jnp.dot(attn_in, qkv_cols, preferred_element_type=f32)
    q_raw = projected[:, :local_width]
    k_raw = projected[:, local_width : 2 * local_width]
    value = projected[:, 2 * local_width :].astype(low)
    squares = jnp.stack([jnp.sum(q_raw * q_raw, axis=-1), jnp.sum(k_raw * k_raw, axis=-1)])
    squares = lax.psum(squares, "seq")
    q_r, k_r = (lax.rsqrt(row / width + norm_eps)[:, None] for row in squares)
    q_n = q_raw * q_r
    k_n = k_raw * k_r
    query = rope(q_n * gain_q).astype(low)
    key = rope(k_n * gain_k).astype(low)
    query_head = query.reshape(group_tok, heads_local, HEAD_DIM)
    key_head = key.reshape(group_tok, heads_local, HEAD_DIM)
    value_head = value.reshape(group_tok, heads_local, HEAD_DIM)
    scores = jnp.einsum("ihd,jhd->hij", query_head, key_head, preferred_element_type=f32)
    scores = jnp.where(allowed[None], scores * score_scale, -1e30)
    score_peak = jnp.max(scores, axis=-1, keepdims=True)
    weights_exp = jnp.exp(scores - score_peak)
    attn_probs = weights_exp / jnp.sum(weights_exp, axis=-1, keepdims=True)
    probs_low = attn_probs.astype(low)
    mix_head = jnp.einsum("hij,jhd->ihd", probs_low, value_head, preferred_element_type=f32)
    mix_head = mix_head.astype(low).reshape(group_tok, local_width)
    attn_mix = lax.all_to_all(mix_head, "seq", split_axis=0, concat_axis=1, tiled=True)
    mix_all = lax.all_gather(mix_head, "seq", axis=1, tiled=True)
    resid = layer_input[0].astype(f32) + jnp.dot(attn_mix, full_out, preferred_element_type=f32)
    ffn_r = lax.rsqrt(jnp.mean(resid * resid, axis=-1, keepdims=True) + norm_eps)
    ffn_n = resid * ffn_r
    ffn_in = (ffn_n * gain_cols[:, 3]).astype(low)

    ffn_all = lax.all_gather(ffn_in, "shard", axis=0, tiled=False)
    named = pair_weight > 0.0
    rank = jnp.cumsum(named.astype(jnp.int32), axis=1) - 1
    slots = jnp.arange(capacity, dtype=jnp.int32)
    pick = (rank[:, None, :] == slots[None, :, None]) & named[:, None, :]
    pick_low = pick.astype(low)
    slot_weight = jnp.sum(jnp.where(pick, pair_weight[:, None, :], 0.0), axis=2)

    def gather_rows(rows):
        return jnp.einsum("brt,btd->brd", pick_low, rows, preferred_element_type=f32)

    def spread_rows(rows):
        return jnp.einsum(
            "brt,brd->btd",
            pick_low,
            rows.reshape(experts, capacity, width),
            preferred_element_type=f32,
        )

    gate_weight = weight_gate[0]
    up_weight = weight_up[0]
    down_weight = weight_down[0]
    rows_in = gather_rows(ffn_all).astype(low).reshape(-1, width)
    gate = jnp.dot(rows_in, gate_weight, preferred_element_type=f32)
    up = jnp.dot(rows_in, up_weight, preferred_element_type=f32)
    sigma = jax.nn.sigmoid(gate)
    silu = gate * sigma
    hidden = (silu * up).astype(low)
    d_expert = (gather_rows(grad_all) * slot_weight[:, :, None]).astype(low).reshape(-1, width)
    d_hidden = contract_cols(d_expert, down_weight)
    d_gate = (d_hidden * up * sigma * (1.0 + gate * (1.0 - sigma))).astype(low)
    d_up = (d_hidden * silu).astype(low)
    d_pair = (contract_cols(d_gate, gate_weight) + contract_cols(d_up, up_weight)).astype(low)
    d_ffn_in = scatter_sum(spread_rows(d_pair).astype(low), 1, f32)

    expert_out = jnp.dot(hidden, down_weight, preferred_element_type=f32).astype(low)
    out_part = (spread_rows(expert_out) * pair_weight[:, :, None]).astype(low)
    mixed_out = scatter_sum(out_part, 2, f32)
    layer_output = (resid + mixed_out).astype(low)
    part_down = contract_rows(hidden, d_expert).astype(low)
    part_gate = contract_rows(rows_in, d_gate).astype(low)
    part_up = contract_rows(rows_in, d_up).astype(low)
    sum_gate, sum_up, sum_down = (
        lax.psum_scatter(part, "seq", scatter_dimension=0, tiled=True).astype(f32)
        for part in (part_gate, part_up, part_down)
    )

    grad_tokens = out_cotangent[0].astype(f32)
    d_scaled = d_ffn_in * gain_cols[:, 3]
    d_resid = grad_tokens + ffn_r * (
        d_scaled - ffn_n * jnp.mean(d_scaled * ffn_n, axis=-1, keepdims=True)
    )
    grad_g_ffn = jnp.sum(d_ffn_in * ffn_n, axis=0)
    d_branch = d_resid.astype(low)
    d_mix = contract_cols(d_branch, full_out).astype(low)
    d_mix_head = lax.all_to_all(d_mix, "seq", split_axis=1, concat_axis=0, tiled=True).reshape(
        group_tok, heads_local, HEAD_DIM
    )
    branch_cols = lax.all_to_all(d_branch, "seq", split_axis=1, concat_axis=0, tiled=True)
    d_probs = jnp.einsum("ihd,jhd->hij", d_mix_head, value_head, preferred_element_type=f32)
    delta_rows = jnp.sum(attn_probs * d_probs, axis=-1, keepdims=True)
    d_scores = (attn_probs * (d_probs - delta_rows)).astype(low)
    d_query = (
        jnp.einsum("hij,jhd->ihd", d_scores, key_head, preferred_element_type=f32) * score_scale
    ).astype(low)
    d_key = (
        jnp.einsum("hij,ihd->jhd", d_scores, query_head, preferred_element_type=f32) * score_scale
    ).astype(low)
    d_value = jnp.einsum(
        "hij,ihd->jhd", probs_low, d_mix_head, preferred_element_type=f32
    ).astype(low)
    dq_rot = rope_back(d_query.reshape(group_tok, local_width).astype(f32))
    dk_rot = rope_back(d_key.reshape(group_tok, local_width).astype(f32))
    grad_g_q = jnp.sum(dq_rot * q_n, axis=0)
    grad_g_k = jnp.sum(dk_rot * k_n, axis=0)
    dq_scaled = dq_rot * gain_q
    dk_scaled = dk_rot * gain_k
    dots = jnp.stack([jnp.sum(dq_scaled * q_n, axis=-1), jnp.sum(dk_scaled * k_n, axis=-1)])
    dots = lax.psum(dots, "seq") / width
    dq_raw = q_r * (dq_scaled - q_n * dots[0][:, None])
    dk_raw = k_r * (dk_scaled - k_n * dots[1][:, None])
    d_qkv = jnp.concatenate(
        [dq_raw.astype(low), dk_raw.astype(low), d_value.reshape(group_tok, local_width)], axis=1
    )
    d_attn_part = contract_cols(d_qkv, qkv_cols).astype(low)
    d_attn_in = lax.psum_scatter(d_attn_part, "seq", scatter_dimension=0, tiled=True).astype(f32)
    own_n = lax.dynamic_slice_in_dim(group_n, seq_at * tok_rows, tok_rows)
    own_r = lax.dynamic_slice_in_dim(group_r, seq_at * tok_rows, tok_rows)
    dx_scaled = d_attn_in * gain_cols[:, 0]
    dx_norm = own_r * (dx_scaled - own_n * jnp.mean(dx_scaled * own_n, axis=-1, keepdims=True))
    grad_g_attn = jnp.sum(d_attn_in * own_n, axis=0)
    input_grad = (d_resid + dx_norm).astype(low)

    term_qkv = contract_rows(attn_in, d_qkv).astype(low)
    term_out = contract_rows(mix_all, branch_cols).astype(low)
    terms = jnp.concatenate([term_qkv, term_out], axis=1).reshape(experts, weight_rows, -1)
    sums = scatter_sum(terms, 3, low)
    sums_all = lax.all_gather(sums, "seq", axis=0, tiled=False).astype(f32)
    rows_qkv = (
        sums_all[:, :, : 3 * local_width]
        .reshape(seq_count, weight_rows, 3, local_width)
        .transpose(1, 2, 0, 3)
        .reshape(weight_rows, 3 * width)
    )
    rows_out = sums_all[:, :, 3 * local_width :].transpose(1, 0, 2).reshape(weight_rows, width)
    zeros = jnp.zeros((width,), f32)
    gain_terms = jnp.stack(
        [
            grad_g_attn,
            lax.dynamic_update_slice_in_dim(zeros, grad_g_q, seq_at * local_width, 0),
            lax.dynamic_update_slice_in_dim(zeros, grad_g_k, seq_at * local_width, 0),
            grad_g_ffn,
        ]
    )
    gain_terms = lax.psum(gain_terms, ("seq", "shard"))
    rows_gain = lax.dynamic_slice_in_dim(gain_terms, shard_at * weight_rows, weight_rows, 1).T
    return (
        layer_output[None],
        input_grad[None],
        rows_qkv,
        rows_out,
        rows_gain,
        sum_gate[None],
        sum_up[None],
        sum_down[None],
    )


def solution(mesh):
    in_specs = (
        P("shard", "seq", None),
        P("shard", None),
        P("shard", None),
        P("shard", "seq", None),
        P("shard", "seq", None),
        P("shard", None),
        P("shard", None),
        P("shard", None),
        P("shard", None, None),
        P("shard", None, None),
        P("shard", None, None),
        P("shard", "seq", None),
    )
    out_specs = (
        P("shard", "seq", None),
        P("shard", "seq", None),
        P("shard", None),
        P("shard", None),
        P("shard", None),
        P("shard", "seq", None),
        P("shard", "seq", None),
        P("shard", "seq", None),
    )
    return jax.shard_map(shards, mesh=mesh, in_specs=in_specs, out_specs=out_specs, check_vma=False)
```

time: 1520 us -> 950 us (0.62)
  waiting for transfers between devices: 1040 us -> 300 us
  Pallas kernels: 0 us -> 268 us
  starting transfers between devices: 119 us -> 12.3 us
  blocking collectives: 28.9 us -> 94.8 us
  local copies, waits for them, and re-layouts: 83.7 us -> 28.7 us
    all_to_all x10 -> x1, waiting for transfers between devices: 401 us -> 0.01 us  [shards(): lax.all_to_all(d_branch, 'seq', split_axis=1, concat_axis=0, tiled=True)]
    reduce_scatter x5 -> x4, waiting for transfers between devices: 395 us -> 25.6 us  [the longest x3 25.6 us: shards(): lax.psum_scatter(part, 'seq', scatter_dimension=0, tiled=True).astype(f32)]
    pallas_call x0 -> x3, Pallas kernels: none -> 268 us  [scatter_sum(): pl.pallas_call(functools.partial(scatter_kernel, stages), out_shape=jax.S...]
    all_gather x2 -> x7, waiting for transfers between devices: 120 us -> 265 us  [the longest x1 102 us: shards(): lax.all_gather(own_cols.reshape(weight_rows, 3 * local_width), 'shard', a...]
    all_to_all x10 -> x1, starting transfers between devices: 112 us -> 4.21 us  [shards(): lax.all_to_all(d_branch, 'seq', split_axis=1, concat_axis=0, tiled=True)]
    psum x1 -> x0, waiting for transfers between devices: 58 us -> none  [shards(): lax.psum(rows_qkv.astype(jnp.bfloat16), 'seq').astype(jnp.float32)]
    unnamed x10 -> x11, waiting for transfers between devices: 56.6 us -> 2.52 us
    psum x1 -> x3, blocking collectives: 4.93 us -> 51 us  [the longest x1 41.1 us: shards(): gain_terms = lax.psum(gain_terms, ('seq', 'shard'))]
  transfers between devices with their start and end apart: 21 -> 14, of which waited for: 19 -> 6; matrix products, arithmetic and copies ran while one was open for 15% -> 16% of each run, Pallas kernels for 0% -> 7%
where the time goes in v1:
time: 950 us; the launch traced here: 942 us
  waiting for transfers between devices  300 us (32%)
  Pallas kernels  268 us (28%)
  matrix products  171 us (18%)
  blocking collectives  94.8 us (10%)
  other arithmetic  52.3 us (6%)
  local copies, waits for them, and re-layouts  28.7 us (3%)
  between operations  15 us (2%)
  starting transfers between devices  12.3 us (1%)
    pallas_call x3, Pallas kernels, scatter_sum(): pl.pallas_call(functools.partial(scatter_kernel, stages), out_shape=jax.S...  268 us
    all_gather x1, waiting for transfers between devices, shards(): lax.all_gather(own_cols.reshape(weight_rows, 3 * local_width), 'shard', a...  102 us
    all_gather x1, waiting for transfers between devices, shards(): ffn_all = lax.all_gather(ffn_in, 'shard', axis=0, tiled=False)  67.6 us
    dot_general x5, matrix products, contract_cols(): lax.dot_general(left_side, right_side, (((1,), (1,)), ((), ())), preferre...  54.3 us
    all_gather x1, waiting for transfers between devices, shards(): grad_all = lax.all_gather(out_cotangent[0], 'shard', axis=0, tiled=False)  48.2 us
    all_gather x1, waiting for transfers between devices, shards(): full_out = lax.all_gather(weight_out, 'shard', axis=0, tiled=True)  47.9 us
    dot_general x5, matrix products, contract_rows(): lax.dot_general(left_side, right_side, (((0,), (0,)), ((), ())), preferre...  43.5 us
    psum x1, blocking collectives, shards(): gain_terms = lax.psum(gain_terms, ('seq', 'shard'))  41.1 us
  transfers between devices with their start and end apart: 14, of which 6 were waited for; matrix products, arithmetic and copies ran while one was open for 16% of the time, Pallas kernels for 7%

profile of v1, /device:TPU:0, one launch (start us, length us, event | category | flops | bytes accessed | tf_op | source)
XLA Modules:
  0.0 942.3 jit_solution(14227092485379068563)
XLA Ops:
  8.0 1.9 copy.130
  12.6 23.1 %all_gather.37 = bf16[2048,4]{0,1:T(4,128)(2,1)S(1)} all-gather(bf16[128,4]{0,1:T(4,128)(2,1)S(1)} %copy-done.26), channel_id=1, replica_groups=mesh['seq'=2,'shard'=16] {'shard'}, dimensions={0}, use_global_device_ids=true | all-gather | bytes 17408 | tf_op jit(solution)/shard_map/all_gather | solution.py:284
  36.6 1.5 fusion.12
  38.1 101.7 %all-gather.12.cloned.1.call-done = bf16[2048,3072]{0,1:T(8,128)(2,1)} async-done(((bf16[128,3072]{0,1:T(8,128)(2,1)}), bf16[2048,3072]{0,1:T(8,128)(2,1)}) %all-gather.12.cloned.1.call-update) | async-done | bytes 12582928 | tf_op jit(solution)/shard_map/all_gather | solution.py:281
  139.8 6.8 fusion.47
  146.6 1.7 copy-done
  148.5 4.9 psum.21
  153.5 1.8 multiply_bitcast_fusion.1
  157.2 2.5 fusion.74
  159.7 2.3 convolution_convert_fusion.11
  163.1 3.5 all-to-all-start
  166.6 47.9 %all-gather.14.cloned.1.call-done = bf16[2048,2048]{1,0:T(8,128)(2,1)} async-done(((bf16[128,2048]{1,0:T(8,128)(2,1)}), bf16[2048,2048]{1,0:T(8,128)(2,1)}) %all-gather.14.cloned.1.call-update) | async-done | bytes 8388624 | tf_op jit(solution)/shard_map/all_gather | solution.py:287
  214.5 4.8 multiply_reduce_fusion.5
  220.3 20.7 %all-gather.1 = f32[256,128]{1,0:T(8,128)S(1)} all-gather(f32[16,128]{1,0:T(8,128)S(1)} %select_reduce_fusion.1), channel_id=3, replica_groups=mesh['seq'=2,'shard'=16] {'shard'}, dimensions={0}, use_global_device_ids=true | all-gather | bytes 139264 | tf_op jit(solution)/shard_map/all_gather | solution.py:289
  241.7 48.2 %all-gather.16.cloned.1.call-done = bf16[16,128,2048]{2,1,0:T(8,128)(2,1)} async-done(((bf16[1,128,2048]{2,1,0:T(8,128)(2,1)}), bf16[16,128,2048]{2,1,0:T(8,128)(2,1)}) %all-gather.16.cloned.1.call-update) | async-done | bytes 8388624 | tf_op jit(solution)/shard_map/all_gather | solution.py:288
  290.0 7.9 multiply_convert_fusion.1
  297.9 67.6 %all-gather.22.cloned.1.call-done = bf16[2048,2048]{1,0:T(8,128)(2,1)} async-done(((bf16[128,2048]{1,0:T(8,128)(2,1)}), bf16[2048,2048]{1,0:T(8,128)(2,1)}) %all-gather.22.cloned.1.call-update) | async-done | bytes 8388624 | tf_op jit(solution)/shard_map/all_gather | solution.py:342
  365.5 5.3 convolution_convert_fusion.3
  370.8 8.6 fusion.6
  379.4 8.5 fusion.10
  388.0 15.4 %multiply_convert_fusion.2 = (bf16[1536,1024]{1,0:T(8,128)(2,1)}, bf16[1536,1024]{1,0:T(8,128)(2,1)}, bf16[1536,1024]{1,0:T(8,128)(2,1)}) fusion(f32[1536,1024]{1,0:T(8,128)} %fusion.10, f32[1536,1024]{1,0:T(8,128)} %fusion.6, bf16[1536,2048]{1,0:T(8,128)(2,1)S(1)} %bitcast.214, bf16[1,1024,2048]{2,1,0:T(8,128)(2,1)} %param.22), kind=kOutput, calls=%fused_computation.7 | convolution fusion | flops 6466043904 | bytes 32505856 | tf_op jit(solution)/shard_map/dot_general | solution.py:65
  403.4 12.4 %fusion.8 = f32[1536,2048]{1,0:T(8,128)} fusion(bf16[1536,1024]{1,0:T(8,128)(2,1)} %get-tuple-element.49, bf16[1,2048,1024]{2,1,0:T(8,128)(2,1)} %param.20), kind=kOutput, calls=%fused_computation.20 | convolution fusion | flops 6442450944 | bytes 19922944 | tf_op jit(solution)/shard_map/dot_general | solution.py:65
  415.8 11.1 %add_convert_fusion = bf16[1536,2048]{1,0:T(8,128)(2,1)S(1)} fusion(f32[1536,2048]{1,0:T(8,128)} %fusion.8, bf16[1536,1024]{1,0:T(8,128)(2,1)} %get-tuple-element.48, bf16[1,2048,1024]{2,1,0:T(8,128)(2,1)S(1)} %copy-done.29), kind=kOutput, calls=%fused_computation.3 | convolution fusion | flops 6448742400 | bytes 26214400 | tf_op jit(solution)/shard_map/dot_general | solution.py:65
  426.8 5.6 convolution_convert_fusion.2
  432.5 69.0 %scatter_sum_1.1 = f32[128,2048]{1,0:T(8,128)} custom-call(bf16[4,2,2,128,2048]{4,3,2,1,0:T(8,128)(2,1)} %bitcast.204), custom_call_target="tpu_custom_call" | custom-call | tf_op jit(solution)/shard_map/scatter_sum_1/pallas_call | solution.py:213
  501.5 1.6 multiply_reduce_fusion.1
  503.0 1.6 fusion.68
  504.6 6.3 convolution_convert_fusion.9
  511.7 3.5 all-to-all-start.1
  516.6 6.2 all-to-all-done.1
  522.8 4.2 all-to-all-start.2
  527.7 2.2 convolution_convert_fusion.10
  530.0 1.7 multiply_reduce_fusion
  532.9 1.5 fusion.17
  534.4 1.7 fusion.19
  537.1 3.0 multiply_subtract_fusion.1
  541.4 4.9 psum.22
  546.3 4.1 multiply_convert_fusion.8
  550.5 2.8 convolution_convert_fusion.7
  553.3 6.9 convolution_convert_fusion
  560.2 12.1 %pad_maximum_fusion = bf16[2048,4096]{1,0:T(8,128)(2,1)} fusion(bf16[2048,1024]{1,0:T(8,128)(2,1)S(1)} %convolution_convert_fusion.7, bf16[2048,3072]{1,0:T(8,128)(2,1)} %convolution_convert_fusion), kind=kLoop, calls=%fused_computation.1 | loop fusion | flops 33554432 | bytes 33554432 | tf_op jit(solution)/shard_map/concatenate | solution.py:437
  572.3 129.5 %scatter_sum_3.1 = bf16[128,4096]{1,0:T(8,128)(2,1)} custom-call(bf16[4,2,2,128,4096]{4,3,2,1,0:T(8,128)(2,1)} %bitcast.203), custom_call_target="tpu_custom_call" | custom-call | tf_op jit(solution)/shard_map/scatter_sum_3/pallas_call | solution.py:213
  702.1 9.2 convolution_convert_fusion.8
  711.3 11.5 %convolution_convert_fusion.5 = bf16[2048,1024]{1,0:T(8,128)(2,1)} fusion(bf16[1536,2048]{1,0:T(8,128)(2,1)} %bitcast.209, bf16[1536,1024]{1,0:T(8,128)(2,1)} %get-tuple-element.48), kind=kOutput, calls=%fused_computation.25 | convolution fusion | flops 6444548096 | bytes 13631488 | tf_op jit(solution)/shard_map/dot_general | solution.py:59
  722.9 11.3 %convolution_convert_fusion.4 = bf16[1024,2048]{1,0:T(8,128)(2,1)} fusion(bf16[1536,1024]{1,0:T(8,128)(2,1)} %get-tuple-element.50, bf16[1536,2048]{1,0:T(8,128)(2,1)} %bitcast.211), kind=kOutput, calls=%fused_computation.24 | convolution fusion | flops 6444548096 | bytes 13631488 | tf_op jit(solution)/shard_map/dot_general | solution.py:59
  734.5 11.2 %convolution_convert_fusion.6 = bf16[2048,1024]{1,0:T(8,128)(2,1)} fusion(bf16[1536,2048]{1,0:T(8,128)(2,1)} %bitcast.210, bf16[1536,1024]{1,0:T(8,128)(2,1)} %get-tuple-element.49), kind=kOutput, calls=%fused_computation.26 | convolution fusion | flops 6444548096 | bytes 13631488 | tf_op jit(solution)/shard_map/dot_general | solution.py:59
  745.7 1.5 convert_multiply_fusion
  747.3 9.5 %convolution_convert_fusion.1 = bf16[1536,2048]{1,0:T(8,128)(2,1)S(1)} fusion(bf16[1536,1024]{1,0:T(8,128)(2,1)} %get-tuple-element.50, bf16[1,1024,2048]{2,1,0:T(8,128)(2,1)} %param.22), kind=kOutput, calls=%fused_computation.6 | convolution fusion | flops 6445596672 | bytes 13631488 | tf_op jit(solution)/shard_map/dot_general | solution.py:377
  756.8 4.6 multiply_convert_fusion
  761.5 69.5 %scatter_sum_2.1 = f32[128,2048]{1,0:T(8,128)} custom-call(bf16[4,2,2,128,2048]{4,3,2,1,0:T(8,128)(2,1)} %bitcast.205), custom_call_target="tpu_custom_call" | custom-call | tf_op jit(solution)/shard_map/scatter_sum_2/pallas_call | solution.py:213
  831.1 3.6 slice.96
  834.7 2.5 convert.28
  837.2 3.5 copy.173
  840.7 3.8 copy.155
  844.5 3.7 copy.157
  848.2 1.4 slice_bitcast_fusion
  849.6 1.1 copy.179
  850.7 1.7 fusion.26
  852.5 41.1 %psum.23 = f32[4,2048]{1,0:T(4,128)S(1)} all-reduce(f32[4,2048]{1,0:T(4,128)S(1)} %pad_maximum_fusion.6), channel_id=1, replica_groups=mesh['seq'=2,'shard'=16] {'seq','shard'}, use_global_device_ids=true, to_apply=%region_25.26 | all-reduce | flops 8192 | bytes 65536 | tf_op jit(solution)/shard_map/psum | solution.py:456
  894.2 3.1 fusion.39
  897.3 4.2 bitcast_convert_fusion.1
  901.5 4.1 bitcast_convert_fusion
  905.7 25.6 %reduce-scatter.7.cloned.1.call-done = bf16[1024,1024]{1,0:T(8,128)(2,1)} async-done(((bf16[2048,1024]{1,0:T(8,128)(2,1)}), bf16[1024,1024]{1,0:T(8,128)(2,1)}) %reduce-scatter.7.cloned.1.call-update) | async-done | bytes 2097168 | tf_op jit(solution)/shard_map/reduce_scatter | solution.py:385
  931.3 4.1 bitcast_convert_fusion.2
  (148 shorter events, 17.1 us)
Async XLA Ops:
  7.2 5.0 copy-start.31
  7.2 5.0 copy-start.30
  7.2 5.4 copy-start.26
  7.2 29.4 %all-gather.20.cloned.1.call-start = ((), (), s32[]{:S(2)}) async-start(), calls=%async_computation.15 | async-start | bytes 1572864 | tf_op jit(solution)/shard_map/all_gather | solution.py:285
  7.9 131.9 %all-gather.12.cloned.1.call-start = ((), (), s32[]{:S(2)}) async-start(), calls=%async_computation.7 | async-start | bytes 13369344 | tf_op jit(solution)/shard_map/all_gather | solution.py:281
  10.9 203.6 %all-gather.14.cloned.1.call-start = ((), (), s32[]{:S(2)}) async-start(), calls=%async_computation.8 | async-start | bytes 8912896 | tf_op jit(solution)/shard_map/all_gather | solution.py:287
  11.6 278.4 %all-gather.16.cloned.1.call-start = ((), (), s32[]{:S(2)}) async-start(), calls=%async_computation.9 | async-start | bytes 8912896 | tf_op jit(solution)/shard_map/all_gather | solution.py:288
  146.6 1.7 copy-start
  157.2 4.9 copy-start.14
  157.2 4.9 copy-start.16
  157.2 4.9 copy-start.18
  159.7 54.8 %copy-start.10 = (bf16[1,128,2048]{2,1,0:T(8,128)(2,1)S(1)}, bf16[1,128,2048]{2,1,0:T(8,128)(2,1)}, u32[]{:S(2)}) copy-start(bf16[1,128,2048]{2,1,0:T(8,128)(2,1)} %param.12) | copy-start | bytes 1572868
  162.1 57.2 %copy-start.13 = (bf16[8,128,256]{2,1,0:T(8,128)(2,1)}, bf16[8,128,256]{2,1,0:T(8,128)(2,1)S(1)}, u32[]{:S(2)}) copy-start(bf16[8,128,256]{2,1,0:T(8,128)(2,1)S(1)} %convolution_convert_fusion.11) | copy-start | bytes 1572868
  163.1 51.5 %all-to-all-start = ((bf16[2,128,1024]{1,2,0:T(8,128)(2,1)}), bf16[2,128,1024]{1,2,0:T(8,128)(2,1)S(1)}, u32[]{:S(2)}, u32[]{:S(2)}) async-start(bf16[2,128,1024]{1,2,0:T(8,128)(2,1)} %copy.137), calls=%async_computation | async-start | bytes 1048576 | tf_op jit(solution)/shard_map/all_to_all | solution.py:335
  166.6 198.9 %all-gather.22.cloned.1.call-start = ((), (), s32[]{:S(2)}) async-start(), calls=%async_computation.16 | async-start | bytes 8912896 | tf_op jit(solution)/shard_map/all_gather | solution.py:342
  214.5 5.8 copy-start.24
  214.5 5.8 copy-start.25
  241.0 56.8 %copy-start.22 = (f32[16,1,128]{2,1,0:T(1,128)}, f32[16,1,128]{2,1,0:T(1,128)S(1)}, u32[]{:S(2)}) copy-start(f32[16,1,128]{2,1,0:T(1,128)S(1)} %get-tuple-element.47) | copy-start | bytes 24580
  365.5 5.3 copy-start.28
  370.8 8.7 copy-start.2
  370.8 8.6 copy-start.27
  370.8 17.1 %slice-start = ((s8[6291456]{0:T(1024)(128)(4,1)}), s8[4194304]{0:T(1024)(128)(4,1)S(1)}, s32[]{:S(2)}) async-start(s8[6291456]{0:T(1024)(128)(4,1)} %bitcast.212), calls=%async_computation.18 | async-start | bytes 8388608
  379.4 8.5 slice-start.1
  403.4 12.4 %copy-start.29 = (bf16[1,2048,1024]{2,1,0:T(8,128)(2,1)S(1)}, bf16[1,2048,1024]{2,1,0:T(8,128)(2,1)}, u32[]{:S(2)}) copy-start(bf16[1,2048,1024]{2,1,0:T(8,128)(2,1)} %param.21) | copy-start | bytes 12582916
  432.5 70.6 %copy-start.8 = (bf16[1,128,2048]{2,1,0:T(8,128)(2,1)S(1)}, bf16[1,128,2048]{2,1,0:T(8,128)(2,1)}, u32[]{:S(2)}) copy-start(bf16[1,128,2048]{2,1,0:T(8,128)(2,1)} %param.23) | copy-start | bytes 1572868
  511.7 11.1 %all-to-all-start.1 = ((bf16[128,2,1024]{2,0,1:T(8,128)(2,1)}), bf16[128,2,1024]{2,0,1:T(8,128)(2,1)S(1)}, u32[]{:S(2)}, u32[]{:S(2)}) async-start(bf16[128,2,1024]{2,0,1:T(8,128)(2,1)} %bitcast.202), calls=%async_computation.1 | async-start | bytes 1048576 | tf_op jit(solution)/shard_map/all_to_all | solution.py:397
  515.2 35.3 %all-gather.18.cloned.1.call-start = ((), (), s32[]{:S(2)}) async-start(), calls=%async_computation.11 | async-start | bytes 1572864 | tf_op jit(solution)/shard_map/all_gather | solution.py:336
  522.8 27.6 %all-to-all-start.2 = ((bf16[128,2,1024]{2,0,1:T(8,128)(2,1)}), bf16[128,2,1024]{2,0,1:T(8,128)(2,1)}, u32[]{:S(2)}, u32[]{:S(2)}) async-start(bf16[128,2,1024]{2,0,1:T(8,128)(2,1)} %bitcast.201), calls=%async_computation.3 | async-start | bytes 1048576 | tf_op jit(solution)/shard_map/all_to_all | solution.py:400
  527.1 304.0 %all-gather.24.cloned.1.call-start = ((), (), s32[]{:S(2)}) async-start(), calls=%async_computation.17 | async-start | bytes 3145728 | tf_op jit(solution)/shard_map/all_gather | solution.py:439
  527.7 2.3 copy-start.12
  531.7 1.0 copy-start.17
  531.7 1.2 copy-start.19
  531.7 2.7 copy-start.15
  537.1 3.2 copy-start.1
  540.1 1.1 copy-start.6
  540.1 1.3 copy-start.7
  550.5 2.8 copy-start.5
  550.5 2.8 copy-start.11
  550.5 2.8 copy-start.20
  550.5 2.8 copy-start.21
  701.8 148.9 %reduce-scatter.5.cloned.1.call-start = ((), (), s32[]{:S(2)}) async-start(), calls=%async_computation.10 | async-start | bytes 1572864 | tf_op jit(solution)/shard_map/reduce_scatter | solution.py:427
  711.3 186.1 %reduce-scatter.9.cloned.1.call-start = ((), (), s32[]{:S(2)}) async-start(), calls=%async_computation.13 | async-start | bytes 6291456 | tf_op jit(solution)/shard_map/reduce_scatter | solution.py:385
  722.8 178.7 %reduce-scatter.11.cloned.1.call-start = ((), (), s32[]{:S(2)}) async-start(), calls=%async_computation.14 | async-start | bytes 6291456 | tf_op jit(solution)/shard_map/reduce_scatter | solution.py:385
  734.2 197.1 %reduce-scatter.7.cloned.1.call-start = ((), (), s32[]{:S(2)}) async-start(), calls=%async_computation.12 | async-start | bytes 6291456 | tf_op jit(solution)/shard_map/reduce_scatter | solution.py:385
  747.3 9.6 %copy-start.23 = (f32[16,1,128]{2,1,0:T(1,128)S(1)}, f32[16,1,128]{2,1,0:T(1,128)}, u32[]{:S(2)}) copy-start(f32[16,1,128]{2,1,0:T(1,128)} %copy-done.22) | copy-start | bytes 24580
  831.1 3.6 copy-start.4
  848.1 46.0 %copy-start.3 = (f32[128,2048]{1,0:T(8,128)S(1)}, f32[128,2048]{1,0:T(8,128)}, u32[]{:S(2)}) copy-start(f32[128,2048]{1,0:T(8,128)} %scatter_sum_1.1) | copy-start | bytes 3145732
  848.2 46.0 %copy-start.9 = (bf16[1,128,2048]{2,1,0:T(8,128)(2,1)S(1)}, bf16[1,128,2048]{2,1,0:T(8,128)(2,1)}, u32[]{:S(2)}) copy-start(bf16[1,128,2048]{2,1,0:T(8,128)(2,1)} %param.23) | copy-start | bytes 1572868
Sparse Core Ops, SparseCore 0:
  9.5 23.9 all-gather.19
  36.3 103.4 all-gather.11
  142.0 72.4 all-gather.13
  216.5 73.3 all-gather.15
  292.5 72.8 all-gather.21
  517.2 27.2 all-gather.17
  701.9 34.2 all-gather.23
  738.4 20.3 reduce-scatter.4
  761.7 54.3 reduce-scatter.8
  818.3 55.0 reduce-scatter.10
  876.3 54.9 reduce-scatter.6

commit v2 on v1

--- a/solution.py
+++ b/solution.py
@@ -68,173 +68,284 @@
 
 
 MESH_ID = pl.DeviceIdType.MESH
+VMEM_LIMIT = 60 * 1024 * 1024
 ROW_TILE = 16
 
 
-def shard_stages(count):
-    inner = 2 if count <= 16 else 4
-    return (inner, 2, count // (2 * inner))
-
-
-def scatter_kernel(stages, part_ref, total_ref, *scratch):
-    in_one, sum_one, in_two, sum_two, in_three = scratch[:5]
-    send_one, recv_one, send_two, recv_two, send_three, recv_three = scratch[5:]
-    n1, n2, n3 = stages
-    rows = total_ref.shape[0]
+def low_bit(index):
+    return index & -index
+
+
+def bit_list(count):
+    return [1 << b for b in range(count.bit_length() - 1)]
+
+
+def relative_place(count, me):
+    values = [(bit, lax.rem(me // bit, 2)) for bit in bit_list(count)]
+
+    def place(r):
+        total = 0
+        for bit, value in values:
+            total = total + bit * ((1 - value) if r & bit else value)
+        return total
+
+    return place
+
+
+def meet(count, place, seq, seq_count=1):
+    barrier = pltpu.get_barrier_semaphore()
+    for bit in bit_list(count):
+        pl.semaphore_signal(barrier, 1, device_id=(seq, place(bit)), device_id_type=MESH_ID)
+    for j in range(1, seq_count):
+        pl.semaphore_signal(
+            barrier, 1, device_id=(lax.rem(seq + j, seq_count), place(0)), device_id_type=MESH_ID
+        )
+    pl.semaphore_wait(barrier, len(bit_list(count)) + seq_count - 1)
+
+
+def remote(src, dst, send_sem, recv_sem, device):
+    return pltpu.make_async_remote_copy(
+        src_ref=src,
+        dst_ref=dst,
+        send_sem=send_sem,
+        recv_sem=recv_sem,
+        device_id=device,
+        device_id_type=MESH_ID,
+    )
+
+
+def arrival_order(count):
+    def key(r):
+        later = r >> 2
+        return (later + ((r >> 1) & 1), (r >> 1) & 1)
+
+    return sorted(range(2, count, 2), key=key)
+
+
+def gather_kernel(count, groups, *refs):
+    arrays = sum(len(group) for group in groups)
+    own, full = refs[:arrays], refs[arrays : 2 * arrays]
+    send, recv, local = refs[2 * arrays :]
     me = lax.axis_index("shard")
     seq = lax.axis_index("seq")
-    c = lax.rem(me, n1)
-    y = lax.rem(me // n1, n2)
-    z = me // (n1 * n2)
-
-    def device(z_to, y_to, c_to):
-        return (seq, (z_to * n2 + y_to) * n1 + c_to)
-
-    barrier = pltpu.get_barrier_semaphore()
-    for j in range(1, n1):
-        pl.semaphore_signal(
-            barrier, 1, device_id=device(z, y, lax.rem(c + j, n1)), device_id_type=MESH_ID
+    place = relative_place(count, me)
+    meet(count, place, seq)
+    copies = {}
+
+    def send_on(a, r):
+        source = own[a] if r == 0 else full[a].at[place(r)]
+        below = low_bit(r) if r else count
+        for bit in reversed(bit_list(count)):
+            if bit < below:
+                copy = remote(
+                    source,
+                    full[a].at[place(r)],
+                    send.at[a, r | bit],
+                    recv.at[a, r | bit],
+                    (seq, place(bit)),
+                )
+                copies[a, r | bit] = copy
+
+    def start(a, r):
+        send_on(a, r)
+        below = low_bit(r) if r else count
+        bits = [bit for bit in bit_list(count) if bit < below]
+        for bit in sorted(bits, key=lambda bit: (bit < 4, bit)):
+            copies[a, r | bit].start()
+
+    keeps = []
+    for a in range(arrays):
+        keep = pltpu.make_async_copy(own[a], full[a].at[me], local.at[a])
+        keep.start()
+        keeps.append(keep)
+    arrivals = arrival_order(count)
+    last = max(i for i, r in enumerate(arrivals) if not r & 2) + 1
+    events = [(0, 0)]
+    for g in range(len(groups)):
+        events += [(g, r) for r in arrivals[:last]]
+        if g + 1 < len(groups):
+            events.append((g + 1, 0))
+        events += [(g, r) for r in arrivals[last:]]
+    for g, r in events:
+        for a in groups[g]:
+            if r:
+                copies[a, r].wait_recv()
+            start(a, r)
+    for a in range(arrays):
+        for r in range(1, count, 2):
+            copies[a, r].wait_recv()
+    for copy in copies.values():
+        copy.wait_send()
+    for keep in keeps:
+        keep.wait()
+
+
+def gather_blocks(blocks, collective_id, groups=((0,),)):
+    count = lax.axis_size("shard")
+    arrays = len(blocks)
+    return pl.pallas_call(
+        functools.partial(gather_kernel, count, groups),
+        out_shape=[jax.ShapeDtypeStruct((count,) + b.shape, b.dtype) for b in blocks],
+        in_specs=[pl.BlockSpec(memory_space=pltpu.VMEM)] * arrays,
+        out_specs=[pl.BlockSpec(memory_space=pl.ANY)] * arrays,
+        scratch_shapes=[
+            pltpu.SemaphoreType.DMA((arrays, count)),
+            pltpu.SemaphoreType.DMA((arrays, count)),
+            pltpu.SemaphoreType.DMA((arrays,)),
+        ],
+        compiler_params=pltpu.CompilerParams(collective_id=collective_id, has_side_effects=True),
+        name="gather_blocks_%d" % collective_id,
+    )(*blocks)
+
+
+def scatter_kernel(count, seq_count, arrays, sides, *refs):
+    parts, refs = refs[:arrays], refs[arrays:]
+    side_from, refs = refs[:sides], refs[sides:]
+    totals, refs = refs[:arrays], refs[arrays:]
+    side_to, refs = refs[:sides], refs[sides:]
+    held = refs[:arrays]
+    send, recv, seq_send, seq_recv, side_send, side_recv = refs[arrays:]
+    planes = seq_count if seq_count > 1 else 1 + (sides > 0)
+    me = lax.axis_index("shard")
+    seq = lax.axis_index("seq")
+    place = relative_place(count, me)
+    bits = bit_list(count)
+    meet(count, place, seq, planes)
+    copies = {}
+    shared = []
+    for i in range(sides):
+        half = side_to[i].shape[0]
+        copy = remote(
+            side_from[i].at[pl.ds(pl.multiple_of((1 - seq) * half, half), half)],
+            side_to[i],
+            side_send.at[i],
+            side_recv.at[i],
+            (1 - seq, me),
         )
-    for j in range(1, n2):
-        pl.semaphore_signal(
-            barrier, 1, device_id=device(z, lax.rem(y + j, n2), c), device_id_type=MESH_ID
-        )
-    for j in range(1, n3):
-        pl.semaphore_signal(
-            barrier, 1, device_id=device(lax.rem(z + j, n3), y, c), device_id_type=MESH_ID
-        )
-    pl.semaphore_wait(barrier, n1 + n2 + n3 - 3)
-
-    first, second, third = [], [], []
-    for k in range(n3):
-        z_to = lax.rem(z + k + 1, n3)
-        copies = []
-        for j in range(1, n1):
-            c_to = lax.rem(c + j, n1)
-            slot = n1 - 1 - j
-            copy = pltpu.make_async_remote_copy(
-                src_ref=part_ref.at[z_to, :, c_to],
-                dst_ref=in_one.at[k, slot],
-                send_sem=send_one.at[k, j - 1],
-                recv_sem=recv_one.at[k, slot],
-                device_id=device(z, y, c_to),
-                device_id_type=MESH_ID,
+        copy.start()
+        shared.append(copy)
+
+    def share(a):
+        for j in range(1, seq_count):
+            copy = remote(
+                totals[a].at[seq],
+                totals[a].at[seq],
+                seq_send.at[a, j - 1],
+                seq_recv.at[a, j - 1],
+                (lax.rem(seq + j, seq_count), me),
             )
             copy.start()
-            copies.append(copy)
-        first.append(copies)
-
-    def fold_one(k):
-        z_to = lax.rem(z + k + 1, n3)
-        for copy in first[k]:
-            copy.wait_recv()
+            shared.append(copy)
+
+    def start(a, r, source):
+        copy = remote(
+            source, held[a].at[r], send.at[a, r], recv.at[a, r], (seq, place(low_bit(r)))
+        )
+        copy.start()
+        copies[a, r] = copy
+
+    def fold(a, r, bit):
+        came = r | bit
+        copies[a, came].wait_recv()
+        rows = held[a].shape[1]
+        last = bit == bits[-1]
 
         def step(i, carry):
             at = pl.ds(pl.multiple_of(i * ROW_TILE, ROW_TILE), ROW_TILE)
-            for y_to in range(n2):
-                value = part_ref[z_to, y_to, c, at, :].astype(jnp.float32)
-                for slot in range(n1 - 1):
-                    value += in_one[k, slot, y_to, at, :].astype(jnp.float32)
-                sum_one[k, y_to, at, :] = value.astype(sum_one.dtype)
+            if bit == 1:
+                mine = parts[a][place(r), at, :]
+            else:
+                mine = held[a][r | (bit >> 1), at, :]
+            value = mine.astype(jnp.float32) + held[a][came, at, :].astype(jnp.float32)
+            if last and seq_count > 1:
+                totals[a][seq, at, :] = value.astype(totals[a].dtype)
+            elif last:
+                totals[a][at, :] = value.astype(totals[a].dtype)
+            else:
+                held[a][came, at, :] = value.astype(held[a].dtype)
             return carry
 
         lax.fori_loop(0, rows // ROW_TILE, step, 0)
-        copies = []
-        for j in range(1, n2):
-            y_to = lax.rem(y + j, n2)
-            slot = n2 - 1 - j
-            copy = pltpu.make_async_remote_copy(
-                src_ref=sum_one.at[k, y_to],
-                dst_ref=in_two.at[k, slot],
-                send_sem=send_two.at[k, j - 1],
-                recv_sem=recv_two.at[k, slot],
-                device_id=device(z, y_to, c),
-                device_id_type=MESH_ID,
-            )
-            copy.start()
-            copies.append(copy)
-        second.append(copies)
-
-    def fold_two(k):
-        for copy in second[k]:
-            copy.wait_recv()
-
-        def step(i, carry):
-            at = pl.ds(pl.multiple_of(i * ROW_TILE, ROW_TILE), ROW_TILE)
-            value = sum_one[k, y, at, :].astype(jnp.float32)
-            for slot in range(n2 - 1):
-                value += in_two[k, slot, at, :].astype(jnp.float32)
-            sum_two[k, at, :] = value.astype(sum_two.dtype)
-            return carry
-
-        lax.fori_loop(0, rows // ROW_TILE, step, 0)
-        if k < n3 - 1:
-            slot = n3 - 2 - k
-            copy = pltpu.make_async_remote_copy(
-                src_ref=sum_two.at[k],
-                dst_ref=in_three.at[slot],
-                send_sem=send_three.at[k],
-                recv_sem=recv_three.at[slot],
-                device_id=device(lax.rem(z + k + 1, n3), y, c),
-                device_id_type=MESH_ID,
-            )
-            copy.start()
-            third.append(copy)
-
-    for k in range(n3 + 1):
-        if k < n3:
-            fold_one(k)
-        if k > 0:
-            fold_two(k - 1)
-    for copy in third:
+        upper = bit << 1
+        if last:
+            share(a)
+        elif r & upper:
+            start(a, r, held[a].at[came])
+
+    def reversed_bits(u):
+        return sum(1 << (len(bits) - 3 - b) for b in range(len(bits) - 2) if u >> b & 1)
+
+    order = sorted(range(count // 4), key=reversed_bits, reverse=True)
+    chunks = [(a, u) for a in range(arrays) for u in order]
+    for a, u in chunks:
+        for r in (4 * u + 3, 4 * u + 1):
+            start(a, r, parts[a].at[place(r)])
+    for i in range(len(chunks) + len(bits) - 1):
+        for stage in range(len(bits)):
+            bit = bits[stage]
+            at = i - max(stage, 0)
+            if 0 <= at < len(chunks):
+                a, u = chunks[at]
+                if stage == 0:
+                    fold(a, 4 * u + 2, bit)
+                    fold(a, 4 * u, bit)
+                elif stage == 1 or 4 * u % (2 * bit) == 0:
+                    fold(a, 4 * u, bit)
+    for copy in shared:
         copy.wait_recv()
-
-    def finish(i, carry):
-        at = pl.ds(pl.multiple_of(i * ROW_TILE, ROW_TILE), ROW_TILE)
-        value = sum_two[n3 - 1, at, :].astype(jnp.float32)
-        for slot in range(n3 - 1):
-            value += in_three[slot, at, :].astype(jnp.float32)
-        total_ref[at, :] = value.astype(total_ref.dtype)
-        return carry
-
-    lax.fori_loop(0, rows // ROW_TILE, finish, 0)
-    for copies in first + second:
-        for copy in copies:
-            copy.wait_send()
-    for copy in third:
+    for copy in list(copies.values()) + shared:
         copy.wait_send()
 
 
-def scatter_sum(part, collective_id, out_dtype):
-    count, rows, cols = part.shape
-    stages = shard_stages(count)
-    n1, n2, n3 = stages
-    low = part.dtype
+def scatter_sum(parts, collective_id, out_dtype, seq_count=1, sides=()):
+    count = lax.axis_size("shard")
+    arrays = len(parts)
+    lead = (seq_count,) if seq_count > 1 else ()
+    others = max(seq_count - 1, 1)
     return pl.pallas_call(
-        functools.partial(scatter_kernel, stages),
-        out_shape=jax.ShapeDtypeStruct((rows, cols), out_dtype),
-        in_specs=[pl.BlockSpec(memory_space=pltpu.VMEM)],
-        out_specs=pl.BlockSpec(memory_space=pltpu.VMEM),
-        scratch_shapes=[
-            pltpu.VMEM((n3, n1 - 1, n2, rows, cols), low),
-            pltpu.VMEM((n3, n2, rows, cols), low),
-            pltpu.VMEM((n3, n2 - 1, rows, cols), low),
-            pltpu.VMEM((n3, rows, cols), low),
-            pltpu.VMEM((n3 - 1, rows, cols), low),
-            pltpu.SemaphoreType.DMA((n3, n1 - 1)),
-            pltpu.SemaphoreType.DMA((n3, n1 - 1)),
-            pltpu.SemaphoreType.DMA((n3, n2 - 1)),
-            pltpu.SemaphoreType.DMA((n3, n2 - 1)),
-            pltpu.SemaphoreType.DMA((n3 - 1,)),
-            pltpu.SemaphoreType.DMA((n3 - 1,)),
+        functools.partial(scatter_kernel, count, seq_count, arrays, len(sides)),
+        out_shape=[jax.ShapeDtypeStruct(lead + p.shape[1:], out_dtype) for p in parts]
+        + [jax.ShapeDtypeStruct((s.shape[0] // 2, s.shape[1]), s.dtype) for s in sides],
+        in_specs=[pl.BlockSpec(memory_space=pltpu.VMEM)] * arrays
+        + [pl.BlockSpec(memory_space=pl.ANY)] * len(sides),
+        out_specs=[pl.BlockSpec(memory_space=pltpu.VMEM)] * arrays
+        + [pl.BlockSpec(memory_space=pl.ANY)] * len(sides),
+        scratch_shapes=[pltpu.VMEM(p.shape, p.dtype) for p in parts]
+        + [
+            pltpu.SemaphoreType.DMA((arrays, count)),
+            pltpu.SemaphoreType.DMA((arrays, count)),
+            pltpu.SemaphoreType.DMA((arrays, others)),
+            pltpu.SemaphoreType.DMA((arrays, others)),
+            pltpu.SemaphoreType.DMA((max(len(sides), 1),)),
+            pltpu.SemaphoreType.DMA((max(len(sides), 1),)),
         ],
         compiler_params=pltpu.CompilerParams(
-            collective_id=collective_id,
-            has_side_effects=True,
-            vmem_limit_bytes=60 * 1024 * 1024,
+            collective_id=collective_id, has_side_effects=True, vmem_limit_bytes=VMEM_LIMIT
         ),
         name="scatter_sum_%d" % collective_id,
-    )(part.reshape(n3, n2, n1, rows, cols))
+    )(*parts, *sides)
+
+
+def place_kernel(refs_in, seq_count, *refs):
+    for i, o in enumerate(refs_in):
+        out_ref, base = refs[len(refs_in) + o[0]], o[1]
+        cols = refs[i].shape[2]
+        for s in range(seq_count):
+            out_ref[:, base + s * cols : base + (s + 1) * cols] = refs[i][s].astype(out_ref.dtype)
+
+
+def place_rows(pieces, targets, out_cols):
+    seq_count, rows, _ = pieces[0].shape
+    return pl.pallas_call(
+        functools.partial(place_kernel, targets, seq_count),
+        out_shape=[jax.ShapeDtypeStruct((rows, cols), jnp.float32) for cols in out_cols],
+        in_specs=[pl.BlockSpec(memory_space=pltpu.VMEM)] * len(pieces),
+        out_specs=[pl.BlockSpec(memory_space=pltpu.VMEM)] * len(out_cols),
+        name="place_rows",
+    )(*pieces)
+
+
+GAIN_LANES = 128
 
 
 def pair_tables(expert_list, prob_list, expert_count):
@@ -277,16 +388,31 @@
     def take_seq(array, axis):
         return lax.dynamic_index_in_dim(array, seq_at, axis, keepdims=False)
 
+    def seq_sum(part):
+        if seq_count != 2:
+            return lax.psum_scatter(part, "seq", scatter_dimension=0, tiled=True).astype(f32)
+        halves = part.reshape(2, part.shape[0] // 2, part.shape[1])
+        there = lax.dynamic_index_in_dim(halves, 1 - seq_at, 0, keepdims=False)
+        here = lax.dynamic_index_in_dim(halves, seq_at, 0, keepdims=False)
+        came = lax.ppermute(there, "seq", [(0, 1), (1, 0)])
+        return here.astype(f32) + came.astype(f32)
+
     own_cols = take_seq(weight_qkv.reshape(weight_rows, 3, seq_count, local_width), 2)
-    qkv_cols = lax.all_gather(
-        own_cols.reshape(weight_rows, 3 * local_width), "shard", axis=0, tiled=True
-    )
-    gain_cols = lax.all_gather(norm_gains, "shard", axis=0, tiled=True).astype(f32)
+    own_gains = jnp.pad(norm_gains, ((0, 0), (0, GAIN_LANES - norm_gains.shape[1])))
+    table = pair_tables(expert_ids[0], expert_probs[0], experts)
+    own_block = jnp.concatenate(
+        [own_cols.reshape(weight_rows, 3 * local_width), own_gains], axis=1
+    )
+    qkv_cols, full_out, tables_all = gather_blocks(
+        [own_block, weight_out, table], 1, ((0,), (1, 2))
+    )
+    own_grad, qkv_cols = lax.optimization_barrier((out_cotangent[0], qkv_cols))
+    grad_all = lax.all_gather(own_grad, "shard", axis=0, tiled=False)
+    qkv_cols = qkv_cols.reshape(width, 3 * local_width + GAIN_LANES)
+    gain_cols = qkv_cols[:, 3 * local_width :][:, : norm_gains.shape[1]].astype(f32)
+    qkv_cols = qkv_cols[:, : 3 * local_width]
+    full_out = full_out.reshape(width, width)
     group_in = lax.all_gather(layer_input[0], "seq", axis=0, tiled=True).astype(f32)
-    table = pair_tables(expert_ids[0], expert_probs[0], experts)
-    full_out = lax.all_gather(weight_out, "shard", axis=0, tiled=True)
-    grad_all = lax.all_gather(out_cotangent[0], "shard", axis=0, tiled=False)
-    tables_all = lax.all_gather(table, "shard", axis=0, tiled=False)
     pair_weight = lax.dynamic_index_in_dim(tables_all, shard_at, 1, keepdims=False)
 
     segment, position = group_layout(seq_lengths[0], seq_order[0], group_tok)
@@ -339,7 +465,7 @@
     ffn_n = resid * ffn_r
     ffn_in = (ffn_n * gain_cols[:, 3]).astype(low)
 
-    ffn_all = lax.all_gather(ffn_in, "shard", axis=0, tiled=False)
+    (ffn_all,) = gather_blocks([ffn_in], 2)
     named = pair_weight > 0.0
     rank = jnp.cumsum(named.astype(jnp.int32), axis=1) - 1
     slots = jnp.arange(capacity, dtype=jnp.int32)
@@ -372,19 +498,19 @@
     d_gate = (d_hidden * up * sigma * (1.0 + gate * (1.0 - sigma))).astype(low)
     d_up = (d_hidden * silu).astype(low)
     d_pair = (contract_cols(d_gate, gate_weight) + contract_cols(d_up, up_weight)).astype(low)
-    d_ffn_in = scatter_sum(spread_rows(d_pair).astype(low), 1, f32)
-
     expert_out = jnp.dot(hidden, down_weight, preferred_element_type=f32).astype(low)
     out_part = (spread_rows(expert_out) * pair_weight[:, :, None]).astype(low)
-    mixed_out = scatter_sum(out_part, 2, f32)
-    layer_output = (resid + mixed_out).astype(low)
     part_down = contract_rows(hidden, d_expert).astype(low)
     part_gate = contract_rows(rows_in, d_gate).astype(low)
     part_up = contract_rows(rows_in, d_up).astype(low)
-    sum_gate, sum_up, sum_down = (
-        lax.psum_scatter(part, "seq", scatter_dimension=0, tiled=True).astype(f32)
-        for part in (part_gate, part_up, part_down)
-    )
+    d_spread = spread_rows(d_pair).astype(low)
+    pairs = seq_count == 2
+    d_ffn_in, *came_down = scatter_sum([d_spread], 3, f32, sides=[part_down] if pairs else [])
+    out_part, d_ffn_in = lax.optimization_barrier((out_part, d_ffn_in))
+    mixed_out = lax.psum_scatter(
+        out_part.reshape(experts * tok_rows, width), "shard", scatter_dimension=0, tiled=True
+    ).astype(f32)
+    layer_output = (resid + mixed_out).astype(low)
 
     grad_tokens = out_cotangent[0].astype(f32)
     d_scaled = d_ffn_in * gain_cols[:, 3]
@@ -423,8 +549,7 @@
     d_qkv = jnp.concatenate(
         [dq_raw.astype(low), dk_raw.astype(low), d_value.reshape(group_tok, local_width)], axis=1
     )
-    d_attn_part = contract_cols(d_qkv, qkv_cols).astype(low)
-    d_attn_in = lax.psum_scatter(d_attn_part, "seq", scatter_dimension=0, tiled=True).astype(f32)
+    d_attn_in = seq_sum(contract_cols(d_qkv, qkv_cols).astype(low))
     own_n = lax.dynamic_slice_in_dim(group_n, seq_at * tok_rows, tok_rows)
     own_r = lax.dynamic_slice_in_dim(group_r, seq_at * tok_rows, tok_rows)
     dx_scaled = d_attn_in * gain_cols[:, 0]
@@ -432,18 +557,6 @@
     grad_g_attn = jnp.sum(d_attn_in * own_n, axis=0)
     input_grad = (d_resid + dx_norm).astype(low)
 
-    term_qkv = contract_rows(attn_in, d_qkv).astype(low)
-    term_out = contract_rows(mix_all, branch_cols).astype(low)
-    terms = jnp.concatenate([term_qkv, term_out], axis=1).reshape(experts, weight_rows, -1)
-    sums = scatter_sum(terms, 3, low)
-    sums_all = lax.all_gather(sums, "seq", axis=0, tiled=False).astype(f32)
-    rows_qkv = (
-        sums_all[:, :, : 3 * local_width]
-        .reshape(seq_count, weight_rows, 3, local_width)
-        .transpose(1, 2, 0, 3)
-        .reshape(weight_rows, 3 * width)
-    )
-    rows_out = sums_all[:, :, 3 * local_width :].transpose(1, 0, 2).reshape(weight_rows, width)
     zeros = jnp.zeros((width,), f32)
     gain_terms = jnp.stack(
         [
@@ -451,10 +564,31 @@
             lax.dynamic_update_slice_in_dim(zeros, grad_g_q, seq_at * local_width, 0),
             lax.dynamic_update_slice_in_dim(zeros, grad_g_k, seq_at * local_width, 0),
             grad_g_ffn,
-        ]
-    )
-    gain_terms = lax.psum(gain_terms, ("seq", "shard"))
-    rows_gain = lax.dynamic_slice_in_dim(gain_terms, shard_at * weight_rows, weight_rows, 1).T
+        ],
+        axis=1,
+    )
+    gain_terms = jnp.pad(gain_terms, ((0, 0), (0, GAIN_LANES - gain_terms.shape[1])))
+    terms = [
+        contract_rows(attn_in, d_qkv[:, i * local_width : (i + 1) * local_width]) for i in range(3)
+    ]
+    terms += [contract_rows(mix_all, branch_cols), gain_terms]
+    terms = [term.astype(low).reshape(experts, weight_rows, -1) for term in terms]
+    results = scatter_sum(
+        terms, 4, low, seq_count, sides=[part_gate, part_up] if pairs else []
+    )
+    *sums, sum_gains = results[: len(terms)]
+    came = list(results[len(terms) :]) + came_down
+    if pairs:
+        sum_gate, sum_up, sum_down = (
+            lax.dynamic_slice_in_dim(part, seq_at * other.shape[0], other.shape[0]).astype(f32)
+            + other.astype(f32)
+            for part, other in zip((part_gate, part_up, part_down), came)
+        )
+    else:
+        sum_gate, sum_up, sum_down = (seq_sum(p) for p in (part_gate, part_up, part_down))
+    targets = [(0, 0), (0, width), (0, 2 * width), (1, 0)]
+    rows_qkv, rows_out = place_rows(sums, targets, (3 * width, width))
+    rows_gain = jnp.sum(sum_gains[:, :, : norm_gains.shape[1]].astype(f32), axis=0)
     return (
         layer_output[None],
         input_grad[None],

time: 950 us -> 715 us (0.75)
  waiting for transfers between devices: 300 us -> 6.86 us
  Pallas kernels: 268 us -> 441 us
  blocking collectives: 94.8 us -> 10.1 us
  other arithmetic: 52.3 us -> 35.5 us
  local copies, waits for them, and re-layouts: 28.7 us -> 16.7 us
    all_gather x5 -> x1, waiting for transfers between devices: 265 us -> 0.01 us  [shards(): grad_all = lax.all_gather(own_grad, 'shard', axis=0, tiled=False)]
    pallas_call x3 -> x5, Pallas kernels: 268 us -> 441 us  [the longest x2 226 us: gather_blocks(): pl.pallas_call(functools.partial(gather_kernel, count, groups), out_shape...]
    all_gather x2 -> x0, blocking collectives: 43.8 us -> none  [the longest x1 23.1 us: shards(): lax.all_gather(norm_gains, 'shard', axis=0, tiled=True).astype(f32)]
    psum x1 -> x0, blocking collectives: 41.1 us -> none  [shards(): gain_terms = lax.psum(gain_terms, ('seq', 'shard'))]
    reduce_scatter x4 -> x1, waiting for transfers between devices: 25.6 us -> 0.01 us  [shards(): lax.psum_scatter(out_part.reshape(experts * tok_rows, width), 'shard', sc...]
    concatenate x1, other arithmetic: 12.1 us -> 0.95 us  [shards(): jnp.concatenate([own_cols.reshape(weight_rows, 3 * local_width), own_gain...]
    dot_general x5 -> x7, matrix products: 43.5 us -> 49.4 us  [contract_rows(): lax.dot_general(left_side, right_side, (((0,), (0,)), ((), ())), preferre...]
  transfers between devices with their start and end apart: 14 -> 8, of which waited for: 6 -> 1; matrix products, arithmetic and copies ran while one was open for 16% -> 30% of each run, Pallas kernels for 7% -> 62%
where the time goes in v2:
time: 715 us; the launch traced here: 708 us
  Pallas kernels  441 us (62%)
  matrix products  169 us (24%)
  other arithmetic  35.5 us (5%)
  local copies, waits for them, and re-layouts  16.7 us (2%)
  between operations  15.2 us (2%)
  starting transfers between devices  13.4 us (2%)
  blocking collectives  10.1 us (1%)
    pallas_call x2, Pallas kernels, gather_blocks(): pl.pallas_call(functools.partial(gather_kernel, count, groups), out_shape...  226 us
    pallas_call x2, Pallas kernels, scatter_sum(): pl.pallas_call(functools.partial(scatter_kernel, count, seq_count, arrays...  211 us
    dot_general x5, matrix products, contract_cols(): lax.dot_general(left_side, right_side, (((1,), (1,)), ((), ())), preferre...  50.1 us
    dot_general x7, matrix products, contract_rows(): lax.dot_general(left_side, right_side, (((0,), (0,)), ((), ())), preferre...  49.4 us
  transfers between devices with their start and end apart: 8, of which 1 were waited for; matrix products, arithmetic and copies ran while one was open for 30% of the time, Pallas kernels for 62%

profile of v2, /device:TPU:0, one launch (start us, length us, event | category | flops | bytes accessed | tf_op | source)
XLA Modules:
  0.0 707.7 jit_solution(4827550698158363548)
XLA Ops:
  8.0 1.9 copy.129
  11.1 0.9 fusion.39.refs_0_
  12.0 146.3 %gather_blocks_1.1 = (bf16[16,128,3200]{2,1,0:T(8,128)(2,1)}, bf16[16,128,2048]{2,1,0:T(8,128)(2,1)}, f32[16,16,128]{2,1,0:T(8,128)}) custom-call(bf16[128,3200]{1,0:T(8,128)(2,1)} %fusion.39.refs_0_, bf16[128,2048]{1,0:T(8,128)(2,1)} %refs_1_.1, f32[16,128]{1,0:T(8,128)} %select_reduce_fusion.1.refs_2_), custom_call_target="tpu_custom_call" | custom-call | tf_op jit(solution)/shard_map/gather_blocks_1/pallas_call | solution.py:186
  158.3 1.1 slice.85
  160.0 0.9 broadcast_compare_fusion
  162.0 1.2 fusion.66
  163.2 1.6 fusion.19
  164.8 6.8 fusion.3
  171.9 4.9 psum.14
  178.2 1.8 subtract_convert_fusion.1
  180.0 2.8 fusion.80
  182.8 1.3 copy-done.17
  184.1 2.5 convolution_convert_fusion.12
  186.6 1.2 all_to_all.40
  187.8 0.9 copy.139
  188.7 3.5 all-to-all-start
  192.4 1.5 convert_multiply_fusion
  194.7 5.6 all-to-all-done
  200.3 4.7 multiply_reduce_fusion.7
  205.0 1.0 multiply_convert_fusion.9.refs_0_
  206.0 80.1 %gather_blocks_2.1 = bf16[16,128,2048]{2,1,0:T(8,128)(2,1)} custom-call(bf16[128,2048]{1,0:T(8,128)(2,1)} %multiply_convert_fusion.9.refs_0_), custom_call_target="tpu_custom_call" | custom-call | tf_op jit(solution)/shard_map/gather_blocks_2/pallas_call | solution.py:186
  286.1 5.3 convolution_convert_fusion.2
  291.5 8.5 %fusion.10 = f32[1536,1024]{1,0:T(8,128)} fusion(bf16[1536,2048]{1,0:T(8,128)(2,1)S(1)} %bitcast.206, bf16[1,2048,1024]{2,1,0:T(8,128)(2,1)S(1)} %copy-done.58), kind=kOutput, calls=%fused_computation.20 | convolution fusion | flops 6442450944 | bytes 16777216 | tf_op jit(solution)/shard_map/dot_general | solution.py:492
  300.0 8.4 %fusion.14 = f32[1536,1024]{1,0:T(8,128)} fusion(bf16[1536,2048]{1,0:T(8,128)(2,1)S(1)} %bitcast.207, bf16[1,2048,1024]{2,1,0:T(8,128)(2,1)S(1)} %copy-done.56), kind=kOutput, calls=%fused_computation.24 | convolution fusion | flops 6442450944 | bytes 16777216 | tf_op jit(solution)/shard_map/dot_general | solution.py:491
  308.4 5.2 multiply_convert_fusion.1
  313.6 15.4 %multiply_convert_fusion.2 = (bf16[1536,1024]{1,0:T(8,128)(2,1)}, bf16[1536,1024]{1,0:T(8,128)(2,1)}, bf16[1536,1024]{1,0:T(8,128)(2,1)}) fusion(f32[1536,1024]{1,0:T(8,128)} %fusion.14, f32[1536,1024]{1,0:T(8,128)} %fusion.10, bf16[1536,2048]{1,0:T(8,128)(2,1)S(1)} %bitcast.210, bf16[1,1024,2048]{2,1,0:T(8,128)(2,1)} %param.22), kind=kOutput, calls=%fused_computation.9 | convolution fusion | flops 6466043904 | bytes 32505856 | tf_op jit(solution)/shard_map/dot_general | solution.py:65
  329.0 11.0 %convolution_convert_fusion.5.refs_1_ = bf16[1024,2048]{1,0:T(8,128)(2,1)} fusion(bf16[1536,1024]{1,0:T(8,128)(2,1)} %get-tuple-element.78, bf16[1536,2048]{1,0:T(8,128)(2,1)S(1)} %bitcast.211), kind=kOutput, calls=%fused_computation.31 | convolution fusion | flops 6444548096 | bytes 13631488 | tf_op jit(solution)/shard_map/dot_general | solution.py:59
  340.0 8.7 %convolution_convert_fusion = bf16[1536,2048]{1,0:T(8,128)(2,1)} fusion(bf16[1536,1024]{1,0:T(8,128)(2,1)S(1)} %copy-done.62, bf16[1,1024,2048]{2,1,0:T(8,128)(2,1)S(1)} %copy-done.55), kind=kOutput, calls=%fused_computation.8 | convolution fusion | flops 6445596672 | bytes 13631488 | tf_op jit(solution)/shard_map/dot_general | solution.py:501
  348.8 9.1 %fusion.12 = f32[1536,2048]{1,0:T(8,128)} fusion(bf16[1536,1024]{1,0:T(8,128)(2,1)S(1)} %copy-done.63, bf16[1,2048,1024]{2,1,0:T(8,128)(2,1)S(1)} %copy-done.57), kind=kOutput, calls=%fused_computation.22 | convolution fusion | flops 6442450944 | bytes 19922944 | tf_op jit(solution)/shard_map/dot_general | solution.py:65
  357.9 10.9 %add_convert_fusion = bf16[1536,2048]{1,0:T(8,128)(2,1)S(1)} fusion(f32[1536,2048]{1,0:T(8,128)} %fusion.12, bf16[1536,1024]{1,0:T(8,128)(2,1)} %get-tuple-element.76, bf16[1,2048,1024]{2,1,0:T(8,128)(2,1)S(1)} %copy-done.59), kind=kOutput, calls=%fused_computation.2 | convolution fusion | flops 6448742400 | bytes 26214400 | tf_op jit(solution)/shard_map/dot_general | solution.py:65
  368.8 5.6 convolution_convert_fusion.1.refs_0_
  374.4 4.6 multiply_convert_fusion
  379.1 80.0 %scatter_sum_3.1 = (f32[128,2048]{1,0:T(8,128)}, bf16[512,2048]{1,0:T(8,128)(2,1)}) custom-call(bf16[16,128,2048]{2,1,0:T(8,128)(2,1)} %convolution_convert_fusion.1.refs_0_, bf16[1024,2048]{1,0:T(8,128)(2,1)} %convolution_convert_fusion.5.refs_1_), custom_call_target="tpu_custom_call" | custom-call | tf_op jit(solution)/shard_map/scatter_sum_3/pallas_call | solution.py:305
  459.1 1.6 multiply_reduce_fusion.1
  460.7 1.6 fusion.74
  462.2 6.3 convolution_convert_fusion.10
  468.5 0.8 copy.210
  469.3 3.5 all-to-all-start.1
  473.4 11.5 %convolution_convert_fusion.3.refs_6_ = bf16[2048,1024]{1,0:T(8,128)(2,1)} fusion(bf16[1536,2048]{1,0:T(8,128)(2,1)} %bitcast.208, bf16[1536,1024]{1,0:T(8,128)(2,1)} %get-tuple-element.76), kind=kOutput, calls=%fused_computation.29 | convolution fusion | flops 6444548096 | bytes 13631488 | tf_op jit(solution)/shard_map/dot_general | solution.py:59
  484.9 12.0 %convolution_convert_fusion.4.refs_5_ = bf16[2048,1024]{1,0:T(8,128)(2,1)} fusion(bf16[1536,2048]{1,0:T(8,128)(2,1)} %bitcast.209, bf16[1536,1024]{1,0:T(8,128)(2,1)S(1)} %copy-done.64), kind=kOutput, calls=%fused_computation.30 | convolution fusion | flops 6444548096 | bytes 13631488 | tf_op jit(solution)/shard_map/dot_general | solution.py:59
  496.9 2.8 add_bitcast_fusion
  499.8 0.8 copy.209
  500.6 4.2 all-to-all-start.2
  505.3 2.1 convolution_convert_fusion.11
  507.4 1.0 copy.165
  508.4 3.1 multiply_reduce_fusion
  514.0 1.0 multiply_subtract_fusion.1
  515.9 1.0 fusion.34
  516.9 5.2 psum.15
  522.1 3.2 multiply_convert_fusion.8
  525.4 8.5 %fusion.16 = bf16[256,2048]{1,0:T(8,128)(2,1)S(1)} fusion(bf16[2048,3200]{1,0:T(8,128)(2,1)} %bitcast.254, bf16[256,1024]{1,0:T(8,128)(2,1)S(1)} %copy-done.36, bf16[256,1024]{1,0:T(8,128)(2,1)S(1)} %get-tuple-element.80, bf16[256,1024]{1,0:T(8,128)(2,1)S(1)} %get-tuple-element.79), kind=kOutput, calls=%fused_computation.38 | convolution fusion | flops 3226468352 | bytes 15204352 | tf_op jit(solution)/shard_map/dot_general | solution.py:65
  533.9 0.9 dynamic-slice_bitcast_fusion
  534.8 1.9 collective-permute-start
  536.7 4.8 convolution_convert_fusion.6
  541.5 3.4 convolution_convert_fusion.7
  544.9 3.4 convolution_convert_fusion.8
  548.4 3.4 convolution_convert_fusion.9
  552.6 0.9 pad.10.clone
  553.5 130.6 %scatter_sum_4.1 = (bf16[2,128,1024]{2,1,0:T(8,128)(2,1)}, bf16[2,128,1024]{2,1,0:T(8,128)(2,1)}, bf16[2,128,1024]{2,1,0:T(8,128)(2,1)}, bf16[2,128,1024]{2,1,0:...) custom-call(bf16[16,128,1024]{2,1,0:T(8,128)(2,1)} %bitcast.205, ...), custom_call_target="tpu_custom_call" | custom-call | tf_op jit(solution)/shard_map/scatter_sum_4/pallas_call | solution.py:305
  684.1 0.9 convert_reduce_fusion
  685.6 3.7 place_rows.1
  689.4 5.3 add_bitcast_fusion.1
  694.7 2.9 add_bitcast_fusion.2
  697.7 3.0 fusion.46
  (199 shorter events, 11.9 us)
Async XLA Ops:
  7.2 3.1 copy-start.53
  7.2 3.3 copy-start.52
  7.2 3.2 copy-start.51
  7.2 156.0 %all-gather.8.cloned.1.call-start = ((), (), s32[]{:S(2)}) async-start(), calls=%async_computation.6 | async-start | bytes 1572864 | tf_op jit(solution)/shard_map/all_gather | solution.py:415
  7.9 300.5 %all-gather.10.cloned.1.call-start = ((), (), s32[]{:S(2)}) async-start(), calls=%async_computation.7 | async-start | bytes 8912896 | tf_op jit(solution)/shard_map/all_gather | solution.py:410
  9.9 149.7 %copy-start.60 = (s32[1,3]{1,0:T(1,128)S(1)}, s32[1,3]{1,0:T(1,128)}, u32[]{:S(2)}) copy-start(s32[1,3]{1,0:T(1,128)} %param.13) | copy-start | bytes 40
  9.9 149.7 %copy-start.61 = (s32[1,3]{1,0:T(1,128)S(1)}, s32[1,3]{1,0:T(1,128)}, u32[]{:S(2)}) copy-start(s32[1,3]{1,0:T(1,128)} %param.14) | copy-start | bytes 40
  161.2 10.4 %copy-start.33 = (f32[2048,1]{0,1:T(1,128)}, f32[2048,1]{0,1:T(1,128)S(1)}, u32[]{:S(2)}) copy-start(f32[2048,1]{0,1:T(1,128)S(1)} %get-tuple-element.104) | copy-start | bytes 24580
  161.2 15.6 %copy-start.39 = (f32[1024,1]{0,1:T(1,128)}, f32[1024,1]{0,1:T(1,128)S(1)}, u32[]{:S(2)}) copy-start(f32[1024,1]{0,1:T(1,128)S(1)} %get-tuple-element.118) | copy-start | bytes 12292
  161.2 15.6 %copy-start.41 = (f32[1024,1]{0,1:T(1,128)}, f32[1024,1]{0,1:T(1,128)S(1)}, u32[]{:S(2)}) copy-start(f32[1024,1]{0,1:T(1,128)S(1)} %get-tuple-element.119) | copy-start | bytes 12292
  163.1 15.1 %copy-start.31 = (f32[256,64]{1,0:T(8,128)}, f32[256,64]{1,0:T(8,128)S(1)}, u32[]{:S(2)}) copy-start(f32[256,64]{1,0:T(8,128)S(1)} %get-tuple-element.111) | copy-start | bytes 196612
  164.8 29.2 %copy-start.43 = (f32[256]{0:T(256)}, f32[256]{0:T(256)S(1)}, u32[]{:S(2)}) copy-start(f32[256]{0:T(256)S(1)} %add_rsqrt_fusion) | copy-start | bytes 3076
  171.6 5.7 copy-start.2
  180.0 2.8 copy-start.19
  180.0 2.8 copy-start.21
  182.8 5.0 copy-start.49
  184.1 8.3 %copy-start = (bf16[1,256,2048]{2,1,0:T(8,128)(2,1)S(1)}, bf16[1,256,2048]{2,1,0:T(8,128)(2,1)}, u32[]{:S(2)}) copy-start(bf16[1,256,2048]{2,1,0:T(8,128)(2,1)} %all-gather.8.cloned.1.call-done) | copy-start | bytes 3145732
  186.6 13.7 %copy-start.14 = (bf16[1,128,2048]{2,1,0:T(8,128)(2,1)S(1)}, bf16[1,128,2048]{2,1,0:T(8,128)(2,1)}, u32[]{:S(2)}) copy-start(bf16[1,128,2048]{2,1,0:T(8,128)(2,1)} %param.12) | copy-start | bytes 1572868
  188.7 11.6 %all-to-all-start = ((bf16[2,128,1024]{1,2,0:T(8,128)(2,1)}), bf16[2,128,1024]{1,2,0:T(8,128)(2,1)S(1)}, u32[]{:S(2)}, u32[]{:S(2)}) async-start(bf16[2,128,1024]{1,2,0:T(8,128)(2,1)} %copy.139), calls=%async_computation | async-start | bytes 1048576 | tf_op jit(solution)/shard_map/all_to_all | solution.py:461
  192.2 344.5 %all-gather.6.cloned.1.call-start = ((), (), s32[]{:S(2)}) async-start(), calls=%async_computation.5 | async-start | bytes 1572864 | tf_op jit(solution)/shard_map/all_gather | solution.py:462
  286.1 5.3 copy-start.58
  291.4 8.6 %copy-start.4 = (bf16[16,96,2048]{2,1,0:T(8,128)(2,1)}, bf16[16,96,2048]{2,1,0:T(8,128)(2,1)S(1)}, u32[]{:S(2)}) copy-start(bf16[16,96,2048]{2,1,0:T(8,128)(2,1)S(1)} %convolution_convert_fusion.2) | copy-start | bytes 18874372
  291.5 8.5 %copy-start.56 = (bf16[1,2048,1024]{2,1,0:T(8,128)(2,1)S(1)}, bf16[1,2048,1024]{2,1,0:T(8,128)(2,1)}, u32[]{:S(2)}) copy-start(bf16[1,2048,1024]{2,1,0:T(8,128)(2,1)} %param.20) | copy-start | bytes 12582916
  329.0 11.0 %copy-start.55 = (bf16[1,1024,2048]{2,1,0:T(8,128)(2,1)S(1)}, bf16[1,1024,2048]{2,1,0:T(8,128)(2,1)}, u32[]{:S(2)}) copy-start(bf16[1,1024,2048]{2,1,0:T(8,128)(2,1)} %param.22) | copy-start | bytes 12582916
  329.0 11.0 %copy-start.62 = (bf16[1536,1024]{1,0:T(8,128)(2,1)S(1)}, bf16[1536,1024]{1,0:T(8,128)(2,1)}, u32[]{:S(2)}) copy-start(bf16[1536,1024]{1,0:T(8,128)(2,1)} %get-tuple-element.78) | copy-start | bytes 9437188
  340.0 8.8 %copy-start.57 = (bf16[1,2048,1024]{2,1,0:T(8,128)(2,1)S(1)}, bf16[1,2048,1024]{2,1,0:T(8,128)(2,1)}, u32[]{:S(2)}) copy-start(bf16[1,2048,1024]{2,1,0:T(8,128)(2,1)} %param.20) | copy-start | bytes 12582916
  340.0 8.8 %copy-start.63 = (bf16[1536,1024]{1,0:T(8,128)(2,1)S(1)}, bf16[1536,1024]{1,0:T(8,128)(2,1)}, u32[]{:S(2)}) copy-start(bf16[1536,1024]{1,0:T(8,128)(2,1)} %get-tuple-element.77) | copy-start | bytes 9437188
  348.8 9.1 %copy-start.59 = (bf16[1,2048,1024]{2,1,0:T(8,128)(2,1)S(1)}, bf16[1,2048,1024]{2,1,0:T(8,128)(2,1)}, u32[]{:S(2)}) copy-start(bf16[1,2048,1024]{2,1,0:T(8,128)(2,1)} %param.21) | copy-start | bytes 12582916
  368.8 5.6 slice-start
  368.8 5.6 slice-start.1
  368.8 5.6 copy-start.38
  379.1 81.6 %copy-start.11 = (bf16[1,128,2048]{2,1,0:T(8,128)(2,1)S(1)}, bf16[1,128,2048]{2,1,0:T(8,128)(2,1)}, u32[]{:S(2)}) copy-start(bf16[1,128,2048]{2,1,0:T(8,128)(2,1)} %param.23) | copy-start | bytes 1572868
  469.3 31.3 %all-to-all-start.1 = ((bf16[128,2,1024]{2,0,1:T(8,128)(2,1)}), bf16[128,2,1024]{2,0,1:T(8,128)(2,1)S(1)}, u32[]{:S(2)}, u32[]{:S(2)}) async-start(bf16[128,2,1024]{2,0,1:T(8,128)(2,1)} %bitcast.197), calls=%async_computation.2 | async-start | bytes 1048576 | tf_op jit(solution)/shard_map/all_to_all | solution.py:523
  472.8 224.8 %reduce-scatter.2.cloned.1.call-start = ((), (), s32[]{:S(2)}) async-start(), calls=%async_computation.4 | async-start | bytes 8912896 | tf_op jit(solution)/shard_map/reduce_scatter | solution.py:510
  473.4 11.5 %copy-start.64 = (bf16[1536,1024]{1,0:T(8,128)(2,1)S(1)}, bf16[1536,1024]{1,0:T(8,128)(2,1)}, u32[]{:S(2)}) copy-start(bf16[1536,1024]{1,0:T(8,128)(2,1)} %get-tuple-element.77) | copy-start | bytes 9437188
  484.9 12.0 %copy-start.6 = (bf16[1024,2048]{1,0:T(8,128)(2,1)S(1)}, bf16[1024,2048]{1,0:T(8,128)(2,1)}, u32[]{:S(2)}) copy-start(bf16[1024,2048]{1,0:T(8,128)(2,1)} %convolution_convert_fusion.5.refs_1_) | copy-start | bytes 12582916
  484.9 12.0 %copy-start.25 = (bf16[512,2048]{1,0:T(8,128)(2,1)S(1)}, bf16[512,2048]{1,0:T(8,128)(2,1)}, u32[]{:S(2)}) copy-start(bf16[512,2048]{1,0:T(8,128)(2,1)} %get-tuple-element.43) | copy-start | bytes 6291460
  499.8 5.5 copy-start.50
  500.6 36.1 %all-to-all-start.2 = ((bf16[128,2,1024]{2,0,1:T(8,128)(2,1)}), bf16[128,2,1024]{2,0,1:T(8,128)(2,1)}, u32[]{:S(2)}, u32[]{:S(2)}) async-start(bf16[128,2,1024]{2,0,1:T(8,128)(2,1)} %bitcast.196), calls=%async_computation.3 | async-start | bytes 1048576 | tf_op jit(solution)/shard_map/all_to_all | solution.py:526
  507.4 4.1 copy-start.15
  508.4 3.2 copy-start.18
  514.0 1.9 copy-start.3
  514.0 1.9 copy-start.40
  514.0 1.9 copy-start.42
  514.0 1.9 copy-start.46
  514.0 1.9 copy-start.48
  515.1 1.8 copy-start.8
  522.1 3.3 copy-start.36
  525.3 8.5 %copy-start.27 = (bf16[256,1024]{1,0:T(8,128)(2,1)}, bf16[256,1024]{1,0:T(8,128)(2,1)S(1)}, u32[]{:S(2)}) copy-start(bf16[256,1024]{1,0:T(8,128)(2,1)S(1)} %get-tuple-element.79) | copy-start | bytes 1572868
  525.4 8.5 %copy-start.29 = (bf16[256,1024]{1,0:T(8,128)(2,1)}, bf16[256,1024]{1,0:T(8,128)(2,1)S(1)}, u32[]{:S(2)}) copy-start(bf16[256,1024]{1,0:T(8,128)(2,1)S(1)} %get-tuple-element.80) | copy-start | bytes 1572868
  533.9 17.9 %copy-start.13 = (bf16[256,2048]{1,0:T(8,128)(2,1)}, bf16[256,2048]{1,0:T(8,128)(2,1)S(1)}, u32[]{:S(2)}) copy-start(bf16[256,2048]{1,0:T(8,128)(2,1)S(1)} %fusion.16) | copy-start | bytes 3145732
  534.8 17.0 %collective-permute-start = (bf16[128,2048]{1,0:T(8,128)(2,1)}, bf16[128,2048]{1,0:T(8,128)(2,1)S(1)}, u32[]{:S(2)}, u32[]{:S(2)}) collective-permute-start(bf16[128,2048]{1,0:T(8,128)(2,1)} %dynamic-slice_bitcast_fusion), channel_id=1, source_target_pairs={{0,16},{16,0},{1,17},{17,1},{2,18},{18,2},{3,19},{19,3},{4,20},{20... | collective-permute-start | bytes 1572872 | tf_op jit(solution)/shard_map/ppermute | solution.py:397
  536.7 4.8 copy-start.1
  536.7 4.8 copy-start.16
  536.7 4.8 copy-start.34
  536.7 4.8 copy-start.44
  541.5 3.4 copy-start.30
  544.9 3.5 copy-start.28
  548.4 3.4 copy-start.10
  689.4 5.3 copy-start.5
  689.4 5.3 copy-start.26
  694.7 3.0 copy-start.7
  694.7 3.0 copy-start.12
  694.7 3.0 copy-start.54
  (11 other events, 13.6 us)
Sparse Core Ops, SparseCore 0:
  9.5 23.9 all-gather.7
  158.4 89.0 all-gather.9
  249.0 22.7 all-gather.5
  477.4 110.5 reduce-scatter.1

commit v3 on v2

--- a/solution.py
+++ b/solution.py
@@ -70,6 +70,8 @@
 MESH_ID = pl.DeviceIdType.MESH
 VMEM_LIMIT = 60 * 1024 * 1024
 ROW_TILE = 16
+AHEAD = 2
+GRAD_TILE = 256
 
 
 def low_bit(index):
@@ -198,14 +200,16 @@
     )(*blocks)
 
 
-def scatter_kernel(count, seq_count, arrays, sides, *refs):
+def scatter_kernel(count, seq_count, arrays, sides, work, *refs):
     parts, refs = refs[:arrays], refs[arrays:]
     side_from, refs = refs[:sides], refs[sides:]
+    work_in, refs = refs[: work.inputs], refs[work.inputs :]
     totals, refs = refs[:arrays], refs[arrays:]
     side_to, refs = refs[:sides], refs[sides:]
-    held = refs[:arrays]
-    send, recv, seq_send, seq_recv, side_send, side_recv = refs[arrays:]
-    planes = seq_count if seq_count > 1 else 1 + (sides > 0)
+    work_out, refs = refs[: work.outputs], refs[work.outputs :]
+    held, refs = refs[:arrays], refs[arrays:]
+    send, recv, seq_send, seq_recv, side_send, side_recv = refs[:6]
+    planes = seq_count if seq_count > 1 else 1 + (sides > 0 or work.outputs > 0)
     me = lax.axis_index("shard")
     seq = lax.axis_index("seq")
     place = relative_place(count, me)
@@ -214,9 +218,8 @@
     copies = {}
     shared = []
     for i in range(sides):
-        half = side_to[i].shape[0]
         copy = remote(
-            side_from[i].at[pl.ds(pl.multiple_of((1 - seq) * half, half), half)],
+            side_from[i],
             side_to[i],
             side_send.at[i],
             side_recv.at[i],
@@ -272,44 +275,139 @@
         elif r & upper:
             start(a, r, held[a].at[came])
 
-    def reversed_bits(u):
-        return sum(1 << (len(bits) - 3 - b) for b in range(len(bits) - 2) if u >> b & 1)
-
-    order = sorted(range(count // 4), key=reversed_bits, reverse=True)
-    chunks = [(a, u) for a in range(arrays) for u in order]
+    chunks = [(a, u) for a in range(arrays) for u in reversed(range(count // 4))]
     for a, u in chunks:
         for r in (4 * u + 3, 4 * u + 1):
             start(a, r, parts[a].at[place(r)])
-    for i in range(len(chunks) + len(bits) - 1):
-        for stage in range(len(bits)):
-            bit = bits[stage]
-            at = i - max(stage, 0)
-            if 0 <= at < len(chunks):
-                a, u = chunks[at]
-                if stage == 0:
-                    fold(a, 4 * u + 2, bit)
+    tasks = work.tasks(seq, me, work_in, work_out, refs[6:])
+    steps = len(chunks) + AHEAD
+    for i in range(steps):
+        if i < len(chunks):
+            a, u = chunks[i]
+            fold(a, 4 * u + 2, 1)
+            fold(a, 4 * u, 1)
+        if i >= AHEAD:
+            a, u = chunks[i - AHEAD]
+            for bit in bits[1:]:
+                if 4 * u % (2 * bit) == 0:
                     fold(a, 4 * u, bit)
-                elif stage == 1 or 4 * u % (2 * bit) == 0:
-                    fold(a, 4 * u, bit)
+        for task in tasks[len(tasks) * i // steps : len(tasks) * (i + 1) // steps]:
+            task()
     for copy in shared:
         copy.wait_recv()
     for copy in list(copies.values()) + shared:
         copy.wait_send()
-
-
-def scatter_sum(parts, collective_id, out_dtype, seq_count=1, sides=()):
+    work.finish()
+
+
+class NoWork:
+    inputs = outputs = 0
+    operands, results, scratch = (), (), ()
+
+    def tasks(self, seq, me, arrays, results, scratch):
+        return []
+
+    def finish(self):
+        pass
+
+
+class ExpertGrads:
+    def __init__(self, products):
+        self.operands = []
+        for pair in products:
+            for array in pair:
+                if not any(array is other for other in self.operands):
+                    self.operands.append(array)
+        self.pairs = [
+            tuple(next(i for i, o in enumerate(self.operands) if o is array) for array in pair)
+            for pair in products
+        ]
+        low = products[0][0].dtype
+        shapes = [(left.shape[1] // 2, right.shape[1]) for left, right in products]
+        halves = [jax.ShapeDtypeStruct(shape, low) for shape in shapes for _ in range(2)]
+        self.results = halves
+        self.inputs, self.outputs = len(self.operands), len(self.results)
+        self.scratch = [pltpu.VMEM(a.shape, a.dtype) for a in self.operands]
+        self.scratch += [pltpu.VMEM(h.shape, h.dtype) for h in halves]
+        self.scratch += [
+            pltpu.SemaphoreType.DMA((self.inputs,)),
+            pltpu.SemaphoreType.DMA((self.outputs,)),
+            pltpu.SemaphoreType.DMA((2,)),
+        ]
+
+    def tasks(self, seq, me, arrays, results, scratch):
+        here, scratch = scratch[: self.inputs], scratch[self.inputs :]
+        tiles, (in_sem, out_sem, side_sem) = scratch[: self.outputs], scratch[self.outputs :]
+        loads = [
+            pltpu.make_async_copy(arrays[i], here[i], in_sem.at[i]) for i in range(self.inputs)
+        ]
+        for load in loads:
+            load.start()
+        waited = set()
+        self.open = []
+        self.remote = None
+
+        def multiply(p, k, first, last):
+            left, right = self.pairs[p]
+            out = tiles[2 * p + k]
+            for i in (left, right):
+                if i not in waited:
+                    loads[i].wait()
+                    waited.add(i)
+            base = ((1 - seq) if k == 0 else seq) * out.shape[0]
+
+            def step(i, carry):
+                from_at = pl.ds(pl.multiple_of(base + i * GRAD_TILE, GRAD_TILE), GRAD_TILE)
+                to_at = pl.ds(pl.multiple_of(i * GRAD_TILE, GRAD_TILE), GRAD_TILE)
+                out[to_at, :] = contract_rows(here[left][:, from_at], here[right][...]).astype(
+                    out.dtype
+                )
+                return carry
+
+            lax.fori_loop(first, last, step, 0)
+            if last * GRAD_TILE == out.shape[0]:
+                if p == 0 and k == 0:
+                    copy = remote(
+                        out, results[0], side_sem.at[0], side_sem.at[1], (1 - seq, me)
+                    )
+                    self.remote = copy
+                else:
+                    copy = pltpu.make_async_copy(
+                        out, results[2 * p + k], out_sem.at[2 * p + k]
+                    )
+                    self.open.append(copy)
+                copy.start()
+
+        found = []
+        for p in range(len(self.pairs)):
+            for k in range(2):
+                count = tiles[2 * p + k].shape[0] // GRAD_TILE
+                step = max(count // 2, 1)
+                for first in range(0, count, step):
+                    found.append(functools.partial(multiply, p, k, first, first + step))
+        return found
+
+    def finish(self):
+        for copy in self.open:
+            copy.wait()
+        self.remote.wait()
+
+
+def scatter_sum(parts, collective_id, out_dtype, seq_count=1, sides=(), work=None):
+    work = work or NoWork()
     count = lax.axis_size("shard")
     arrays = len(parts)
     lead = (seq_count,) if seq_count > 1 else ()
     others = max(seq_count - 1, 1)
     return pl.pallas_call(
-        functools.partial(scatter_kernel, count, seq_count, arrays, len(sides)),
+        functools.partial(scatter_kernel, count, seq_count, arrays, len(sides), work),
         out_shape=[jax.ShapeDtypeStruct(lead + p.shape[1:], out_dtype) for p in parts]
-        + [jax.ShapeDtypeStruct((s.shape[0] // 2, s.shape[1]), s.dtype) for s in sides],
+        + [jax.ShapeDtypeStruct(s.shape, s.dtype) for s in sides]
+        + list(work.results),
         in_specs=[pl.BlockSpec(memory_space=pltpu.VMEM)] * arrays
-        + [pl.BlockSpec(memory_space=pl.ANY)] * len(sides),
+        + [pl.BlockSpec(memory_space=pl.ANY)] * (len(sides) + work.inputs),
         out_specs=[pl.BlockSpec(memory_space=pltpu.VMEM)] * arrays
-        + [pl.BlockSpec(memory_space=pl.ANY)] * len(sides),
+        + [pl.BlockSpec(memory_space=pl.ANY)] * (len(sides) + work.outputs),
         scratch_shapes=[pltpu.VMEM(p.shape, p.dtype) for p in parts]
         + [
             pltpu.SemaphoreType.DMA((arrays, count)),
@@ -318,12 +416,13 @@
             pltpu.SemaphoreType.DMA((arrays, others)),
             pltpu.SemaphoreType.DMA((max(len(sides), 1),)),
             pltpu.SemaphoreType.DMA((max(len(sides), 1),)),
-        ],
+        ]
+        + list(work.scratch),
         compiler_params=pltpu.CompilerParams(
             collective_id=collective_id, has_side_effects=True, vmem_limit_bytes=VMEM_LIMIT
         ),
         name="scatter_sum_%d" % collective_id,
-    )(*parts, *sides)
+    )(*parts, *sides, *work.operands)
 
 
 def place_kernel(refs_in, seq_count, *refs):
@@ -343,6 +442,228 @@
         out_specs=[pl.BlockSpec(memory_space=pltpu.VMEM)] * len(out_cols),
         name="place_rows",
     )(*pieces)
+
+
+class Tree:
+    def __init__(self, count, own, full, send, recv, seq, place):
+        self.count, self.own, self.full = count, own, full
+        self.copies = {}
+        for r in range(count):
+            below = low_bit(r) if r else count
+            for bit in bit_list(count):
+                if bit < below:
+                    self.copies[r | bit] = remote(
+                        own if r == 0 else full.at[place(r)],
+                        full.at[place(r)],
+                        send.at[r | bit],
+                        recv.at[r | bit],
+                        (seq, place(bit)),
+                    )
+
+    def start(self, r):
+        below = low_bit(r) if r else self.count
+        bits = [bit for bit in bit_list(self.count) if bit < below]
+        for bit in sorted(bits, key=lambda bit: (bit < 4, bit)):
+            self.copies[r | bit].start()
+
+    def arrive(self, r):
+        self.copies[r].wait_recv()
+        self.start(r)
+
+    def steps(self):
+        order, done, found = arrival_order(self.count), 0, []
+        for i in range(self.count // 2):
+            upto = order.index(2 * i) + 1 if i else 0
+            found.append(order[done:upto])
+            done = max(done, upto)
+        return found
+
+    def finish(self):
+        for copy in self.copies.values():
+            copy.wait_send()
+
+
+def expert_kernel(count, *refs):
+    (ffn_own, grad_own, weight), refs = refs[:3], refs[3:]
+    matrices, refs = refs[:3], refs[3:]
+    (rows_out, hidden_out, mixed_out, expert_out, gate_out, up_out), refs = refs[:6], refs[6:]
+    pair_out, refs = refs[:2], refs[2:]
+    (ffn_all, grad_all, gate_w, up_w, down_w, gate_all, up_all), refs = refs[:7], refs[7:]
+    (hidden_at, mixed_at, expert_at, gate_at, up_at, left_at, right_at), refs = refs[:7], refs[7:]
+    ffn_send, ffn_recv, grad_send, grad_recv, load, own_sem, rows_sem, out_sem = refs
+    me = lax.axis_index("shard")
+    seq = lax.axis_index("seq")
+    place = relative_place(count, me)
+    tiles = count // 2
+    low, f32 = ffn_own.dtype, jnp.float32
+    meet(count, place, seq)
+    ffn = Tree(count, ffn_own, ffn_all, ffn_send, ffn_recv, seq, place)
+    grad = Tree(count, grad_own, grad_all, grad_send, grad_recv, seq, place)
+    ffn.start(0)
+    loads = [
+        pltpu.make_async_copy(source, target, load.at[i])
+        for i, (source, target) in enumerate(zip(matrices, (gate_w, up_w, down_w)))
+    ]
+    for copy in loads:
+        copy.start()
+    ffn_keep = pltpu.make_async_copy(ffn_own, ffn_all.at[me], own_sem.at[0])
+    grad_keep = pltpu.make_async_copy(grad_own, grad_all.at[me], own_sem.at[1])
+    ffn_keep.start()
+    grad_keep.start()
+    ffn_keep.wait()
+    for copy in loads:
+        copy.wait()
+
+    pair = me // 2
+
+    def tile_of(i):
+        total = 0
+        for bit in bit_list(tiles):
+            mine, other = lax.rem(pair // bit, 2), lax.rem(i // bit, 2)
+            total = total + bit * (mine + other - 2 * mine * other)
+        return total
+
+    def put(number, slot, staged, target, tile):
+        return pltpu.make_async_copy(staged.at[slot], target.at[tile], out_sem.at[number, slot])
+
+    def keep_rows(tile):
+        return pltpu.make_async_copy(
+            ffn_all.at[pl.ds(2 * tile, 2)], rows_out.at[pl.ds(2 * tile, 2)], rows_sem.at[tile]
+        )
+
+    def arrivals(tree, i, extra):
+        for at, order in enumerate(tree.steps()):
+
+            @pl.when(i == at)
+            def _(at=at, order=order):
+                for r in order:
+                    tree.arrive(r)
+                if at in extra:
+                    extra[at]()
+                tree.copies[2 * at + 1].wait_recv()
+
+    columns = gate_w.shape[1] // 2
+
+    def forward(i, carry):
+        arrivals(ffn, i, {tiles - 3: lambda: grad.start(0)})
+        tile = tile_of(i)
+        slot = lax.rem(i, 2)
+        keep_rows(tile).start()
+
+        @pl.when(i >= 2)
+        def _():
+            put(0, slot, hidden_at, hidden_out, tile_of(i - 2)).wait()
+            put(1, slot, mixed_at, mixed_out, tile_of(i - 2)).wait()
+
+        rows = ffn_all[pl.ds(2 * tile, 2)].reshape(-1, ffn_all.shape[2])
+        for c in range(2):
+            at = slice(c * columns, (c + 1) * columns)
+            gate = jnp.dot(rows, gate_w[:, at], preferred_element_type=f32)
+            up = jnp.dot(rows, up_w[:, at], preferred_element_type=f32)
+            gate_all[i, :, at] = gate
+            up_all[i, :, at] = up
+            hidden_at[slot, :, at] = (gate * jax.nn.sigmoid(gate) * up).astype(low)
+        put(0, slot, hidden_at, hidden_out, tile).start()
+        half = down_w.shape[1] // 2
+        for c in range(2):
+            at = slice(c * half, (c + 1) * half)
+            result = jnp.dot(hidden_at[slot], down_w[:, at], preferred_element_type=f32)
+            mixed_at[slot, :, at] = (result.astype(low).astype(f32) * weight[tile]).astype(low)
+        put(1, slot, mixed_at, mixed_out, tile).start()
+        return carry
+
+    lax.fori_loop(0, tiles, forward, 0)
+    grad_keep.wait()
+
+    def backward(i, carry):
+        arrivals(grad, i, {})
+        tile = tile_of(i)
+        slot = lax.rem(i, 2)
+
+        @pl.when(i >= 2)
+        def _():
+            before = tile_of(i - 2)
+            put(2, slot, expert_at, expert_out, before).wait()
+            put(3, slot, gate_at, gate_out, before).wait()
+            put(4, slot, up_at, up_out, before).wait()
+            put(5, slot, left_at, pair_out[0], before).wait()
+            put(6, slot, right_at, pair_out[1], before).wait()
+
+        rows = grad_all[pl.ds(2 * tile, 2)].reshape(-1, grad_all.shape[2])
+        expert_at[slot] = (rows.astype(f32) * weight[tile]).astype(low)
+        put(2, slot, expert_at, expert_out, tile).start()
+        for c in range(2):
+            at = slice(c * columns, (c + 1) * columns)
+            d_hidden = contract_cols(expert_at[slot], down_w[at, :])
+            gate, up = gate_all[i, :, at], up_all[i, :, at]
+            sigma = jax.nn.sigmoid(gate)
+            gate_at[slot, :, at] = (
+                d_hidden * up * sigma * (1.0 + gate * (1.0 - sigma))
+            ).astype(low)
+            up_at[slot, :, at] = (d_hidden * (gate * sigma)).astype(low)
+        put(3, slot, gate_at, gate_out, tile).start()
+        put(4, slot, up_at, up_out, tile).start()
+        half = gate_w.shape[0] // 2
+        for c, staged in enumerate((left_at, right_at)):
+            at = slice(c * half, (c + 1) * half)
+            staged[slot] = (
+                contract_cols(gate_at[slot], gate_w[at, :]) + contract_cols(up_at[slot], up_w[at, :])
+            ).astype(low)
+            put(5 + c, slot, staged, pair_out[c], tile).start()
+        return carry
+
+    lax.fori_loop(0, tiles, backward, 0)
+    ffn.finish()
+    grad.finish()
+    for i in range(tiles):
+        keep_rows(i).wait()
+    outs = (hidden_out, mixed_out, expert_out, gate_out, up_out, pair_out[0], pair_out[1])
+    staged = (hidden_at, mixed_at, expert_at, gate_at, up_at, left_at, right_at)
+    for i in (tiles - 2, tiles - 1):
+        for number in range(7):
+            put(number, i % 2, staged[number], outs[number], tile_of(i)).wait()
+
+
+def run_experts(ffn_in, own_grad, weight, gate_w, up_w, down_w, collective_id):
+    count = lax.axis_size("shard")
+    rows, width = ffn_in.shape
+    inner = gate_w.shape[1]
+    tiles, two = count // 2, 2 * rows
+    low = ffn_in.dtype
+    shape = jax.ShapeDtypeStruct
+    wide, narrow = (tiles, two, width), (tiles, two, inner)
+    outs = [shape((count, rows, width), low)]
+    outs += [shape(s, low) for s in (narrow, wide, wide, narrow, narrow)]
+    outs += [shape((tiles, two, width // 2), low)] * 2
+    vmem, hbm = pl.BlockSpec(memory_space=pltpu.VMEM), pl.BlockSpec(memory_space=pl.ANY)
+    staged = [inner, width, width, inner, inner, width // 2, width // 2]
+    return pl.pallas_call(
+        functools.partial(expert_kernel, count),
+        out_shape=outs,
+        in_specs=[vmem] * 3 + [hbm] * 3,
+        out_specs=[hbm] * len(outs),
+        scratch_shapes=[
+            pltpu.VMEM((count, rows, width), low),
+            pltpu.VMEM((count, rows, width), low),
+            pltpu.VMEM(gate_w.shape, low),
+            pltpu.VMEM(up_w.shape, low),
+            pltpu.VMEM(down_w.shape, low),
+            pltpu.VMEM((tiles, two, inner), jnp.float32),
+            pltpu.VMEM((tiles, two, inner), jnp.float32),
+        ]
+        + [pltpu.VMEM((2, two, cols), low) for cols in staged]
+        + [pltpu.SemaphoreType.DMA((count,))] * 4
+        + [
+            pltpu.SemaphoreType.DMA((3,)),
+            pltpu.SemaphoreType.DMA((2,)),
+            pltpu.SemaphoreType.DMA((tiles,)),
+            pltpu.SemaphoreType.DMA((len(staged), 2)),
+        ],
+        compiler_params=pltpu.CompilerParams(
+            collective_id=collective_id, has_side_effects=True, vmem_limit_bytes=VMEM_LIMIT
+        ),
+        name="run_experts",
+    )(ffn_in, own_grad, weight, gate_w, up_w, down_w)
 
 
 GAIN_LANES = 128
@@ -375,8 +696,6 @@
     group_tok = tok_rows * seq_count
     experts = lax.axis_size("shard")
     shard_at = lax.axis_index("shard")
-    top_count = expert_ids.shape[-1]
-    capacity = min(tok_rows, 3 * tok_rows * top_count // (2 * experts))
     weight_rows = weight_qkv.shape[0]
     heads_local = HEADS // seq_count
     local_width = heads_local * HEAD_DIM
@@ -406,8 +725,6 @@
     qkv_cols, full_out, tables_all = gather_blocks(
         [own_block, weight_out, table], 1, ((0,), (1, 2))
     )
-    own_grad, qkv_cols = lax.optimization_barrier((out_cotangent[0], qkv_cols))
-    grad_all = lax.all_gather(own_grad, "shard", axis=0, tiled=False)
     qkv_cols = qkv_cols.reshape(width, 3 * local_width + GAIN_LANES)
     gain_cols = qkv_cols[:, 3 * local_width :][:, : norm_gains.shape[1]].astype(f32)
     qkv_cols = qkv_cols[:, : 3 * local_width]
@@ -465,50 +782,46 @@
     ffn_n = resid * ffn_r
     ffn_in = (ffn_n * gain_cols[:, 3]).astype(low)
 
-    (ffn_all,) = gather_blocks([ffn_in], 2)
-    named = pair_weight > 0.0
-    rank = jnp.cumsum(named.astype(jnp.int32), axis=1) - 1
-    slots = jnp.arange(capacity, dtype=jnp.int32)
-    pick = (rank[:, None, :] == slots[None, :, None]) & named[:, None, :]
-    pick_low = pick.astype(low)
-    slot_weight = jnp.sum(jnp.where(pick, pair_weight[:, None, :], 0.0), axis=2)
-
-    def gather_rows(rows):
-        return jnp.einsum("brt,btd->brd", pick_low, rows, preferred_element_type=f32)
-
-    def spread_rows(rows):
-        return jnp.einsum(
-            "brt,brd->btd",
-            pick_low,
-            rows.reshape(experts, capacity, width),
-            preferred_element_type=f32,
-        )
-
+    pairs = seq_count == 2
     gate_weight = weight_gate[0]
     up_weight = weight_up[0]
     down_weight = weight_down[0]
-    rows_in = gather_rows(ffn_all).astype(low).reshape(-1, width)
-    gate = jnp.dot(rows_in, gate_weight, preferred_element_type=f32)
-    up = jnp.dot(rows_in, up_weight, preferred_element_type=f32)
-    sigma = jax.nn.sigmoid(gate)
-    silu = gate * sigma
-    hidden = (silu * up).astype(low)
-    d_expert = (gather_rows(grad_all) * slot_weight[:, :, None]).astype(low).reshape(-1, width)
-    d_hidden = contract_cols(d_expert, down_weight)
-    d_gate = (d_hidden * up * sigma * (1.0 + gate * (1.0 - sigma))).astype(low)
-    d_up = (d_hidden * silu).astype(low)
-    d_pair = (contract_cols(d_gate, gate_weight) + contract_cols(d_up, up_weight)).astype(low)
-    expert_out = jnp.dot(hidden, down_weight, preferred_element_type=f32).astype(low)
-    out_part = (spread_rows(expert_out) * pair_weight[:, :, None]).astype(low)
-    part_down = contract_rows(hidden, d_expert).astype(low)
-    part_gate = contract_rows(rows_in, d_gate).astype(low)
-    part_up = contract_rows(rows_in, d_up).astype(low)
-    d_spread = spread_rows(d_pair).astype(low)
-    pairs = seq_count == 2
-    d_ffn_in, *came_down = scatter_sum([d_spread], 3, f32, sides=[part_down] if pairs else [])
+    if experts <= 16:
+        tile_weight = pair_weight.reshape(experts // 2, 2 * tok_rows, 1)
+        results = run_experts(
+            ffn_in, out_cotangent[0], tile_weight, gate_weight, up_weight, down_weight, 2
+        )
+        rows_in, hidden, out_part, d_expert, d_gate, d_up, *halves = (
+            result.reshape(experts * tok_rows, -1) for result in results
+        )
+    else:
+        slot_weight = pair_weight.reshape(-1, 1)
+        (ffn_all, grad_all) = gather_blocks([ffn_in, out_cotangent[0]], 2, ((0,), (1,)))
+        rows_in = ffn_all.reshape(-1, width)
+        gate = jnp.dot(rows_in, gate_weight, preferred_element_type=f32)
+        up = jnp.dot(rows_in, up_weight, preferred_element_type=f32)
+        sigma = jax.nn.sigmoid(gate)
+        silu = gate * sigma
+        hidden = (silu * up).astype(low)
+        expert_out = jnp.dot(hidden, down_weight, preferred_element_type=f32).astype(low)
+        out_part = (expert_out.astype(f32) * slot_weight).astype(low)
+        d_expert = (grad_all.reshape(-1, width).astype(f32) * slot_weight).astype(low)
+        d_hidden = contract_cols(d_expert, down_weight)
+        d_gate = (d_hidden * up * sigma * (1.0 + gate * (1.0 - sigma))).astype(low)
+        d_up = (d_hidden * silu).astype(low)
+        d_pair = contract_cols(d_gate, gate_weight) + contract_cols(d_up, up_weight)
+        halves = jnp.split(d_pair.astype(low), 2, axis=1)
+    halves = [part.reshape(experts, tok_rows, -1) for part in halves]
+    products = [(hidden, d_expert), (rows_in, d_gate), (rows_in, d_up)]
+    if pairs:
+        results = scatter_sum(halves, 3, f32, work=ExpertGrads(products))
+        d_left, d_right, down_came, down_mine, gate_there, gate_mine, up_there, up_mine = results
+    else:
+        d_left, d_right = scatter_sum(halves, 3, f32)
+    d_ffn_in = jnp.concatenate([d_left, d_right], axis=1)
     out_part, d_ffn_in = lax.optimization_barrier((out_part, d_ffn_in))
     mixed_out = lax.psum_scatter(
-        out_part.reshape(experts * tok_rows, width), "shard", scatter_dimension=0, tiled=True
+        out_part, "shard", scatter_dimension=0, tiled=True
     ).astype(f32)
     layer_output = (resid + mixed_out).astype(low)
 
@@ -573,19 +886,22 @@
     ]
     terms += [contract_rows(mix_all, branch_cols), gain_terms]
     terms = [term.astype(low).reshape(experts, weight_rows, -1) for term in terms]
-    results = scatter_sum(
-        terms, 4, low, seq_count, sides=[part_gate, part_up] if pairs else []
-    )
+    sides = [gate_there, up_there] if pairs else []
+    results = scatter_sum(terms, 4, low, seq_count, sides=sides)
     *sums, sum_gains = results[: len(terms)]
-    came = list(results[len(terms) :]) + came_down
     if pairs:
+        gate_came, up_came = results[len(terms) :]
         sum_gate, sum_up, sum_down = (
-            lax.dynamic_slice_in_dim(part, seq_at * other.shape[0], other.shape[0]).astype(f32)
-            + other.astype(f32)
-            for part, other in zip((part_gate, part_up, part_down), came)
+            mine.astype(f32) + came.astype(f32)
+            for mine, came in ((gate_mine, gate_came), (up_mine, up_came), (down_mine, down_came))
         )
     else:
-        sum_gate, sum_up, sum_down = (seq_sum(p) for p in (part_gate, part_up, part_down))
+        sum_down, sum_gate, sum_up = (
+            lax.psum_scatter(
+                contract_rows(left, right).astype(low), "seq", scatter_dimension=0, tiled=True
+            ).astype(f32)
+            for left, right in products
+        )
     targets = [(0, 0), (0, width), (0, 2 * width), (1, 0)]
     rows_qkv, rows_out = place_rows(sums, targets, (3 * width, width))
     rows_gain = jnp.sum(sum_gains[:, :, : norm_gains.shape[1]].astype(f32), axis=0)

time: 715 us -> 631 us (0.88)
  matrix products: 169 us -> 53.8 us
  Pallas kernels: 441 us -> 462 us
  local copies, waits for them, and re-layouts: 16.7 us -> 24.5 us
    pallas_call x0 -> x1, Pallas kernels: none -> 115 us  [run_experts(): pl.pallas_call(functools.partial(expert_kernel, count), out_shape=outs, i...]
    pallas_call x2 -> x1, Pallas kernels: 226 us -> 146 us  [gather_blocks(): pl.pallas_call(functools.partial(gather_kernel, count, groups), out_shape...]
    dot_general x7 -> x0, matrix products: 46.4 us -> none  [the longest x2 10.5 us: gather_rows(): jnp.einsum('brt,btd->brd', pick_low, rows, preferred_element_type=f32)]
    dot_general x5 -> x2, matrix products: 50.1 us -> 15.3 us  [contract_cols(): lax.dot_general(left_side, right_side, (((1,), (1,)), ((), ())), preferre...]
    dot_general x7 -> x4, matrix products: 49.4 us -> 14.8 us  [contract_rows(): lax.dot_general(left_side, right_side, (((0,), (0,)), ((), ())), preferre...]
    pallas_call x2, Pallas kernels: 211 us -> 198 us  [scatter_sum(): pl.pallas_call(functools.partial(scatter_kernel, count, seq_count, arrays...]
  transfers between devices with their start and end apart: 8 -> 7, of which waited for: 1 -> 2; matrix products, arithmetic and copies ran while one was open for 30% -> 14% of each run, Pallas kernels for 62% -> 74%
where the time goes in v3:
time: 631 us; the launch traced here: 622 us
  Pallas kernels  462 us (73%)
  matrix products  53.8 us (9%)
  other arithmetic  36.9 us (6%)
  local copies, waits for them, and re-layouts  24.5 us (4%)
  between operations  14.6 us (2%)
  starting transfers between devices  14.1 us (2%)
  blocking collectives  10.1 us (2%)
    pallas_call x2, Pallas kernels, scatter_sum(): pl.pallas_call(functools.partial(scatter_kernel, count, seq_count, arrays...  198 us
    pallas_call x1, Pallas kernels, gather_blocks(): pl.pallas_call(functools.partial(gather_kernel, count, groups), out_shape...  146 us
    pallas_call x1, Pallas kernels, run_experts(): pl.pallas_call(functools.partial(expert_kernel, count), out_shape=outs, i...  115 us
    dot_general x2, matrix products, contract_cols(): lax.dot_general(left_side, right_side, (((1,), (1,)), ((), ())), preferre...  15.3 us
    dot_general x4, matrix products, contract_rows(): lax.dot_general(left_side, right_side, (((0,), (0,)), ((), ())), preferre...  14.8 us
  transfers between devices with their start and end apart: 7, of which 2 were waited for; matrix products, arithmetic and copies ran while one was open for 14% of the time, Pallas kernels for 74%

profile of v3, /device:TPU:0, one launch (start us, length us, event | category | flops | bytes accessed | tf_op | source)
XLA Modules:
  0.0 622.2 jit_solution(13593987410278850294)
XLA Ops:
  7.2 0.7 all-gather.6.cloned.1.call-update
  7.9 1.9 copy.132
  10.7 0.9 fusion.28.refs_0_
  11.6 0.6 select_reduce_fusion.refs_2_
  12.2 146.3 %gather_blocks_1.1 = (bf16[16,128,3200]{2,1,0:T(8,128)(2,1)}, bf16[16,128,2048]{2,1,0:T(8,128)(2,1)}, f32[16,16,128]{2,1,0:T(8,128)}) custom-call(bf16[128,3200]{1,0:T(8,128)(2,1)} %fusion.28.refs_0_, bf16[128,2048]{1,0:T(8,128)(2,1)} %refs_1_.1, f32[16,128]{1,0:T(8,128)} %select_reduce_fusion.refs_2_), custom_call_target="tpu_custom_call" | custom-call | tf_op jit(solution)/shard_map/gather_blocks_1/pallas_call | solution.py:188
  158.5 1.1 slice.85
  160.6 0.5 fusion.42
  161.1 1.5 fusion.8
  162.6 6.8 %fusion.3 = f32[256,3072]{1,0:T(8,128)S(1)} fusion(bf16[2048,3200]{1,0:T(8,128)(2,1)} %bitcast.219, f32[2048]{0:T(1024)S(1)} %bitcast.202, f32[256]{0:T(256)S(1)} %add_rsqrt_fusion, bf16[1,256,2048]{2,1,0:T(8,128)(2,1)} %all-gather.6.cloned.1.call-done), kind=kOutput, calls=%fused_computation.3 | convolution fusion | flops 3223322624 | bytes 16786432 | tf_op jit(solution)/shard_map/dot_general | solution.py:756
  169.5 1.7 copy-done.1
  171.3 4.9 psum.14
  176.3 1.8 multiply_bitcast_fusion.1
  179.2 1.8 subtract_convert_fusion.1
  181.0 2.8 fusion.55
  183.7 2.3 convolution_convert_fusion.6
  186.3 0.9 copy.142
  187.1 3.5 all-to-all-start
  190.7 0.9 dynamic-slice_reduce_fusion
  191.5 1.8 reshape.374.refs_2_
  193.5 4.8 all-to-all-done
  198.3 4.9 multiply_reduce_fusion.7
  203.2 1.0 multiply_convert_fusion.4.refs_0_
  204.2 114.9 %run_experts.1 = (bf16[16,128,2048]{2,1,0:T(8,128)(2,1)}, bf16[8,256,1024]{2,1,0:T(8,128)(2,1)}, bf16[8,256,2048]{2,1,0:T(8,128)(2,1)}, bf16[8,256,2048]{2,1,0:T...) custom-call(bf16[128,2048]{1,0:T(8,128)(2,1)} %multiply_convert_fusi, ...), custom_call_target="tpu_custom_call" | custom-call | tf_op jit(solution)/shard_map/run_experts/pallas_call | solution.py:640
  319.1 73.2 %scatter_sum_3.1 = (f32[128,1024]{1,0:T(8,128)}, f32[128,1024]{1,0:T(8,128)}, bf16[512,2048]{1,0:T(8,128)(2,1)}, bf16[512,2048]{1,0:T(8,128)(2,1)}, bf16[1024,10...) custom-call(bf16[16,128,1024]{2,1,0:T(8,128)(2,1)} %bitcast.185, ...), custom_call_target="tpu_custom_call" | custom-call | tf_op jit(solution)/shard_map/scatter_sum_3/pallas_call | solution.py:402
  392.3 1.3 pad_maximum_fusion
  393.7 1.1 copy-done
  394.8 1.5 convert_multiply_fusion
  397.1 7.2 %convolution_convert_fusion.4 = bf16[128,2048]{1,0:T(8,128)(2,1)S(1)} fusion(bf16[128,2048]{1,0:T(8,128)(2,1)S(1)} %fusion.50, bf16[2048,2048]{1,0:T(8,128)(2,1)} %bitcast.167), kind=kOutput, calls=%fused_computation.16 | convolution fusion | flops 1074003968 | bytes 9437184 | tf_op jit(solution)/shard_map/dot_general | solution.py:65
  404.3 0.8 copy.211
  405.1 4.2 all-to-all-start.1
  409.3 5.5 add_bitcast_fusion
  414.9 0.9 copy.210
  416.0 4.2 all-to-all-start.2
  420.2 1.9 copy.183
  422.2 2.2 copy.155
  424.3 3.1 convolution_convert_fusion.5
  427.4 2.1 copy.169
  429.5 2.7 multiply_reduce_fusion
  432.2 0.4 multiply_convert_fusion
  432.6 0.7 copy-done.22
  433.4 0.5 fusion.19
  433.9 0.5 copy-done.19
  434.6 0.7 fusion.21
  435.4 1.0 multiply_subtract_fusion.1
  436.4 0.9 copy-done.2
  437.3 1.0 fusion.23
  438.4 5.1 psum.15
  443.5 3.9 multiply_convert_fusion.3
  447.5 8.1 %fusion.5 = bf16[256,2048]{1,0:T(8,128)(2,1)S(1)} fusion(bf16[2048,3200]{1,0:T(8,128)(2,1)} %bitcast.220, bf16[256,1024]{1,0:T(8,128)(2,1)S(1)} %copy-done.28, bf16[256,1024]{1,0:T(8,128)(2,1)S(1)} %get-tuple-element.97, bf16[256,1024]{1,0:T(8,128)(2,1)S(1)} %get-tuple-element.96), kind=kOutput, calls=%fused_computation.14 | convolution fusion | flops 3226468352 | bytes 15204352 | tf_op jit(solution)/shard_map/dot_general | solution.py:65
  455.7 2.1 collective-permute-start
  457.7 3.3 convolution_convert_fusion.1
  461.1 3.4 convolution_convert_fusion.2
  464.6 3.4 convolution_convert_fusion.3
  468.0 0.4 multiply_reduce_fusion.2
  468.4 0.4 copy-done.24
  469.1 0.9 pad.10.clone
  470.1 4.6 convolution_convert_fusion
  474.6 124.3 %scatter_sum_4.1 = (bf16[2,128,1024]{2,1,0:T(8,128)(2,1)}, bf16[2,128,1024]{2,1,0:T(8,128)(2,1)}, bf16[2,128,1024]{2,1,0:T(8,128)(2,1)}, bf16[2,128,1024]{2,1,0:...) custom-call(bf16[16,128,1024]{2,1,0:T(8,128)(2,1)} %bitcast.170, ...), custom_call_target="tpu_custom_call" | custom-call | tf_op jit(solution)/shard_map/scatter_sum_4/pallas_call | solution.py:402
  598.9 0.9 convert_reduce_fusion
  599.8 0.7 copy.160
  600.5 3.7 place_rows.1
  604.2 5.3 add_bitcast_fusion.1
  609.5 2.9 add_bitcast_fusion.2
  612.4 3.0 fusion.30
  (114 shorter events, 5.4 us)
Async XLA Ops:
  7.2 153.9 %all-gather.6.cloned.1.call-start = ((), (), s32[]{:S(2)}) async-start(), calls=%async_computation.6 | async-start | bytes 1572864 | tf_op jit(solution)/shard_map/all_gather | solution.py:732
  9.8 0.7 copy-start.31
  9.8 1.8 copy-start.29
  9.8 1.8 copy-start.30
  10.6 149.2 %copy-start.32 = (s32[1,3]{1,0:T(1,128)S(1)}, s32[1,3]{1,0:T(1,128)}, u32[]{:S(2)}) copy-start(s32[1,3]{1,0:T(1,128)} %param.13) | copy-start | bytes 40
  10.6 149.2 %copy-start.33 = (s32[1,3]{1,0:T(1,128)S(1)}, s32[1,3]{1,0:T(1,128)}, u32[]{:S(2)}) copy-start(s32[1,3]{1,0:T(1,128)} %param.14) | copy-start | bytes 40
  169.4 1.7 copy-start.1
  181.0 2.8 copy-start.18
  181.0 2.8 copy-start.20
  183.7 2.4 copy-start.15
  186.1 7.3 %copy-start.17 = (bf16[8,128,256]{2,1,0:T(8,128)(2,1)}, bf16[8,128,256]{2,1,0:T(8,128)(2,1)S(1)}, u32[]{:S(2)}) copy-start(bf16[8,128,256]{2,1,0:T(8,128)(2,1)S(1)} %convolution_convert_fusion.6) | copy-start | bytes 1572868
  186.2 12.1 %copy-start.13 = (bf16[1,128,2048]{2,1,0:T(8,128)(2,1)S(1)}, bf16[1,128,2048]{2,1,0:T(8,128)(2,1)}, u32[]{:S(2)}) copy-start(bf16[1,128,2048]{2,1,0:T(8,128)(2,1)} %param.12) | copy-start | bytes 1572868
  187.1 11.2 %all-to-all-start = ((bf16[2,128,1024]{1,2,0:T(8,128)(2,1)}), bf16[2,128,1024]{1,2,0:T(8,128)(2,1)S(1)}, u32[]{:S(2)}, u32[]{:S(2)}) async-start(bf16[2,128,1024]{1,2,0:T(8,128)(2,1)} %copy.142), calls=%async_computation | async-start | bytes 1048576 | tf_op jit(solution)/shard_map/all_to_all | solution.py:778
  190.6 279.4 %all-gather.4.cloned.1.call-start = ((), (), s32[]{:S(2)}) async-start(), calls=%async_computation.5 | async-start | bytes 1572864 | tf_op jit(solution)/shard_map/all_gather | solution.py:779
  193.4 419.0 %reduce-scatter.2.cloned.1.call-start = ((), (), s32[]{:S(2)}) async-start(), calls=%async_computation.4 | async-start | bytes 8912896 | tf_op jit(solution)/shard_map/reduce_scatter | solution.py:823
  393.6 1.2 copy-start
  394.8 1.9 copy-start.8
  397.1 7.2 %copy-start.10 = (bf16[128,2048]{1,0:T(8,128)(2,1)}, bf16[128,2048]{1,0:T(8,128)(2,1)S(1)}, u32[]{:S(2)}) copy-start(bf16[128,2048]{1,0:T(8,128)(2,1)S(1)} %fusion.50) | copy-start | bytes 1572868
  405.1 10.9 %all-to-all-start.1 = ((bf16[128,2,1024]{2,0,1:T(8,128)(2,1)}), bf16[128,2,1024]{2,0,1:T(8,128)(2,1)}, u32[]{:S(2)}, u32[]{:S(2)}) async-start(bf16[128,2,1024]{2,0,1:T(8,128)(2,1)} %bitcast.199), calls=%async_computation.2 | async-start | bytes 1048576 | tf_op jit(solution)/shard_map/all_to_all | solution.py:836
  409.3 5.6 copy-start.11
  416.0 54.1 %all-to-all-start.2 = ((bf16[128,2,1024]{2,0,1:T(8,128)(2,1)}), bf16[128,2,1024]{2,0,1:T(8,128)(2,1)}, u32[]{:S(2)}, u32[]{:S(2)}) async-start(bf16[128,2,1024]{2,0,1:T(8,128)(2,1)} %bitcast.198), calls=%async_computation.3 | async-start | bytes 1048576 | tf_op jit(solution)/shard_map/all_to_all | solution.py:839
  429.5 2.8 copy-start.16
  432.2 1.0 copy-start.22
  432.2 1.2 copy-start.23
  433.4 1.1 copy-start.19
  433.4 1.2 copy-start.21
  435.3 1.9 copy-start.2
  436.3 1.9 copy-start.3
  436.4 1.9 copy-start.4
  436.4 1.9 copy-start.5
  436.4 2.0 copy-start.6
  443.5 3.9 copy-start.28
  447.4 10.3 %copy-start.14 = (bf16[8,128,256]{2,1,0:T(8,128)(2,1)S(1)}, bf16[8,128,256]{2,1,0:T(8,128)(2,1)}, u32[]{:S(2)}) copy-start(bf16[8,128,256]{2,1,0:T(8,128)(2,1)} %convolution_convert_fusion.5) | copy-start | bytes 1572868
  455.6 12.4 %copy-start.12 = (bf16[256,2048]{1,0:T(8,128)(2,1)}, bf16[256,2048]{1,0:T(8,128)(2,1)S(1)}, u32[]{:S(2)}) copy-start(bf16[256,2048]{1,0:T(8,128)(2,1)S(1)} %fusion.5) | copy-start | bytes 3145732
  455.7 12.3 %collective-permute-start = (bf16[128,2048]{1,0:T(8,128)(2,1)S(1)}, bf16[128,2048]{1,0:T(8,128)(2,1)S(1)}, u32[]{:S(2)}, u32[]{:S(2)}) collective-permute-start(bf16[128,2048]{1,0:T(8,128)(2,1)S(1)} %dynamic-slice_bitcast_fusion), channel_id=1, source_target_pairs={{0,16},{16,0},{1,17},{17,1},{2,18},{18,2},{3,19},{19,3},{4,20},{20... | collective-permute-start | bytes 1572872 | tf_op jit(solution)/shard_map/ppermute | solution.py:716
  464.5 3.4 copy-start.7
  468.0 0.8 copy-start.24
  604.2 5.3 copy-start.26
  604.2 5.3 copy-start.27
  609.5 2.9 copy-start.9
  609.5 2.9 copy-start.25
Sparse Core Ops, SparseCore 0:
  9.5 23.9 all-gather.5
  193.5 18.9 all-gather.3
  393.8 102.0 reduce-scatter.1

commit v4 on v3

--- a/solution.py
+++ b/solution.py
@@ -124,75 +124,193 @@
     return sorted(range(2, count, 2), key=key)
 
 
-def gather_kernel(count, groups, *refs):
+LINE = 16
+
+
+class Line:
+    def __init__(self, count, own, full, send, recv, seq, pieces=1):
+        me = lax.axis_index("shard")
+        spot = me // 4
+        self.upper = spot // 2
+        self.inner = spot + self.upper * (3 - 2 * spot)
+        self.y = lax.rem(me // 2, 2)
+        self.core = lax.rem(me, 2)
+        low = lax.rem(me, 4)
+        near = (seq, self.block(1) * 4 + low)
+        far = (seq, (3 - spot) * 4 + low)
+        across = (seq, spot * 4 + (1 - self.y) * 2 + self.core)
+        twin = (seq, spot * 4 + self.y * 2 + 1 - self.core)
+        self.peers = (near, far, across, twin)
+        self.copies = []
+        self.inward = []
+        rows = own.shape[0] // pieces
+        for p in range(pieces):
+            at = pl.ds(p * rows, rows)
+            target = [full.at[self.place(r), at] for r in range(count)]
+            source = [own.at[at]] + target[1:]
+
+            def copy(r, sent, received, device, source=source, target=target, p=p):
+                return remote(
+                    source[r], target[r], send.at[p, sent], recv.at[p, received], device
+                )
+
+            copies = {4: copy(0, 4, 4, near)}
+            for r in range(0, count, 4):
+                copies[r | 2] = copy(r, r | 2, r | 2, across)
+            for r in range(0, count, 2):
+                copies[r | 1] = copy(r, r | 1, r | 1, twin)
+            inward = {0: copy(0, 8, 8, far), 4: copy(4, 12, 12, far)}
+            inward[8] = copy(8, 0, 8, near)
+            inward[12] = copy(12, count, 12, near)
+            copies[8] = inward[0]
+            copies[12] = inward[4]
+            self.copies.append(copies)
+            self.inward.append(inward)
+
+    def block(self, k):
+        if isinstance(k, int):
+            spot = k if k >= 2 else self.inner + k * (1 - 2 * self.inner)
+        else:
+            far = k // 2
+            spot = far * k + (1 - far) * lax.rem(k + self.inner, 2)
+        return spot + self.upper * (3 - 2 * spot)
+
+    def place(self, r):
+        y = (1 - self.y) if r & 2 else self.y
+        core = (1 - self.core) if r & 1 else self.core
+        return self.block(r >> 2) * 4 + y * 2 + core
+
+    def pair(self, i):
+        k, y = i // 2, lax.rem(i, 2)
+        return self.block(k) * 2 + self.y + y - 2 * self.y * y
+
+    def meet(self):
+        barrier = pltpu.get_barrier_semaphore()
+        for peer in self.peers:
+            pl.semaphore_signal(barrier, 1, device_id=peer, device_id_type=MESH_ID)
+        pl.semaphore_wait(barrier, len(self.peers))
+
+    def start(self, r):
+        for p in range(len(self.copies)):
+            self.start_piece(p, r)
+
+    def start_piece(self, p, r):
+        copies, inward = self.copies[p], self.inward[p]
+        if r == 0:
+            copies[4].start()
+        if r % 4 == 0:
+
+            @pl.when(self.inner == 1)
+            def _():
+                inward[r].start()
+
+            copies[r | 2].start()
+        copies[r | 1].start()
+
+    def arrive(self, r):
+        for p in range(len(self.copies)):
+            self.copies[p][r].wait_recv()
+            self.start_piece(p, r)
+
+    def wait_twin(self, r):
+        for copies in self.copies:
+            copies[r | 1].wait_recv()
+
+    order = (4, 2, 8, 6, 12, 10, 14)
+
+    def finish(self):
+        for copies, inward in zip(self.copies, self.inward):
+            for r in (4, 2, 6, 10, 14, 1, 3, 5, 7, 9, 11, 13, 15):
+                copies[r].wait_send()
+
+            @pl.when(self.inner == 1)
+            def _(inward=inward):
+                for copy in inward.values():
+                    copy.wait_send()
+
+
+class Tree:
+    def __init__(self, count, own, full, send, recv, seq, pieces=1):
+        self.count, self.seq = count, seq
+        self.place = relative_place(count, lax.axis_index("shard"))
+        self.order = arrival_order(count)
+        self.copies = {}
+        for r in range(count):
+            below = low_bit(r) if r else count
+            for bit in bit_list(count):
+                if bit < below:
+                    self.copies[r | bit] = remote(
+                        own if r == 0 else full.at[self.place(r)],
+                        full.at[self.place(r)],
+                        send.at[0, r | bit],
+                        recv.at[0, r | bit],
+                        (seq, self.place(bit)),
+                    )
+
+    def meet(self):
+        meet(self.count, self.place, self.seq)
+
+    def start(self, r):
+        below = low_bit(r) if r else self.count
+        bits = [bit for bit in bit_list(self.count) if bit < below]
+        for bit in sorted(bits, key=lambda bit: (bit < 4, bit)):
+            self.copies[r | bit].start()
+
+    def arrive(self, r):
+        self.copies[r].wait_recv()
+        self.start(r)
+
+    def wait_twin(self, r):
+        self.copies[r | 1].wait_recv()
+
+    def finish(self):
+        for copy in self.copies.values():
+            copy.wait_send()
+
+
+def gather_kernel(count, groups, pieces, *refs):
     arrays = sum(len(group) for group in groups)
     own, full = refs[:arrays], refs[arrays : 2 * arrays]
     send, recv, local = refs[2 * arrays :]
     me = lax.axis_index("shard")
     seq = lax.axis_index("seq")
-    place = relative_place(count, me)
-    meet(count, place, seq)
-    copies = {}
-
-    def send_on(a, r):
-        source = own[a] if r == 0 else full[a].at[place(r)]
-        below = low_bit(r) if r else count
-        for bit in reversed(bit_list(count)):
-            if bit < below:
-                copy = remote(
-                    source,
-                    full[a].at[place(r)],
-                    send.at[a, r | bit],
-                    recv.at[a, r | bit],
-                    (seq, place(bit)),
-                )
-                copies[a, r | bit] = copy
-
-    def start(a, r):
-        send_on(a, r)
-        below = low_bit(r) if r else count
-        bits = [bit for bit in bit_list(count) if bit < below]
-        for bit in sorted(bits, key=lambda bit: (bit < 4, bit)):
-            copies[a, r | bit].start()
-
+    kind = Line if count == LINE else Tree
+    ways = [
+        kind(count, own[a], full[a], send.at[a], recv.at[a], seq, pieces[a])
+        for a in range(arrays)
+    ]
+    ways[0].meet()
     keeps = []
     for a in range(arrays):
         keep = pltpu.make_async_copy(own[a], full[a].at[me], local.at[a])
         keep.start()
         keeps.append(keep)
-    arrivals = arrival_order(count)
-    last = max(i for i, r in enumerate(arrivals) if not r & 2) + 1
-    events = [(0, 0)]
-    for g in range(len(groups)):
-        events += [(g, r) for r in arrivals[:last]]
-        if g + 1 < len(groups):
-            events.append((g + 1, 0))
-        events += [(g, r) for r in arrivals[last:]]
-    for g, r in events:
-        for a in groups[g]:
-            if r:
-                copies[a, r].wait_recv()
-            start(a, r)
+    for group in groups:
+        for a in group:
+            ways[a].start(0)
+        for r in ways[0].order:
+            for a in group:
+                ways[a].arrive(r)
     for a in range(arrays):
-        for r in range(1, count, 2):
-            copies[a, r].wait_recv()
-    for copy in copies.values():
-        copy.wait_send()
+        for r in range(0, count, 2):
+            ways[a].wait_twin(r)
+    for way in ways:
+        way.finish()
     for keep in keeps:
         keep.wait()
 
 
-def gather_blocks(blocks, collective_id, groups=((0,),)):
+def gather_blocks(blocks, collective_id, groups=((0,),), pieces=(1,)):
     count = lax.axis_size("shard")
     arrays = len(blocks)
     return pl.pallas_call(
-        functools.partial(gather_kernel, count, groups),
+        functools.partial(gather_kernel, count, groups, pieces),
         out_shape=[jax.ShapeDtypeStruct((count,) + b.shape, b.dtype) for b in blocks],
         in_specs=[pl.BlockSpec(memory_space=pltpu.VMEM)] * arrays,
         out_specs=[pl.BlockSpec(memory_space=pl.ANY)] * arrays,
         scratch_shapes=[
-            pltpu.SemaphoreType.DMA((arrays, count)),
-            pltpu.SemaphoreType.DMA((arrays, count)),
+            pltpu.SemaphoreType.DMA((arrays, max(pieces), count + 1)),
+            pltpu.SemaphoreType.DMA((arrays, max(pieces), count + 1)),
             pltpu.SemaphoreType.DMA((arrays,)),
         ],
         compiler_params=pltpu.CompilerParams(collective_id=collective_id, has_side_effects=True),
@@ -201,12 +319,15 @@
 
 
 def scatter_kernel(count, seq_count, arrays, sides, work, *refs):
-    parts, refs = refs[:arrays], refs[arrays:]
+    given = 0 if work.part_shapes else arrays
+    parts, refs = refs[:given], refs[given:]
     side_from, refs = refs[:sides], refs[sides:]
     work_in, refs = refs[: work.inputs], refs[work.inputs :]
     totals, refs = refs[:arrays], refs[arrays:]
     side_to, refs = refs[:sides], refs[sides:]
     work_out, refs = refs[: work.outputs], refs[work.outputs :]
+    if work.part_shapes:
+        parts, refs = refs[:arrays], refs[arrays:]
     held, refs = refs[:arrays], refs[arrays:]
     send, recv, seq_send, seq_recv, side_send, side_recv = refs[:6]
     planes = seq_count if seq_count > 1 else 1 + (sides > 0 or work.outputs > 0)
@@ -217,16 +338,14 @@
     meet(count, place, seq, planes)
     copies = {}
     shared = []
-    for i in range(sides):
-        copy = remote(
-            side_from[i],
-            side_to[i],
-            side_send.at[i],
-            side_recv.at[i],
-            (1 - seq, me),
-        )
-        copy.start()
-        shared.append(copy)
+
+    def start_sides():
+        for i in range(sides):
+            copy = remote(
+                side_from[i], side_to[i], side_send.at[i], side_recv.at[i], (1 - seq, me)
+            )
+            copy.start()
+            shared.append(copy)
 
     def share(a):
         for j in range(1, seq_count):
@@ -275,13 +394,23 @@
         elif r & upper:
             start(a, r, held[a].at[came])
 
-    chunks = [(a, u) for a in range(arrays) for u in reversed(range(count // 4))]
-    for a, u in chunks:
+    chunks = [
+        (a, u) for a in work.order or range(arrays) for u in reversed(range(count // 4))
+    ]
+
+    def prepare(a, u):
+        work.fill(parts, a, place(4 * u) - lax.rem(me, 4))
         for r in (4 * u + 3, 4 * u + 1):
             start(a, r, parts[a].at[place(r)])
-    tasks = work.tasks(seq, me, work_in, work_out, refs[6:])
+
+    tasks = work.tasks(seq, me, work_in, work_out, refs[6:], start_sides)
+    lead = AHEAD if work.part_shapes else len(chunks)
+    for a, u in chunks[:lead]:
+        prepare(a, u)
     steps = len(chunks) + AHEAD
     for i in range(steps):
+        if i + lead < len(chunks):
+            prepare(*chunks[i + lead])
         if i < len(chunks):
             a, u = chunks[i]
             fold(a, 4 * u + 2, 1)
@@ -291,7 +420,7 @@
             for bit in bits[1:]:
                 if 4 * u % (2 * bit) == 0:
                     fold(a, 4 * u, bit)
-        for task in tasks[len(tasks) * i // steps : len(tasks) * (i + 1) // steps]:
+        for task in work.at_step(tasks, i, steps):
             task()
     for copy in shared:
         copy.wait_recv()
@@ -302,16 +431,23 @@
 
 class NoWork:
     inputs = outputs = 0
-    operands, results, scratch = (), (), ()
-
-    def tasks(self, seq, me, arrays, results, scratch):
+    operands, results, scratch, part_shapes, order = (), (), (), (), ()
+
+    def fill(self, parts, a, base):
+        pass
+
+    def tasks(self, seq, me, arrays, results, scratch, start_sides):
+        start_sides()
         return []
+
+    def at_step(self, tasks, i, steps):
+        return tasks[len(tasks) * i // steps : len(tasks) * (i + 1) // steps]
 
     def finish(self):
         pass
 
 
-class ExpertGrads:
+class ExpertGrads(NoWork):
     def __init__(self, products):
         self.operands = []
         for pair in products:
@@ -335,7 +471,8 @@
             pltpu.SemaphoreType.DMA((2,)),
         ]
 
-    def tasks(self, seq, me, arrays, results, scratch):
+    def tasks(self, seq, me, arrays, results, scratch, start_sides):
+        start_sides()
         here, scratch = scratch[: self.inputs], scratch[self.inputs :]
         tiles, (in_sem, out_sem, side_sem) = scratch[: self.outputs], scratch[self.outputs :]
         loads = [
@@ -393,22 +530,144 @@
         self.remote.wait()
 
 
+class AttentionGrads(NoWork):
+    def __init__(self, attn_in, d_qkv, mix_all, branch, weights, tokens, d_resid, gains, gain):
+        self.operands = [attn_in, d_qkv, mix_all, branch, weights, tokens, d_resid, gains, gain]
+        self.inputs, self.outputs = len(self.operands), 1
+        low = attn_in.dtype
+        blocks, rows = weights.shape[:2]
+        self.local = d_qkv.shape[1] // 3
+        self.part_shapes = [
+            jax.ShapeDtypeStruct((blocks, rows, cols), low)
+            for cols in (self.local, self.local, self.local, branch.shape[1])
+        ]
+        self.part_shapes.append(jax.ShapeDtypeStruct(gains.shape, low))
+        self.order = (0, 1, 2, 4, 3)
+        self.results = [jax.ShapeDtypeStruct(tokens.shape, low)]
+        self.scratch = [pltpu.VMEM(a.shape, a.dtype) for a in self.operands]
+        self.scratch += [
+            pltpu.VMEM(tokens.shape, low),
+            pltpu.VMEM((2,) + tokens.shape, low),
+            pltpu.VMEM(tokens.shape, low),
+            pltpu.VMEM((ROW_TILE, tokens.shape[1]), jnp.float32),
+            pltpu.SemaphoreType.DMA((self.inputs,)),
+            pltpu.SemaphoreType.DMA((3,)),
+        ]
+
+    def need(self, *numbers):
+        for i in numbers:
+            if i not in self.waited:
+                self.loads[i].wait()
+                self.waited.add(i)
+
+    def fill(self, parts, a, base):
+        part = parts[a]
+        if a == 4:
+            part[pl.ds(base, 4)] = self.here[7][pl.ds(base, 4)].astype(part.dtype)
+            return
+        left, right = (2, 3) if a == 3 else (0, 1)
+        self.need(left, right)
+        rows, cols = part.shape[1:]
+        first = 0 if a == 3 else a * self.local
+
+        def step(i, carry):
+            at = pl.ds(pl.multiple_of((base + i) * rows, rows), rows)
+            part[base + i] = contract_rows(
+                self.here[left][:, at], self.here[right][:, first : first + cols]
+            ).astype(part.dtype)
+            return carry
+
+        lax.fori_loop(0, 4, step, 0)
+
+    def tasks(self, seq, me, arrays, results, scratch, start_sides):
+        self.here, scratch = scratch[: self.inputs], scratch[self.inputs :]
+        here = self.here
+        grad, part, came, total, in_sem, sem = scratch
+        self.loads = [
+            pltpu.make_async_copy(arrays[i], here[i], in_sem.at[i]) for i in range(self.inputs)
+        ]
+        self.waited = set()
+        for load in self.loads:
+            load.start()
+        blocks, rows = here[4].shape[:2]
+        inner = here[1].shape[1]
+        tok_rows, width = came.shape
+        self.exchange = remote(part.at[1 - seq], came, sem.at[0], sem.at[1], (1 - seq, me))
+        self.out = pltpu.make_async_copy(grad, results[0], sem.at[2])
+
+        def multiply(first, last):
+            self.need(1, 4)
+
+            def step(i, carry):
+                at = pl.ds(pl.multiple_of(2 * i * rows, 2 * rows), 2 * rows)
+                weight = here[4][pl.ds(2 * i, 2), :, :inner].reshape(2 * rows, inner)
+                result = contract_cols(here[1][...], weight)
+                part[:, :, at] = result.reshape(2, tok_rows, 2 * rows).astype(part.dtype)
+                return carry
+
+            lax.fori_loop(first, last, step, 0)
+
+        def send():
+            self.exchange.start()
+            start_sides()
+
+        def norm_back():
+            self.need(5, 6, 7, 8)
+            self.exchange.wait_recv()
+            total[...] = jnp.zeros_like(total)
+
+            def step(i, carry):
+                at = pl.ds(pl.multiple_of(i * ROW_TILE, ROW_TILE), ROW_TILE)
+                values = here[5][at, :].astype(jnp.float32)
+                scale = lax.rsqrt(jnp.mean(values * values, axis=-1, keepdims=True) + norm_eps)
+                normed = values * scale
+                d_out = part[seq, at, :].astype(jnp.float32) + came[at, :].astype(jnp.float32)
+                total[...] += d_out * normed
+                scaled = d_out * here[8][0:1, :]
+                mean = jnp.mean(scaled * normed, axis=-1, keepdims=True)
+                d_in = here[6][at, :] + scale * (scaled - normed * mean)
+                grad[at, :] = d_in.astype(grad.dtype)
+                return carry
+
+            lax.fori_loop(0, tok_rows // ROW_TILE, step, 0)
+            summed = jnp.sum(total[...], axis=0, keepdims=True)
+            for n in range(blocks):
+                here[7][n, 0:1, :] = summed[:, n * rows : (n + 1) * rows]
+            self.out.start()
+
+        pairs = blocks // 2
+        found = [functools.partial(multiply, i, i + 2) for i in range(0, pairs, 2)]
+        return found + [send, norm_back]
+
+    def at_step(self, tasks, i, steps):
+        parts = len(self.part_shapes) - 1
+        last = 3 * (steps - AHEAD) // (parts + 1) - AHEAD - 1
+        if i < len(tasks) - 2:
+            return [tasks[i]] + ([tasks[-2]] if i == len(tasks) - 3 else [])
+        return [tasks[-1]] if i == last else []
+
+    def finish(self):
+        self.exchange.wait_send()
+        self.out.wait()
+
+
 def scatter_sum(parts, collective_id, out_dtype, seq_count=1, sides=(), work=None):
     work = work or NoWork()
     count = lax.axis_size("shard")
-    arrays = len(parts)
+    shapes = list(work.part_shapes) or parts
+    arrays = len(shapes)
     lead = (seq_count,) if seq_count > 1 else ()
     others = max(seq_count - 1, 1)
     return pl.pallas_call(
         functools.partial(scatter_kernel, count, seq_count, arrays, len(sides), work),
-        out_shape=[jax.ShapeDtypeStruct(lead + p.shape[1:], out_dtype) for p in parts]
+        out_shape=[jax.ShapeDtypeStruct(lead + p.shape[1:], out_dtype) for p in shapes]
         + [jax.ShapeDtypeStruct(s.shape, s.dtype) for s in sides]
         + list(work.results),
-        in_specs=[pl.BlockSpec(memory_space=pltpu.VMEM)] * arrays
+        in_specs=[pl.BlockSpec(memory_space=pltpu.VMEM)] * len(parts)
         + [pl.BlockSpec(memory_space=pl.ANY)] * (len(sides) + work.inputs),
         out_specs=[pl.BlockSpec(memory_space=pltpu.VMEM)] * arrays
         + [pl.BlockSpec(memory_space=pl.ANY)] * (len(sides) + work.outputs),
-        scratch_shapes=[pltpu.VMEM(p.shape, p.dtype) for p in parts]
+        scratch_shapes=[pltpu.VMEM(p.shape, p.dtype) for p in list(work.part_shapes) + list(shapes)]
         + [
             pltpu.SemaphoreType.DMA((arrays, count)),
             pltpu.SemaphoreType.DMA((arrays, count)),
@@ -444,45 +703,6 @@
     )(*pieces)
 
 
-class Tree:
-    def __init__(self, count, own, full, send, recv, seq, place):
-        self.count, self.own, self.full = count, own, full
-        self.copies = {}
-        for r in range(count):
-            below = low_bit(r) if r else count
-            for bit in bit_list(count):
-                if bit < below:
-                    self.copies[r | bit] = remote(
-                        own if r == 0 else full.at[place(r)],
-                        full.at[place(r)],
-                        send.at[r | bit],
-                        recv.at[r | bit],
-                        (seq, place(bit)),
-                    )
-
-    def start(self, r):
-        below = low_bit(r) if r else self.count
-        bits = [bit for bit in bit_list(self.count) if bit < below]
-        for bit in sorted(bits, key=lambda bit: (bit < 4, bit)):
-            self.copies[r | bit].start()
-
-    def arrive(self, r):
-        self.copies[r].wait_recv()
-        self.start(r)
-
-    def steps(self):
-        order, done, found = arrival_order(self.count), 0, []
-        for i in range(self.count // 2):
-            upto = order.index(2 * i) + 1 if i else 0
-            found.append(order[done:upto])
-            done = max(done, upto)
-        return found
-
-    def finish(self):
-        for copy in self.copies.values():
-            copy.wait_send()
-
-
 def expert_kernel(count, *refs):
     (ffn_own, grad_own, weight), refs = refs[:3], refs[3:]
     matrices, refs = refs[:3], refs[3:]
@@ -493,12 +713,11 @@
     ffn_send, ffn_recv, grad_send, grad_recv, load, own_sem, rows_sem, out_sem = refs
     me = lax.axis_index("shard")
     seq = lax.axis_index("seq")
-    place = relative_place(count, me)
     tiles = count // 2
     low, f32 = ffn_own.dtype, jnp.float32
-    meet(count, place, seq)
-    ffn = Tree(count, ffn_own, ffn_all, ffn_send, ffn_recv, seq, place)
-    grad = Tree(count, grad_own, grad_all, grad_send, grad_recv, seq, place)
+    ffn = Line(count, ffn_own, ffn_all, ffn_send, ffn_recv, seq, 2)
+    grad = Line(count, grad_own, grad_all, grad_send, grad_recv, seq, 2)
+    ffn.meet()
     ffn.start(0)
     loads = [
         pltpu.make_async_copy(source, target, load.at[i])
@@ -514,14 +733,7 @@
     for copy in loads:
         copy.wait()
 
-    pair = me // 2
-
-    def tile_of(i):
-        total = 0
-        for bit in bit_list(tiles):
-            mine, other = lax.rem(pair // bit, 2), lax.rem(i // bit, 2)
-            total = total + bit * (mine + other - 2 * mine * other)
-        return total
+    tile_of = ffn.pair
 
     def put(number, slot, staged, target, tile):
         return pltpu.make_async_copy(staged.at[slot], target.at[tile], out_sem.at[number, slot])
@@ -531,16 +743,20 @@
             ffn_all.at[pl.ds(2 * tile, 2)], rows_out.at[pl.ds(2 * tile, 2)], rows_sem.at[tile]
         )
 
-    def arrivals(tree, i, extra):
-        for at, order in enumerate(tree.steps()):
+    def arrivals(way, i, extra):
+        done = 0
+        for at in range(tiles):
+            upto = way.order.index(2 * at) + 1 if at else 0
+            order = way.order[done:upto]
+            done = max(done, upto)
 
             @pl.when(i == at)
             def _(at=at, order=order):
                 for r in order:
-                    tree.arrive(r)
+                    way.arrive(r)
                 if at in extra:
                     extra[at]()
-                tree.copies[2 * at + 1].wait_recv()
+                way.wait_twin(2 * at)
 
     columns = gate_w.shape[1] // 2
 
@@ -652,7 +868,7 @@
             pltpu.VMEM((tiles, two, inner), jnp.float32),
         ]
         + [pltpu.VMEM((2, two, cols), low) for cols in staged]
-        + [pltpu.SemaphoreType.DMA((count,))] * 4
+        + [pltpu.SemaphoreType.DMA((2, count + 1))] * 4
         + [
             pltpu.SemaphoreType.DMA((3,)),
             pltpu.SemaphoreType.DMA((2,)),
@@ -722,13 +938,13 @@
     own_block = jnp.concatenate(
         [own_cols.reshape(weight_rows, 3 * local_width), own_gains], axis=1
     )
-    qkv_cols, full_out, tables_all = gather_blocks(
-        [own_block, weight_out, table], 1, ((0,), (1, 2))
-    )
+    qkv_cols, tables_all = gather_blocks([own_block, table], 1, ((0, 1),), (2, 1))
+    own_out, qkv_cols = lax.optimization_barrier((weight_out, qkv_cols))
+    full_out = lax.all_gather(own_out, "shard", axis=0, tiled=True)
+    qkv_all = qkv_cols
     qkv_cols = qkv_cols.reshape(width, 3 * local_width + GAIN_LANES)
     gain_cols = qkv_cols[:, 3 * local_width :][:, : norm_gains.shape[1]].astype(f32)
     qkv_cols = qkv_cols[:, : 3 * local_width]
-    full_out = full_out.reshape(width, width)
     group_in = lax.all_gather(layer_input[0], "seq", axis=0, tiled=True).astype(f32)
     pair_weight = lax.dynamic_index_in_dim(tables_all, shard_at, 1, keepdims=False)
 
@@ -786,7 +1002,7 @@
     gate_weight = weight_gate[0]
     up_weight = weight_up[0]
     down_weight = weight_down[0]
-    if experts <= 16:
+    if experts == LINE:
         tile_weight = pair_weight.reshape(experts // 2, 2 * tok_rows, 1)
         results = run_experts(
             ffn_in, out_cotangent[0], tile_weight, gate_weight, up_weight, down_weight, 2
@@ -796,7 +1012,9 @@
         )
     else:
         slot_weight = pair_weight.reshape(-1, 1)
-        (ffn_all, grad_all) = gather_blocks([ffn_in, out_cotangent[0]], 2, ((0,), (1,)))
+        (ffn_all, grad_all) = gather_blocks(
+            [ffn_in, out_cotangent[0]], 2, ((0,), (1,)), (1, 1)
+        )
         rows_in = ffn_all.reshape(-1, width)
         gate = jnp.dot(rows_in, gate_weight, preferred_element_type=f32)
         up = jnp.dot(rows_in, up_weight, preferred_element_type=f32)
@@ -822,8 +1040,7 @@
     out_part, d_ffn_in = lax.optimization_barrier((out_part, d_ffn_in))
     mixed_out = lax.psum_scatter(
         out_part, "shard", scatter_dimension=0, tiled=True
-    ).astype(f32)
-    layer_output = (resid + mixed_out).astype(low)
+    )
 
     grad_tokens = out_cotangent[0].astype(f32)
     d_scaled = d_ffn_in * gain_cols[:, 3]
@@ -857,54 +1074,75 @@
     dk_scaled = dk_rot * gain_k
     dots = jnp.stack([jnp.sum(dq_scaled * q_n, axis=-1), jnp.sum(dk_scaled * k_n, axis=-1)])
     dots = lax.psum(dots, "seq") / width
+    if pairs:
+        dots, gate_there = lax.optimization_barrier((dots, gate_there))
+        gate_came = lax.ppermute(gate_there, "seq", [(0, 1), (1, 0)])
     dq_raw = q_r * (dq_scaled - q_n * dots[0][:, None])
     dk_raw = k_r * (dk_scaled - k_n * dots[1][:, None])
     d_qkv = jnp.concatenate(
         [dq_raw.astype(low), dk_raw.astype(low), d_value.reshape(group_tok, local_width)], axis=1
     )
-    d_attn_in = seq_sum(contract_cols(d_qkv, qkv_cols).astype(low))
-    own_n = lax.dynamic_slice_in_dim(group_n, seq_at * tok_rows, tok_rows)
-    own_r = lax.dynamic_slice_in_dim(group_r, seq_at * tok_rows, tok_rows)
-    dx_scaled = d_attn_in * gain_cols[:, 0]
-    dx_norm = own_r * (dx_scaled - own_n * jnp.mean(dx_scaled * own_n, axis=-1, keepdims=True))
-    grad_g_attn = jnp.sum(d_attn_in * own_n, axis=0)
-    input_grad = (d_resid + dx_norm).astype(low)
-
     zeros = jnp.zeros((width,), f32)
-    gain_terms = jnp.stack(
-        [
-            grad_g_attn,
-            lax.dynamic_update_slice_in_dim(zeros, grad_g_q, seq_at * local_width, 0),
-            lax.dynamic_update_slice_in_dim(zeros, grad_g_k, seq_at * local_width, 0),
-            grad_g_ffn,
-        ],
-        axis=1,
-    )
-    gain_terms = jnp.pad(gain_terms, ((0, 0), (0, GAIN_LANES - gain_terms.shape[1])))
-    terms = [
-        contract_rows(attn_in, d_qkv[:, i * local_width : (i + 1) * local_width]) for i in range(3)
+    gain_rows = [
+        zeros,
+        lax.dynamic_update_slice_in_dim(zeros, grad_g_q, seq_at * local_width, 0),
+        lax.dynamic_update_slice_in_dim(zeros, grad_g_k, seq_at * local_width, 0),
+        grad_g_ffn,
     ]
-    terms += [contract_rows(mix_all, branch_cols), gain_terms]
-    terms = [term.astype(low).reshape(experts, weight_rows, -1) for term in terms]
-    sides = [gate_there, up_there] if pairs else []
-    results = scatter_sum(terms, 4, low, seq_count, sides=sides)
-    *sums, sum_gains = results[: len(terms)]
     if pairs:
-        gate_came, up_came = results[len(terms) :]
+        gain_terms = jnp.stack(gain_rows).reshape(len(gain_rows), experts, weight_rows)
+        gain_terms = jnp.pad(
+            jnp.swapaxes(gain_terms, 0, 1), ((0, 0), (0, ROW_TILE - len(gain_rows)), (0, 0))
+        )
+        work = AttentionGrads(
+            attn_in,
+            d_qkv,
+            mix_all,
+            branch_cols,
+            qkv_all,
+            layer_input[0],
+            d_resid,
+            gain_terms,
+            jnp.broadcast_to(gain_cols[:, 0], (8, width)),
+        )
+        *sums, sum_gains, up_came, input_grad = scatter_sum(
+            [], 4, low, seq_count, sides=[up_there], work=work
+        )
         sum_gate, sum_up, sum_down = (
             mine.astype(f32) + came.astype(f32)
             for mine, came in ((gate_mine, gate_came), (up_mine, up_came), (down_mine, down_came))
         )
+        rows_gain = jnp.sum(sum_gains[:, : norm_gains.shape[1]].astype(f32), axis=0).T
     else:
+        d_attn_in = seq_sum(contract_cols(d_qkv, qkv_cols).astype(low))
+        own_n = lax.dynamic_slice_in_dim(group_n, seq_at * tok_rows, tok_rows)
+        own_r = lax.dynamic_slice_in_dim(group_r, seq_at * tok_rows, tok_rows)
+        dx_scaled = d_attn_in * gain_cols[:, 0]
+        dx_norm = own_r * (
+            dx_scaled - own_n * jnp.mean(dx_scaled * own_n, axis=-1, keepdims=True)
+        )
+        gain_rows[0] = jnp.sum(d_attn_in * own_n, axis=0)
+        input_grad = (d_resid + dx_norm).astype(low)
+        gain_terms = jnp.stack(gain_rows, axis=1)
+        gain_terms = jnp.pad(gain_terms, ((0, 0), (0, GAIN_LANES - gain_terms.shape[1])))
+        terms = [
+            contract_rows(attn_in, d_qkv[:, i * local_width : (i + 1) * local_width])
+            for i in range(3)
+        ]
+        terms += [contract_rows(mix_all, branch_cols), gain_terms]
+        terms = [term.astype(low).reshape(experts, weight_rows, -1) for term in terms]
+        *sums, sum_gains = scatter_sum(terms, 4, low, seq_count)
         sum_down, sum_gate, sum_up = (
             lax.psum_scatter(
                 contract_rows(left, right).astype(low), "seq", scatter_dimension=0, tiled=True
             ).astype(f32)
             for left, right in products
         )
+        rows_gain = jnp.sum(sum_gains[:, :, : norm_gains.shape[1]].astype(f32), axis=0)
+    mixed_out, sums[0] = lax.optimization_barrier((mixed_out, sums[0]))
+    layer_output = (resid + mixed_out.astype(f32)).astype(low)
     targets = [(0, 0), (0, width), (0, 2 * width), (1, 0)]
     rows_qkv, rows_out = place_rows(sums, targets, (3 * width, width))
-    rows_gain = jnp.sum(sum_gains[:, :, : norm_gains.shape[1]].astype(f32), axis=0)
     return (
         layer_output[None],
         input_grad[None],

time: 631 us -> 596 us (0.945)
  Pallas kernels: 462 us -> 418 us
  waiting for transfers between devices: 5.82 us -> 31.9 us
  matrix products: 53.8 us -> 31 us
    pallas_call x1, Pallas kernels: 146 us -> 82.1 us  [gather_blocks(): pl.pallas_call(functools.partial(gather_kernel, count, groups, pieces), o...]
    all_gather x0 -> x1, waiting for transfers between devices: none -> 26.5 us  [shards(): full_out = lax.all_gather(own_out, 'shard', axis=0, tiled=True)]
    pallas_call x2, Pallas kernels: 198 us -> 216 us  [scatter_sum(): pl.pallas_call(functools.partial(scatter_kernel, count, seq_count, arrays...]
    dot_general x4 -> x0, matrix products: 14.8 us -> none  [contract_rows(): lax.dot_general(left_side, right_side, (((0,), (0,)), ((), ())), preferre...]
    dot_general x2 -> x1, matrix products: 15.3 us -> 6.6 us  [contract_cols(): lax.dot_general(left_side, right_side, (((1,), (1,)), ((), ())), preferre...]
  transfers between devices with their start and end apart: 7 -> 8, of which waited for: 2 -> 3; matrix products, arithmetic and copies ran while one was open for 14% -> 15% of each run, Pallas kernels for 74% -> 71%
where the time goes in v4:
time: 596 us; the launch traced here: 586 us
  Pallas kernels  418 us (70%)
  other arithmetic  40 us (7%)
  waiting for transfers between devices  31.9 us (5%)
  matrix products  31 us (5%)
  local copies, waits for them, and re-layouts  25.2 us (4%)
  between operations  14.7 us (2%)
  starting transfers between devices  14.4 us (2%)
  blocking collectives  10.6 us (2%)
    pallas_call x2, Pallas kernels, scatter_sum(): pl.pallas_call(functools.partial(scatter_kernel, count, seq_count, arrays...  216 us
    pallas_call x1, Pallas kernels, run_experts(): pl.pallas_call(functools.partial(expert_kernel, count), out_shape=outs, i...  116 us
    pallas_call x1, Pallas kernels, gather_blocks(): pl.pallas_call(functools.partial(gather_kernel, count, groups, pieces), o...  82.1 us
    all_gather x1, waiting for transfers between devices, shards(): full_out = lax.all_gather(own_out, 'shard', axis=0, tiled=True)  26.5 us
  transfers between devices with their start and end apart: 8, of which 3 were waited for; matrix products, arithmetic and copies ran while one was open for 15% of the time, Pallas kernels for 71%

profile of v4, /device:TPU:0, one launch (start us, length us, event | category | flops | bytes accessed | tf_op | source)
XLA Modules:
  0.0 585.6 jit_solution(9023228378896172045)
XLA Ops:
  7.2 0.7 all-gather.9.cloned.1.call-update
  8.0 0.8 copy.134
  8.8 1.9 copy.133
  11.4 0.6 select_reduce_fusion.refs_1_
  12.0 0.9 fusion.19.refs_0_
  12.9 82.1 %gather_blocks_1.1 = (bf16[16,128,3200]{2,1,0:T(8,128)(2,1)}, f32[16,16,128]{2,1,0:T(8,128)}) custom-call(bf16[128,3200]{1,0:T(8,128)(2,1)} %fusion.19.refs_0_, f32[16,128]{1,0:T(8,128)} %select_reduce_fusion.refs_1_), custom_call_target="tpu_custom_call" | custom-call | tf_op jit(solution)/shard_map/gather_blocks_1/pallas_call | solution.py:306
  95.4 1.1 slice.85
  96.8 0.6 constant_dynamic-slice_fusion
  97.6 0.7 fusion.29
  98.3 0.5 fusion.32
  98.9 1.5 fusion.3
  100.4 1.6 fusion.5.refs_1_
  102.0 6.8 %fusion.1 = f32[256,3072]{1,0:T(8,128)S(1)} fusion(bf16[256,2048]{1,0:T(8,128)(2,1)S(1)} %fusion.5.refs_1_, bf16[2048,3200]{1,0:T(8,128)(2,1)} %bitcast.145), kind=kOutput, calls=%fused_computation.1 | convolution fusion | flops 3221225472 | bytes 16777216 | tf_op jit(solution)/shard_map/dot_general | solution.py:972
  109.1 0.8 pad_maximum_fusion.4
  109.9 5.6 psum.14
  115.5 0.8 fusion.36
  116.3 0.9 multiply_bitcast_fusion.1
  118.3 2.1 subtract_convert_fusion.1
  120.5 4.0 fusion.44
  124.4 2.7 convolution_convert_fusion.2
  127.2 1.4 all_to_all.40
  128.6 0.9 copy.143
  129.5 3.6 all-to-all-start
  133.2 0.9 dynamic-slice_reduce_fusion
  134.0 1.8 reshape.329.refs_2_
  135.9 1.0 copy.170
  136.9 4.2 all-to-all-done
  141.2 26.5 %all-gather.5.cloned.1.call-done = bf16[2048,2048]{1,0:T(8,128)(2,1)} async-done(((bf16[128,2048]{1,0:T(8,128)(2,1)}), bf16[2048,2048]{1,0:T(8,128)(2,1)}) %all-gather.5.cloned.1.call-update) | async-done | bytes 8388624 | tf_op jit(solution)/shard_map/all_gather | solution.py:943
  167.7 4.7 multiply_reduce_fusion.5
  172.5 1.0 multiply_convert_fusion.3.refs_0_
  173.4 115.9 %run_experts.1 = (bf16[16,128,2048]{2,1,0:T(8,128)(2,1)}, bf16[8,256,1024]{2,1,0:T(8,128)(2,1)}, bf16[8,256,2048]{2,1,0:T(8,128)(2,1)}, bf16[8,256,2048]{2,1,0:T...) custom-call(bf16[128,2048]{1,0:T(8,128)(2,1)} %multiply_convert_fusi, ...), custom_call_target="tpu_custom_call" | custom-call | tf_op jit(solution)/shard_map/run_experts/pallas_call | solution.py:856
  289.4 69.6 %scatter_sum_3.1 = (f32[128,1024]{1,0:T(8,128)}, f32[128,1024]{1,0:T(8,128)}, bf16[512,2048]{1,0:T(8,128)(2,1)}, bf16[512,2048]{1,0:T(8,128)(2,1)}, bf16[1024,10...) custom-call(bf16[16,128,1024]{2,1,0:T(8,128)(2,1)} %bitcast.159, ...), custom_call_target="tpu_custom_call" | custom-call | tf_op jit(solution)/shard_map/scatter_sum_3/pallas_call | solution.py:661
  359.0 1.3 pad_maximum_fusion.1
  360.7 0.7 copy-done.6
  361.3 1.3 fusion.39
  362.6 6.6 %convolution_convert_fusion = bf16[128,2048]{1,0:T(8,128)(2,1)S(1)} fusion(bf16[128,2048]{1,0:T(8,128)(2,1)S(1)} %get-tuple-element.88, bf16[2048,2048]{1,0:T(8,128)(2,1)} %all-gather.5.cloned.1.call-done), kind=kOutput, calls=%fused_computation.9 | convolution fusion | flops 1074003968 | bytes 9437184 | tf_op jit(solution)/shard_map/dot_general | solution.py:65
  369.3 0.8 copy.211
  370.1 4.2 all-to-all-start.1
  374.3 5.5 add_bitcast_fusion
  379.8 0.8 copy.210
  381.0 4.4 all-to-all-start.2
  385.4 2.0 copy.183
  387.4 2.1 copy.156
  389.5 1.8 multiply_reduce_fusion
  391.7 0.7 copy-done.10
  392.5 0.7 fusion.13
  394.3 1.0 multiply_subtract_fusion.1
  395.4 0.8 copy-done.1
  396.2 1.0 fusion.15
  397.2 5.0 psum.15
  402.2 2.0 collective-permute-start
  404.2 3.1 convolution_convert_fusion.1
  407.3 2.1 copy.169
  409.4 0.7 pad.9.refs_8_
  410.1 3.2 multiply_convert_fusion.2
  413.3 1.2 pad_maximum_fusion.refs_2_
  414.6 0.6 broadcast_in_dim.112.refs_9_
  415.2 146.5 %scatter_sum_4.1 = (bf16[2,128,1024]{2,1,0:T(8,128)(2,1)}, bf16[2,128,1024]{2,1,0:T(8,128)(2,1)}, bf16[2,128,1024]{2,1,0:T(8,128)(2,1)}, bf16[2,128,1024]{2,1,0:...) custom-call(bf16[1024,1024]{1,0:T(8,128)(2,1)} %get-tuple-element.58.refs_0_, ...), custom_call_target="tpu_custom_call" | custom-call | tf_op jit(solution)/shard_map/scatter_sum_4/pallas_call | solution.py:661
  561.7 1.3 convert_reduce_fusion
  563.0 4.7 add_bitcast_fusion.1
  567.6 4.5 add_bitcast_fusion.2
  572.1 2.0 fusion.20
  574.1 3.7 place_rows.1
  577.9 0.8 copy.217
  (95 shorter events, 5.5 us)
Async XLA Ops:
  7.2 91.7 %all-gather.9.cloned.1.call-start = ((), (), s32[]{:S(2)}) async-start(), calls=%async_computation.7 | async-start | bytes 1572864 | tf_op jit(solution)/shard_map/all_gather | solution.py:948
  7.9 159.8 %all-gather.5.cloned.1.call-start = ((), (), s32[]{:S(2)}) async-start(), calls=%async_computation.4 | async-start | bytes 8912896 | tf_op jit(solution)/shard_map/all_gather | solution.py:943
  10.7 0.7 copy-start.23
  10.7 0.7 copy-start.24
  10.8 84.3 %copy-start.25 = (s32[1,3]{1,0:T(1,128)S(1)}, s32[1,3]{1,0:T(1,128)}, u32[]{:S(2)}) copy-start(s32[1,3]{1,0:T(1,128)} %param.13) | copy-start | bytes 40
  10.8 84.3 %copy-start.26 = (s32[1,3]{1,0:T(1,128)S(1)}, s32[1,3]{1,0:T(1,128)}, u32[]{:S(2)}) copy-start(s32[1,3]{1,0:T(1,128)} %param.14) | copy-start | bytes 40
  102.0 6.8 %copy-start.5 = (bf16[256,2048]{1,0:T(8,128)(2,1)}, bf16[256,2048]{1,0:T(8,128)(2,1)S(1)}, u32[]{:S(2)}) copy-start(bf16[256,2048]{1,0:T(8,128)(2,1)S(1)} %fusion.5.refs_1_) | copy-start | bytes 3145732
  108.9 15.6 %copy-start = (f32[256,3072]{1,0:T(8,128)}, f32[256,3072]{1,0:T(8,128)S(1)}, u32[]{:S(2)}) copy-start(f32[256,3072]{1,0:T(8,128)S(1)} %fusion.1) | copy-start | bytes 9437188
  116.3 1.0 copy-start.19
  116.3 1.0 copy-start.21
  127.2 8.7 %copy-start.12 = (bf16[8,128,256]{2,1,0:T(8,128)(2,1)S(1)}, bf16[8,128,256]{2,1,0:T(8,128)(2,1)}, u32[]{:S(2)}) copy-start(bf16[8,128,256]{2,1,0:T(8,128)(2,1)} %convolution_convert_fusion.2) | copy-start | bytes 1572868
  129.5 38.3 %copy-start.4 = (bf16[1,128,2048]{2,1,0:T(8,128)(2,1)S(1)}, bf16[1,128,2048]{2,1,0:T(8,128)(2,1)}, u32[]{:S(2)}) copy-start(bf16[1,128,2048]{2,1,0:T(8,128)(2,1)} %param.12) | copy-start | bytes 1572868
  129.5 11.7 %all-to-all-start = ((bf16[2,128,1024]{1,2,0:T(8,128)(2,1)}), bf16[2,128,1024]{1,2,0:T(8,128)(2,1)S(1)}, u32[]{:S(2)}, u32[]{:S(2)}) async-start(bf16[2,128,1024]{1,2,0:T(8,128)(2,1)} %copy.143), calls=%async_computation | async-start | bytes 1048576 | tf_op jit(solution)/shard_map/all_to_all | solution.py:994
  133.1 281.5 %all-gather.7.cloned.1.call-start = ((), (), s32[]{:S(2)}) async-start(), calls=%async_computation.6 | async-start | bytes 1572864 | tf_op jit(solution)/shard_map/all_gather | solution.py:995
  136.9 435.2 %reduce-scatter.2.cloned.1.call-start = ((), (), s32[]{:S(2)}) async-start(), calls=%async_computation.5 | async-start | bytes 8912896 | tf_op jit(solution)/shard_map/reduce_scatter | solution.py:1041
  360.3 1.0 copy-start.6
  370.1 10.9 %all-to-all-start.1 = ((bf16[128,2,1024]{2,0,1:T(8,128)(2,1)}), bf16[128,2,1024]{2,0,1:T(8,128)(2,1)}, u32[]{:S(2)}, u32[]{:S(2)}) async-start(bf16[128,2,1024]{2,0,1:T(8,128)(2,1)} %bitcast.143), calls=%async_computation.2 | async-start | bytes 1048576 | tf_op jit(solution)/shard_map/all_to_all | solution.py:1053
  380.6 8.8 %copy-start.7 = (f32[8,256,256]{1,2,0:T(8,128)S(1)}, f32[8,256,256]{1,2,0:T(8,128)}, u32[]{:S(2)}) copy-start(f32[8,256,256]{1,2,0:T(8,128)} %get-tuple-element.122) | copy-start | bytes 6291460
  381.0 33.6 %all-to-all-start.2 = ((bf16[128,2,1024]{2,0,1:T(8,128)(2,1)}), bf16[128,2,1024]{2,0,1:T(8,128)(2,1)}, u32[]{:S(2)}, u32[]{:S(2)}) async-start(bf16[128,2,1024]{2,0,1:T(8,128)(2,1)} %bitcast.166), calls=%async_computation.3 | async-start | bytes 1048576 | tf_op jit(solution)/shard_map/all_to_all | solution.py:1056
  391.3 1.1 copy-start.10
  391.3 1.3 copy-start.11
  392.5 1.0 copy-start.8
  392.5 1.2 copy-start.9
  394.3 1.9 copy-start.1
  394.3 1.9 copy-start.17
  394.3 1.9 copy-start.18
  394.3 1.9 copy-start.20
  394.3 1.9 copy-start.22
  395.3 1.8 copy-start.2
  395.4 1.8 copy-start.3
  402.2 165.5 %collective-permute-start = (bf16[1024,1024]{1,0:T(8,128)(2,1)}, bf16[1024,1024]{1,0:T(8,128)(2,1)}, u32[]{:S(2)}, u32[]{:S(2)}) collective-permute-start(bf16[1024,1024]{1,0:T(8,128)(2,1)} %get-tuple-element.73), channel_id=1, source_target_pairs={{0,16},{16,0},{1,17},{17,1},{2,18},{18,2},{3,19},{19,3},{4,20},{20... | collective-permute-start | bytes 6291464 | tf_op jit(solution)/shard_map/ppermute | solution.py:1079
  410.1 3.2 copy-start.13
  415.2 147.7 %copy-start.15 = (bf16[1024,1024]{1,0:T(8,128)(2,1)S(1)}, bf16[1024,1024]{1,0:T(8,128)(2,1)}, u32[]{:S(2)}) copy-start(bf16[1024,1024]{1,0:T(8,128)(2,1)} %get-tuple-element.74) | copy-start | bytes 6291460
  563.0 4.7 copy-start.14
  572.1 5.7 copy-start.16
Sparse Core Ops, SparseCore 0:
  9.5 23.9 all-gather.8
  95.2 72.5 all-gather.4
  169.3 19.8 all-gather.6
  360.4 123.8 reduce-scatter.1

commit v5 on v4

--- a/solution.py
+++ b/solution.py
@@ -70,7 +70,6 @@
 MESH_ID = pl.DeviceIdType.MESH
 VMEM_LIMIT = 60 * 1024 * 1024
 ROW_TILE = 16
-AHEAD = 2
 GRAD_TILE = 256
 
 
@@ -404,10 +403,10 @@
             start(a, r, parts[a].at[place(r)])
 
     tasks = work.tasks(seq, me, work_in, work_out, refs[6:], start_sides)
-    lead = AHEAD if work.part_shapes else len(chunks)
+    lead = work.ahead if work.part_shapes else len(chunks)
     for a, u in chunks[:lead]:
         prepare(a, u)
-    steps = len(chunks) + AHEAD
+    steps = len(chunks) + work.ahead
     for i in range(steps):
         if i + lead < len(chunks):
             prepare(*chunks[i + lead])
@@ -415,8 +414,8 @@
             a, u = chunks[i]
             fold(a, 4 * u + 2, 1)
             fold(a, 4 * u, 1)
-        if i >= AHEAD:
-            a, u = chunks[i - AHEAD]
+        if i >= work.ahead:
+            a, u = chunks[i - work.ahead]
             for bit in bits[1:]:
                 if 4 * u % (2 * bit) == 0:
                     fold(a, 4 * u, bit)
@@ -432,6 +431,7 @@
 class NoWork:
     inputs = outputs = 0
     operands, results, scratch, part_shapes, order = (), (), (), (), ()
+    ahead = 2
 
     def fill(self, parts, a, base):
         pass
@@ -539,10 +539,11 @@
         self.local = d_qkv.shape[1] // 3
         self.part_shapes = [
             jax.ShapeDtypeStruct((blocks, rows, cols), low)
-            for cols in (self.local, self.local, self.local, branch.shape[1])
+            for cols in 3 * (self.local,) + 2 * (branch.shape[1] // 2,)
         ]
         self.part_shapes.append(jax.ShapeDtypeStruct(gains.shape, low))
-        self.order = (0, 1, 2, 4, 3)
+        self.order = (3, 0, 1, 2, 5, 4)
+        self.ahead = 4
         self.results = [jax.ShapeDtypeStruct(tokens.shape, low)]
         self.scratch = [pltpu.VMEM(a.shape, a.dtype) for a in self.operands]
         self.scratch += [
@@ -562,13 +563,13 @@
 
     def fill(self, parts, a, base):
         part = parts[a]
-        if a == 4:
+        if a == 5:
             part[pl.ds(base, 4)] = self.here[7][pl.ds(base, 4)].astype(part.dtype)
             return
-        left, right = (2, 3) if a == 3 else (0, 1)
+        left, right = (2, 3) if a >= 3 else (0, 1)
         self.need(left, right)
         rows, cols = part.shape[1:]
-        first = 0 if a == 3 else a * self.local
+        first = (a - 3 if a >= 3 else a) * cols
 
         def step(i, carry):
             at = pl.ds(pl.multiple_of((base + i) * rows, rows), rows)
@@ -640,8 +641,8 @@
         return found + [send, norm_back]
 
     def at_step(self, tasks, i, steps):
-        parts = len(self.part_shapes) - 1
-        last = 3 * (steps - AHEAD) // (parts + 1) - AHEAD - 1
+        rounds = (steps - self.ahead) // len(self.order)
+        last = rounds * self.order.index(5) - self.ahead - 1
         if i < len(tasks) - 2:
             return [tasks[i]] + ([tasks[-2]] if i == len(tasks) - 3 else [])
         return [tasks[-1]] if i == last else []
@@ -689,7 +690,8 @@
         out_ref, base = refs[len(refs_in) + o[0]], o[1]
         cols = refs[i].shape[2]
         for s in range(seq_count):
-            out_ref[:, base + s * cols : base + (s + 1) * cols] = refs[i][s].astype(out_ref.dtype)
+            at = base + s * o[2]
+            out_ref[:, at : at + cols] = refs[i][s].astype(out_ref.dtype)
 
 
 def place_rows(pieces, targets, out_cols):
@@ -706,10 +708,10 @@
 def expert_kernel(count, *refs):
     (ffn_own, grad_own, weight), refs = refs[:3], refs[3:]
     matrices, refs = refs[:3], refs[3:]
-    (rows_out, hidden_out, mixed_out, expert_out, gate_out, up_out), refs = refs[:6], refs[6:]
+    (rows_out, grad_out, hidden_out, mixed_out, gate_out, up_out), refs = refs[:6], refs[6:]
     pair_out, refs = refs[:2], refs[2:]
-    (ffn_all, grad_all, gate_w, up_w, down_w, gate_all, up_all), refs = refs[:7], refs[7:]
-    (hidden_at, mixed_at, expert_at, gate_at, up_at, left_at, right_at), refs = refs[:7], refs[7:]
+    (ffn_all, grad_all, both_w, down_w, gate_by, up_by), refs = refs[:6], refs[6:]
+    (hidden_at, mixed_at, both_at, left_at, right_at), refs = refs[:5], refs[5:]
     ffn_send, ffn_recv, grad_send, grad_recv, load, own_sem, rows_sem, out_sem = refs
     me = lax.axis_index("shard")
     seq = lax.axis_index("seq")
@@ -719,9 +721,12 @@
     grad = Line(count, grad_own, grad_all, grad_send, grad_recv, seq, 2)
     ffn.meet()
     ffn.start(0)
+    inner = down_w.shape[0]
+    gate_span, up_span = slice(0, inner), slice(inner, 2 * inner)
+    places = (both_w.at[:, gate_span], both_w.at[:, up_span], down_w)
     loads = [
         pltpu.make_async_copy(source, target, load.at[i])
-        for i, (source, target) in enumerate(zip(matrices, (gate_w, up_w, down_w)))
+        for i, (source, target) in enumerate(zip(matrices, places))
     ]
     for copy in loads:
         copy.start()
@@ -738,10 +743,9 @@
     def put(number, slot, staged, target, tile):
         return pltpu.make_async_copy(staged.at[slot], target.at[tile], out_sem.at[number, slot])
 
-    def keep_rows(tile):
-        return pltpu.make_async_copy(
-            ffn_all.at[pl.ds(2 * tile, 2)], rows_out.at[pl.ds(2 * tile, 2)], rows_sem.at[tile]
-        )
+    def keep_rows(number, rows, target, tile):
+        at = pl.ds(2 * tile, 2)
+        return pltpu.make_async_copy(rows.at[at], target.at[at], rows_sem.at[number, tile])
 
     def arrivals(way, i, extra):
         done = 0
@@ -758,13 +762,16 @@
                     extra[at]()
                 way.wait_twin(2 * at)
 
-    columns = gate_w.shape[1] // 2
+    columns = inner // 2
+
+    def beyond(at):
+        return slice(inner + at.start, inner + at.stop)
 
     def forward(i, carry):
         arrivals(ffn, i, {tiles - 3: lambda: grad.start(0)})
         tile = tile_of(i)
         slot = lax.rem(i, 2)
-        keep_rows(tile).start()
+        keep_rows(0, ffn_all, rows_out, tile).start()
 
         @pl.when(i >= 2)
         def _():
@@ -774,17 +781,20 @@
         rows = ffn_all[pl.ds(2 * tile, 2)].reshape(-1, ffn_all.shape[2])
         for c in range(2):
             at = slice(c * columns, (c + 1) * columns)
-            gate = jnp.dot(rows, gate_w[:, at], preferred_element_type=f32)
-            up = jnp.dot(rows, up_w[:, at], preferred_element_type=f32)
-            gate_all[i, :, at] = gate
-            up_all[i, :, at] = up
-            hidden_at[slot, :, at] = (gate * jax.nn.sigmoid(gate) * up).astype(low)
+            gate = jnp.dot(rows, both_w[:, at], preferred_element_type=f32)
+            up = jnp.dot(rows, both_w[:, beyond(at)], preferred_element_type=f32)
+            sigma = jax.nn.sigmoid(gate)
+            weighted = weight[tile] * sigma
+            silu = weighted * gate
+            hidden_at[slot, :, at] = (silu * up).astype(low)
+            gate_by[i, :, at] = up * (weighted + silu * (1.0 - sigma))
+            up_by[i, :, at] = silu
         put(0, slot, hidden_at, hidden_out, tile).start()
         half = down_w.shape[1] // 2
         for c in range(2):
             at = slice(c * half, (c + 1) * half)
             result = jnp.dot(hidden_at[slot], down_w[:, at], preferred_element_type=f32)
-            mixed_at[slot, :, at] = (result.astype(low).astype(f32) * weight[tile]).astype(low)
+            mixed_at[slot, :, at] = result.astype(low)
         put(1, slot, mixed_at, mixed_out, tile).start()
         return carry
 
@@ -796,47 +806,42 @@
         tile = tile_of(i)
         slot = lax.rem(i, 2)
 
+        keep_rows(1, grad_all, grad_out, tile).start()
+
         @pl.when(i >= 2)
         def _():
             before = tile_of(i - 2)
-            put(2, slot, expert_at, expert_out, before).wait()
-            put(3, slot, gate_at, gate_out, before).wait()
-            put(4, slot, up_at, up_out, before).wait()
-            put(5, slot, left_at, pair_out[0], before).wait()
-            put(6, slot, right_at, pair_out[1], before).wait()
+            put(2, slot, both_at.at[:, :, gate_span], gate_out, before).wait()
+            put(3, slot, both_at.at[:, :, up_span], up_out, before).wait()
+            put(4, slot, left_at, pair_out[0], before).wait()
+            put(5, slot, right_at, pair_out[1], before).wait()
 
         rows = grad_all[pl.ds(2 * tile, 2)].reshape(-1, grad_all.shape[2])
-        expert_at[slot] = (rows.astype(f32) * weight[tile]).astype(low)
-        put(2, slot, expert_at, expert_out, tile).start()
         for c in range(2):
             at = slice(c * columns, (c + 1) * columns)
-            d_hidden = contract_cols(expert_at[slot], down_w[at, :])
-            gate, up = gate_all[i, :, at], up_all[i, :, at]
-            sigma = jax.nn.sigmoid(gate)
-            gate_at[slot, :, at] = (
-                d_hidden * up * sigma * (1.0 + gate * (1.0 - sigma))
-            ).astype(low)
-            up_at[slot, :, at] = (d_hidden * (gate * sigma)).astype(low)
-        put(3, slot, gate_at, gate_out, tile).start()
-        put(4, slot, up_at, up_out, tile).start()
-        half = gate_w.shape[0] // 2
+            d_hidden = contract_cols(rows, down_w[at, :])
+            both_at[slot, :, at] = (d_hidden * gate_by[i, :, at]).astype(low)
+            both_at[slot, :, beyond(at)] = (d_hidden * up_by[i, :, at]).astype(low)
+        put(2, slot, both_at.at[:, :, gate_span], gate_out, tile).start()
+        put(3, slot, both_at.at[:, :, up_span], up_out, tile).start()
+        half = both_w.shape[0] // 2
         for c, staged in enumerate((left_at, right_at)):
             at = slice(c * half, (c + 1) * half)
-            staged[slot] = (
-                contract_cols(gate_at[slot], gate_w[at, :]) + contract_cols(up_at[slot], up_w[at, :])
-            ).astype(low)
-            put(5 + c, slot, staged, pair_out[c], tile).start()
+            staged[slot] = contract_cols(both_at[slot], both_w[at, :]).astype(low)
+            put(4 + c, slot, staged, pair_out[c], tile).start()
         return carry
 
     lax.fori_loop(0, tiles, backward, 0)
     ffn.finish()
     grad.finish()
     for i in range(tiles):
-        keep_rows(i).wait()
-    outs = (hidden_out, mixed_out, expert_out, gate_out, up_out, pair_out[0], pair_out[1])
-    staged = (hidden_at, mixed_at, expert_at, gate_at, up_at, left_at, right_at)
+        keep_rows(0, ffn_all, rows_out, i).wait()
+        keep_rows(1, grad_all, grad_out, i).wait()
+    outs = (hidden_out, mixed_out, gate_out, up_out, pair_out[0], pair_out[1])
+    parts = (both_at.at[:, :, gate_span], both_at.at[:, :, up_span])
+    staged = (hidden_at, mixed_at) + parts + (left_at, right_at)
     for i in (tiles - 2, tiles - 1):
-        for number in range(7):
+        for number in range(len(outs)):
             put(number, i % 2, staged[number], outs[number], tile_of(i)).wait()
 
 
@@ -848,11 +853,11 @@
     low = ffn_in.dtype
     shape = jax.ShapeDtypeStruct
     wide, narrow = (tiles, two, width), (tiles, two, inner)
-    outs = [shape((count, rows, width), low)]
-    outs += [shape(s, low) for s in (narrow, wide, wide, narrow, narrow)]
+    outs = [shape((count, rows, width), low)] * 2
+    outs += [shape(s, low) for s in (narrow, wide, narrow, narrow)]
     outs += [shape((tiles, two, width // 2), low)] * 2
     vmem, hbm = pl.BlockSpec(memory_space=pltpu.VMEM), pl.BlockSpec(memory_space=pl.ANY)
-    staged = [inner, width, width, inner, inner, width // 2, width // 2]
+    staged = [inner, width, 2 * inner, width // 2, width // 2]
     return pl.pallas_call(
         functools.partial(expert_kernel, count),
         out_shape=outs,
@@ -861,8 +866,7 @@
         scratch_shapes=[
             pltpu.VMEM((count, rows, width), low),
             pltpu.VMEM((count, rows, width), low),
-            pltpu.VMEM(gate_w.shape, low),
-            pltpu.VMEM(up_w.shape, low),
+            pltpu.VMEM((width, 2 * inner), low),
             pltpu.VMEM(down_w.shape, low),
             pltpu.VMEM((tiles, two, inner), jnp.float32),
             pltpu.VMEM((tiles, two, inner), jnp.float32),
@@ -872,8 +876,8 @@
         + [
             pltpu.SemaphoreType.DMA((3,)),
             pltpu.SemaphoreType.DMA((2,)),
-            pltpu.SemaphoreType.DMA((tiles,)),
-            pltpu.SemaphoreType.DMA((len(staged), 2)),
+            pltpu.SemaphoreType.DMA((2, tiles)),
+            pltpu.SemaphoreType.DMA((len(staged) + 1, 2)),
         ],
         compiler_params=pltpu.CompilerParams(
             collective_id=collective_id, has_side_effects=True, vmem_limit_bytes=VMEM_LIMIT
@@ -1007,7 +1011,7 @@
         results = run_experts(
             ffn_in, out_cotangent[0], tile_weight, gate_weight, up_weight, down_weight, 2
         )
-        rows_in, hidden, out_part, d_expert, d_gate, d_up, *halves = (
+        rows_in, d_expert, hidden, out_part, d_gate, d_up, *halves = (
             result.reshape(experts * tok_rows, -1) for result in results
         )
     else:
@@ -1141,7 +1145,8 @@
         rows_gain = jnp.sum(sum_gains[:, :, : norm_gains.shape[1]].astype(f32), axis=0)
     mixed_out, sums[0] = lax.optimization_barrier((mixed_out, sums[0]))
     layer_output = (resid + mixed_out.astype(f32)).astype(low)
-    targets = [(0, 0), (0, width), (0, 2 * width), (1, 0)]
+    targets = [(0, i * width, local_width) for i in range(3)]
+    targets += [(1, i * sums[3].shape[2], out_cols) for i in range(len(sums) - 3)]
     rows_qkv, rows_out = place_rows(sums, targets, (3 * width, width))
     return (
         layer_output[None],

time: 596 us -> 586 us (0.983)
  Pallas kernels: 418 us -> 407 us
    pallas_call x2, Pallas kernels: 216 us -> 207 us  [scatter_sum(): pl.pallas_call(functools.partial(scatter_kernel, count, seq_count, arrays...]
  transfers between devices with their start and end apart: 8 -> 8, of which waited for: 3 -> 3; matrix products, arithmetic and copies ran while one was open for 15% -> 15% of each run, Pallas kernels for 71% -> 70%
where the time goes in v5:
time: 586 us; the launch traced here: 575 us
  Pallas kernels  407 us (69%)
  other arithmetic  40 us (7%)
  waiting for transfers between devices  31.9 us (5%)
  matrix products  31 us (5%)
  local copies, waits for them, and re-layouts  25.3 us (4%)
  between operations  14.7 us (3%)
  starting transfers between devices  14.3 us (2%)
  blocking collectives  10.6 us (2%)
    pallas_call x2, Pallas kernels, scatter_sum(): pl.pallas_call(functools.partial(scatter_kernel, count, seq_count, arrays...  207 us
    pallas_call x1, Pallas kernels, run_experts(): pl.pallas_call(functools.partial(expert_kernel, count), out_shape=outs, i...  114 us
    pallas_call x1, Pallas kernels, gather_blocks(): pl.pallas_call(functools.partial(gather_kernel, count, groups, pieces), o...  82.1 us
    all_gather x1, waiting for transfers between devices, shards(): full_out = lax.all_gather(own_out, 'shard', axis=0, tiled=True)  26.5 us
  transfers between devices with their start and end apart: 8, of which 3 were waited for; matrix products, arithmetic and copies ran while one was open for 15% of the time, Pallas kernels for 70%

profile of v5, /device:TPU:0, one launch (start us, length us, event | category | flops | bytes accessed | tf_op | source)
XLA Modules:
  0.0 574.6 jit_solution(2522688462284808952)
XLA Ops:
  7.2 0.7 all-gather.9.cloned.1.call-update
  8.0 0.8 copy.134
  8.8 1.9 copy.133
  11.4 0.6 select_reduce_fusion.refs_1_
  12.0 0.9 fusion.19.refs_0_
  12.9 82.1 %gather_blocks_1.1 = (bf16[16,128,3200]{2,1,0:T(8,128)(2,1)}, f32[16,16,128]{2,1,0:T(8,128)}) custom-call(bf16[128,3200]{1,0:T(8,128)(2,1)} %fusion.19.refs_0_, f32[16,128]{1,0:T(8,128)} %select_reduce_fusion.refs_1_), custom_call_target="tpu_custom_call" | custom-call | tf_op jit(solution)/shard_map/gather_blocks_1/pallas_call | solution.py:305
  95.4 1.1 slice.85
  96.8 0.6 constant_dynamic-slice_fusion
  97.6 0.7 fusion.29
  98.3 0.5 fusion.32
  98.9 1.5 fusion.3
  100.4 1.6 fusion.5.refs_1_
  102.0 6.8 %fusion.1 = f32[256,3072]{1,0:T(8,128)S(1)} fusion(bf16[256,2048]{1,0:T(8,128)(2,1)S(1)} %fusion.5.refs_1_, bf16[2048,3200]{1,0:T(8,128)(2,1)} %bitcast.145), kind=kOutput, calls=%fused_computation.1 | convolution fusion | flops 3221225472 | bytes 16777216 | tf_op jit(solution)/shard_map/dot_general | solution.py:976
  109.1 0.8 pad_maximum_fusion.4
  109.9 5.6 psum.14
  115.5 0.8 fusion.36
  116.3 0.9 multiply_bitcast_fusion.1
  118.3 2.1 subtract_convert_fusion.1
  120.5 4.0 fusion.44
  124.4 2.7 convolution_convert_fusion.2
  127.2 1.4 all_to_all.40
  128.6 0.9 copy.143
  129.5 3.6 all-to-all-start
  133.2 0.9 dynamic-slice_reduce_fusion
  134.0 1.8 reshape.329.refs_2_
  135.9 1.0 copy.170
  136.9 4.2 all-to-all-done
  141.2 26.5 %all-gather.5.cloned.1.call-done = bf16[2048,2048]{1,0:T(8,128)(2,1)} async-done(((bf16[128,2048]{1,0:T(8,128)(2,1)}), bf16[2048,2048]{1,0:T(8,128)(2,1)}) %all-gather.5.cloned.1.call-update) | async-done | bytes 8388624 | tf_op jit(solution)/shard_map/all_gather | solution.py:947
  167.7 4.7 multiply_reduce_fusion.5
  172.5 1.0 multiply_convert_fusion.3.refs_0_
  173.4 114.2 %run_experts.1 = (bf16[16,128,2048]{2,1,0:T(8,128)(2,1)}, bf16[16,128,2048]{2,1,0:T(8,128)(2,1)}, bf16[8,256,1024]{2,1,0:T(8,128)(2,1)}, bf16[8,256,2048]{2,1,0:...) custom-call(bf16[128,2048]{1,0:T(8,128)(2,1)} %multiply_convert_fusi, ...), custom_call_target="tpu_custom_call" | custom-call | tf_op jit(solution)/shard_map/run_experts/pallas_call | solution.py:861
  287.7 69.4 %scatter_sum_3.1 = (f32[128,1024]{1,0:T(8,128)}, f32[128,1024]{1,0:T(8,128)}, bf16[512,2048]{1,0:T(8,128)(2,1)}, bf16[512,2048]{1,0:T(8,128)(2,1)}, bf16[1024,10...) custom-call(bf16[16,128,1024]{2,1,0:T(8,128)(2,1)} %bitcast.159, ...), custom_call_target="tpu_custom_call" | custom-call | tf_op jit(solution)/shard_map/scatter_sum_3/pallas_call | solution.py:662
  357.1 1.3 pad_maximum_fusion.1
  358.7 0.7 copy-done.6
  359.4 1.3 fusion.39
  360.7 6.6 %convolution_convert_fusion = bf16[128,2048]{1,0:T(8,128)(2,1)S(1)} fusion(bf16[128,2048]{1,0:T(8,128)(2,1)S(1)} %get-tuple-element.90, bf16[2048,2048]{1,0:T(8,128)(2,1)} %all-gather.5.cloned.1.call-done), kind=kOutput, calls=%fused_computation.9 | convolution fusion | flops 1074003968 | bytes 9437184 | tf_op jit(solution)/shard_map/dot_general | solution.py:65
  367.3 0.8 copy.211
  368.2 4.2 all-to-all-start.1
  372.4 5.5 add_bitcast_fusion
  377.9 0.8 copy.210
  379.1 4.4 all-to-all-start.2
  383.4 2.0 copy.183
  385.4 2.1 copy.156
  387.6 1.8 multiply_reduce_fusion
  389.7 0.7 copy-done.10
  390.6 0.7 fusion.13
  392.4 1.0 multiply_subtract_fusion.1
  393.5 0.8 copy-done.1
  394.3 1.0 fusion.15
  395.3 5.0 psum.15
  400.3 2.0 collective-permute-start
  402.3 3.1 convolution_convert_fusion.1
  405.3 2.1 copy.169
  407.5 0.7 pad.9.refs_8_
  408.2 3.2 multiply_convert_fusion.2
  411.4 1.2 pad_maximum_fusion.refs_2_
  412.7 0.6 broadcast_in_dim.112.refs_9_
  413.3 137.3 %scatter_sum_4.1 = (bf16[2,128,1024]{2,1,0:T(8,128)(2,1)}, bf16[2,128,1024]{2,1,0:T(8,128)(2,1)}, bf16[2,128,1024]{2,1,0:T(8,128)(2,1)}, bf16[2,128,512]{2,1,0:T...) custom-call(bf16[1024,1024]{1,0:T(8,128)(2,1)} %get-tuple-element.59, ...), custom_call_target="tpu_custom_call" | custom-call | tf_op jit(solution)/shard_map/scatter_sum_4/pallas_call | solution.py:662
  550.7 1.3 convert_reduce_fusion
  551.9 4.7 add_bitcast_fusion.1
  556.6 4.5 add_bitcast_fusion.2
  561.1 2.0 fusion.20
  563.1 3.7 place_rows.1
  566.8 0.8 copy.217
  (95 shorter events, 5.5 us)
Async XLA Ops:
  7.2 91.7 %all-gather.9.cloned.1.call-start = ((), (), s32[]{:S(2)}) async-start(), calls=%async_computation.7 | async-start | bytes 1572864 | tf_op jit(solution)/shard_map/all_gather | solution.py:952
  7.9 159.8 %all-gather.5.cloned.1.call-start = ((), (), s32[]{:S(2)}) async-start(), calls=%async_computation.4 | async-start | bytes 8912896 | tf_op jit(solution)/shard_map/all_gather | solution.py:947
  10.7 0.7 copy-start.23
  10.7 0.7 copy-start.24
  10.8 84.3 %copy-start.25 = (s32[1,3]{1,0:T(1,128)S(1)}, s32[1,3]{1,0:T(1,128)}, u32[]{:S(2)}) copy-start(s32[1,3]{1,0:T(1,128)} %param.13) | copy-start | bytes 40
  10.8 84.3 %copy-start.26 = (s32[1,3]{1,0:T(1,128)S(1)}, s32[1,3]{1,0:T(1,128)}, u32[]{:S(2)}) copy-start(s32[1,3]{1,0:T(1,128)} %param.14) | copy-start | bytes 40
  102.0 6.8 %copy-start.5 = (bf16[256,2048]{1,0:T(8,128)(2,1)}, bf16[256,2048]{1,0:T(8,128)(2,1)S(1)}, u32[]{:S(2)}) copy-start(bf16[256,2048]{1,0:T(8,128)(2,1)S(1)} %fusion.5.refs_1_) | copy-start | bytes 3145732
  108.9 15.6 %copy-start = (f32[256,3072]{1,0:T(8,128)}, f32[256,3072]{1,0:T(8,128)S(1)}, u32[]{:S(2)}) copy-start(f32[256,3072]{1,0:T(8,128)S(1)} %fusion.1) | copy-start | bytes 9437188
  116.3 1.0 copy-start.19
  116.3 1.0 copy-start.21
  127.2 8.7 %copy-start.12 = (bf16[8,128,256]{2,1,0:T(8,128)(2,1)S(1)}, bf16[8,128,256]{2,1,0:T(8,128)(2,1)}, u32[]{:S(2)}) copy-start(bf16[8,128,256]{2,1,0:T(8,128)(2,1)} %convolution_convert_fusion.2) | copy-start | bytes 1572868
  129.5 38.3 %copy-start.4 = (bf16[1,128,2048]{2,1,0:T(8,128)(2,1)S(1)}, bf16[1,128,2048]{2,1,0:T(8,128)(2,1)}, u32[]{:S(2)}) copy-start(bf16[1,128,2048]{2,1,0:T(8,128)(2,1)} %param.12) | copy-start | bytes 1572868
  129.5 11.7 %all-to-all-start = ((bf16[2,128,1024]{1,2,0:T(8,128)(2,1)}), bf16[2,128,1024]{1,2,0:T(8,128)(2,1)S(1)}, u32[]{:S(2)}, u32[]{:S(2)}) async-start(bf16[2,128,1024]{1,2,0:T(8,128)(2,1)} %copy.143), calls=%async_computation | async-start | bytes 1048576 | tf_op jit(solution)/shard_map/all_to_all | solution.py:998
  133.1 279.6 %all-gather.7.cloned.1.call-start = ((), (), s32[]{:S(2)}) async-start(), calls=%async_computation.6 | async-start | bytes 1572864 | tf_op jit(solution)/shard_map/all_gather | solution.py:999
  136.9 424.2 %reduce-scatter.2.cloned.1.call-start = ((), (), s32[]{:S(2)}) async-start(), calls=%async_computation.5 | async-start | bytes 8912896 | tf_op jit(solution)/shard_map/reduce_scatter | solution.py:1045
  358.4 1.0 copy-start.6
  368.2 10.9 %all-to-all-start.1 = ((bf16[128,2,1024]{2,0,1:T(8,128)(2,1)}), bf16[128,2,1024]{2,0,1:T(8,128)(2,1)}, u32[]{:S(2)}, u32[]{:S(2)}) async-start(bf16[128,2,1024]{2,0,1:T(8,128)(2,1)} %bitcast.143), calls=%async_computation.2 | async-start | bytes 1048576 | tf_op jit(solution)/shard_map/all_to_all | solution.py:1057
  378.7 8.8 %copy-start.7 = (f32[8,256,256]{1,2,0:T(8,128)S(1)}, f32[8,256,256]{1,2,0:T(8,128)}, u32[]{:S(2)}) copy-start(f32[8,256,256]{1,2,0:T(8,128)} %get-tuple-element.124) | copy-start | bytes 6291460
  379.1 33.6 %all-to-all-start.2 = ((bf16[128,2,1024]{2,0,1:T(8,128)(2,1)}), bf16[128,2,1024]{2,0,1:T(8,128)(2,1)}, u32[]{:S(2)}, u32[]{:S(2)}) async-start(bf16[128,2,1024]{2,0,1:T(8,128)(2,1)} %bitcast.166), calls=%async_computation.3 | async-start | bytes 1048576 | tf_op jit(solution)/shard_map/all_to_all | solution.py:1060
  389.3 1.1 copy-start.10
  389.4 1.3 copy-start.11
  390.6 1.0 copy-start.8
  390.6 1.2 copy-start.9
  392.4 1.9 copy-start.1
  392.4 1.9 copy-start.17
  392.4 1.9 copy-start.18
  392.4 1.9 copy-start.20
  392.4 1.9 copy-start.22
  393.5 1.8 copy-start.2
  393.5 1.8 copy-start.3
  400.3 156.3 %collective-permute-start = (bf16[1024,1024]{1,0:T(8,128)(2,1)}, bf16[1024,1024]{1,0:T(8,128)(2,1)}, u32[]{:S(2)}, u32[]{:S(2)}) collective-permute-start(bf16[1024,1024]{1,0:T(8,128)(2,1)} %get-tuple-element.75), channel_id=1, source_target_pairs={{0,16},{16,0},{1,17},{17,1},{2,18},{18,2},{3,19},{19,3},{4,20},{20... | collective-permute-start | bytes 6291464 | tf_op jit(solution)/shard_map/ppermute | solution.py:1083
  408.2 3.2 copy-start.13
  413.3 138.6 %copy-start.15 = (bf16[1024,1024]{1,0:T(8,128)(2,1)S(1)}, bf16[1024,1024]{1,0:T(8,128)(2,1)}, u32[]{:S(2)}) copy-start(bf16[1024,1024]{1,0:T(8,128)(2,1)} %get-tuple-element.76) | copy-start | bytes 6291460
  551.9 4.7 copy-start.14
  561.1 5.7 copy-start.16
Sparse Core Ops, SparseCore 0:
  9.5 23.9 all-gather.8
  95.2 72.5 all-gather.4
  169.3 19.8 all-gather.6
  358.5 125.1 reduce-scatter.1

commit v6 on v5

--- a/solution.py
+++ b/solution.py
@@ -768,7 +768,7 @@
         return slice(inner + at.start, inner + at.stop)
 
     def forward(i, carry):
-        arrivals(ffn, i, {tiles - 3: lambda: grad.start(0)})
+        arrivals(ffn, i, {tiles - 2: lambda: grad.start(0)})
         tile = tile_of(i)
         slot = lax.rem(i, 2)
         keep_rows(0, ffn_all, rows_out, tile).start()

time: 586 us -> 590 us (level)
  no operation moved by 1% of the time
where the time goes in v6:
time: 590 us; the launch traced here: 581 us
  Pallas kernels  412 us (70%)
  other arithmetic  40.1 us (7%)
  waiting for transfers between devices  33.5 us (6%)
  matrix products  31.1 us (5%)
  local copies, waits for them, and re-layouts  25.2 us (4%)
  between operations  14.7 us (2%)
  starting transfers between devices  14.2 us (2%)
  blocking collectives  10.5 us (2%)
    pallas_call x2, Pallas kernels, scatter_sum(): pl.pallas_call(functools.partial(scatter_kernel, count, seq_count, arrays...  209 us
    pallas_call x1, Pallas kernels, run_experts(): pl.pallas_call(functools.partial(expert_kernel, count), out_shape=outs, i...  117 us
    pallas_call x1, Pallas kernels, gather_blocks(): pl.pallas_call(functools.partial(gather_kernel, count, groups, pieces), o...  82.1 us
    all_gather x1, waiting for transfers between devices, shards(): full_out = lax.all_gather(own_out, 'shard', axis=0, tiled=True)  26.5 us
  transfers between devices with their start and end apart: 8, of which 3 were waited for; matrix products, arithmetic and copies ran while one was open for 15% of the time, Pallas kernels for 70%

profile of v6, /device:TPU:0, one launch (start us, length us, event | category | flops | bytes accessed | tf_op | source)
XLA Modules:
  0.0 581.4 jit_solution(1710877668164076529)
XLA Ops:
  7.2 0.7 all-gather.9.cloned.1.call-update
  8.0 0.8 copy.134
  8.8 1.9 copy.133
  11.4 0.6 select_reduce_fusion.refs_1_
  12.0 0.9 fusion.19.refs_0_
  12.9 82.1 %gather_blocks_1.1 = (bf16[16,128,3200]{2,1,0:T(8,128)(2,1)}, f32[16,16,128]{2,1,0:T(8,128)}) custom-call(bf16[128,3200]{1,0:T(8,128)(2,1)} %fusion.19.refs_0_, f32[16,128]{1,0:T(8,128)} %select_reduce_fusion.refs_1_), custom_call_target="tpu_custom_call" | custom-call | tf_op jit(solution)/shard_map/gather_blocks_1/pallas_call | solution.py:305
  95.4 1.1 slice.85
  96.8 0.6 constant_dynamic-slice_fusion
  97.6 0.7 fusion.29
  98.9 1.5 fusion.3
  100.4 1.6 fusion.5.refs_1_
  102.0 6.8 %fusion.1 = f32[256,3072]{1,0:T(8,128)S(1)} fusion(bf16[256,2048]{1,0:T(8,128)(2,1)S(1)} %fusion.5.refs_1_, bf16[2048,3200]{1,0:T(8,128)(2,1)} %bitcast.145), kind=kOutput, calls=%fused_computation.1 | convolution fusion | flops 3221225472 | bytes 16777216 | tf_op jit(solution)/shard_map/dot_general | solution.py:976
  109.1 0.8 pad_maximum_fusion.4
  109.9 5.6 psum.14
  115.5 0.8 fusion.36
  116.3 0.9 multiply_bitcast_fusion.1
  118.3 2.1 subtract_convert_fusion.1
  120.5 4.0 fusion.44
  124.4 2.7 convolution_convert_fusion.2
  127.2 1.4 all_to_all.40
  128.6 0.9 copy.143
  129.5 3.6 all-to-all-start
  133.2 0.9 dynamic-slice_reduce_fusion
  134.0 1.8 reshape.329.refs_2_
  135.9 1.0 copy.170
  136.9 4.2 all-to-all-done
  141.2 26.5 %all-gather.5.cloned.1.call-done = bf16[2048,2048]{1,0:T(8,128)(2,1)} async-done(((bf16[128,2048]{1,0:T(8,128)(2,1)}), bf16[2048,2048]{1,0:T(8,128)(2,1)}) %all-gather.5.cloned.1.call-update) | async-done | bytes 8388624 | tf_op jit(solution)/shard_map/all_gather | solution.py:947
  167.7 4.7 multiply_reduce_fusion.5
  172.5 1.0 multiply_convert_fusion.3.refs_0_
  173.4 117.4 %run_experts.1 = (bf16[16,128,2048]{2,1,0:T(8,128)(2,1)}, bf16[16,128,2048]{2,1,0:T(8,128)(2,1)}, bf16[8,256,1024]{2,1,0:T(8,128)(2,1)}, bf16[8,256,2048]{2,1,0:...) custom-call(bf16[128,2048]{1,0:T(8,128)(2,1)} %multiply_convert_fusi, ...), custom_call_target="tpu_custom_call" | custom-call | tf_op jit(solution)/shard_map/run_experts/pallas_call | solution.py:861
  290.8 74.8 %scatter_sum_3.1 = (f32[128,1024]{1,0:T(8,128)}, f32[128,1024]{1,0:T(8,128)}, bf16[512,2048]{1,0:T(8,128)(2,1)}, bf16[512,2048]{1,0:T(8,128)(2,1)}, bf16[1024,10...) custom-call(bf16[16,128,1024]{2,1,0:T(8,128)(2,1)} %bitcast.159, ...), custom_call_target="tpu_custom_call" | custom-call | tf_op jit(solution)/shard_map/scatter_sum_3/pallas_call | solution.py:662
  365.6 1.3 pad_maximum_fusion.1
  367.3 0.7 copy-done.6
  368.0 1.3 fusion.39
  369.3 6.6 %convolution_convert_fusion = bf16[128,2048]{1,0:T(8,128)(2,1)S(1)} fusion(bf16[128,2048]{1,0:T(8,128)(2,1)S(1)} %get-tuple-element.90, bf16[2048,2048]{1,0:T(8,128)(2,1)} %all-gather.5.cloned.1.call-done), kind=kOutput, calls=%fused_computation.9 | convolution fusion | flops 1074003968 | bytes 9437184 | tf_op jit(solution)/shard_map/dot_general | solution.py:65
  375.9 0.8 copy.211
  376.8 4.2 all-to-all-start.1
  381.0 5.5 add_bitcast_fusion
  386.5 0.8 copy.210
  387.4 2.0 all-to-all-done.1
  389.3 4.2 all-to-all-start.2
  393.6 2.0 copy.183
  395.6 2.1 copy.156
  397.7 1.8 multiply_reduce_fusion
  399.9 0.7 copy-done.10
  400.7 0.7 fusion.13
  402.5 1.0 multiply_subtract_fusion.1
  403.6 0.8 copy-done.1
  404.4 1.0 fusion.15
  405.4 4.9 psum.15
  410.3 2.0 collective-permute-start
  412.3 3.1 convolution_convert_fusion.1
  415.4 2.1 copy.169
  417.6 0.7 pad.9.refs_8_
  418.3 3.3 multiply_convert_fusion.2
  421.5 1.2 pad_maximum_fusion.refs_2_
  422.8 0.6 broadcast_in_dim.112.refs_9_
  423.4 134.1 %scatter_sum_4.1 = (bf16[2,128,1024]{2,1,0:T(8,128)(2,1)}, bf16[2,128,1024]{2,1,0:T(8,128)(2,1)}, bf16[2,128,1024]{2,1,0:T(8,128)(2,1)}, bf16[2,128,512]{2,1,0:T...) custom-call(bf16[1024,1024]{1,0:T(8,128)(2,1)} %get-tuple-element.59, ...), custom_call_target="tpu_custom_call" | custom-call | tf_op jit(solution)/shard_map/scatter_sum_4/pallas_call | solution.py:662
  557.5 1.3 convert_reduce_fusion
  558.8 4.7 add_bitcast_fusion.1
  563.4 4.5 add_bitcast_fusion.2
  568.0 2.0 fusion.20
  570.0 3.7 place_rows.1
  573.7 0.8 copy.217
  (95 shorter events, 5.6 us)
Async XLA Ops:
  7.2 91.7 %all-gather.9.cloned.1.call-start = ((), (), s32[]{:S(2)}) async-start(), calls=%async_computation.7 | async-start | bytes 1572864 | tf_op jit(solution)/shard_map/all_gather | solution.py:952
  7.9 159.8 %all-gather.5.cloned.1.call-start = ((), (), s32[]{:S(2)}) async-start(), calls=%async_computation.4 | async-start | bytes 8912896 | tf_op jit(solution)/shard_map/all_gather | solution.py:947
  10.7 0.7 copy-start.23
  10.7 0.7 copy-start.24
  10.8 84.3 %copy-start.25 = (s32[1,3]{1,0:T(1,128)S(1)}, s32[1,3]{1,0:T(1,128)}, u32[]{:S(2)}) copy-start(s32[1,3]{1,0:T(1,128)} %param.13) | copy-start | bytes 40
  10.8 84.3 %copy-start.26 = (s32[1,3]{1,0:T(1,128)S(1)}, s32[1,3]{1,0:T(1,128)}, u32[]{:S(2)}) copy-start(s32[1,3]{1,0:T(1,128)} %param.14) | copy-start | bytes 40
  102.0 6.8 %copy-start.5 = (bf16[256,2048]{1,0:T(8,128)(2,1)}, bf16[256,2048]{1,0:T(8,128)(2,1)S(1)}, u32[]{:S(2)}) copy-start(bf16[256,2048]{1,0:T(8,128)(2,1)S(1)} %fusion.5.refs_1_) | copy-start | bytes 3145732
  108.9 15.6 %copy-start = (f32[256,3072]{1,0:T(8,128)}, f32[256,3072]{1,0:T(8,128)S(1)}, u32[]{:S(2)}) copy-start(f32[256,3072]{1,0:T(8,128)S(1)} %fusion.1) | copy-start | bytes 9437188
  116.3 1.0 copy-start.19
  116.3 1.0 copy-start.21
  127.2 8.7 %copy-start.12 = (bf16[8,128,256]{2,1,0:T(8,128)(2,1)S(1)}, bf16[8,128,256]{2,1,0:T(8,128)(2,1)}, u32[]{:S(2)}) copy-start(bf16[8,128,256]{2,1,0:T(8,128)(2,1)} %convolution_convert_fusion.2) | copy-start | bytes 1572868
  129.5 38.3 %copy-start.4 = (bf16[1,128,2048]{2,1,0:T(8,128)(2,1)S(1)}, bf16[1,128,2048]{2,1,0:T(8,128)(2,1)}, u32[]{:S(2)}) copy-start(bf16[1,128,2048]{2,1,0:T(8,128)(2,1)} %param.12) | copy-start | bytes 1572868
  129.5 11.7 %all-to-all-start = ((bf16[2,128,1024]{1,2,0:T(8,128)(2,1)}), bf16[2,128,1024]{1,2,0:T(8,128)(2,1)S(1)}, u32[]{:S(2)}, u32[]{:S(2)}) async-start(bf16[2,128,1024]{1,2,0:T(8,128)(2,1)} %copy.143), calls=%async_computation | async-start | bytes 1048576 | tf_op jit(solution)/shard_map/all_to_all | solution.py:998
  133.1 289.7 %all-gather.7.cloned.1.call-start = ((), (), s32[]{:S(2)}) async-start(), calls=%async_computation.6 | async-start | bytes 1572864 | tf_op jit(solution)/shard_map/all_gather | solution.py:999
  136.9 431.1 %reduce-scatter.2.cloned.1.call-start = ((), (), s32[]{:S(2)}) async-start(), calls=%async_computation.5 | async-start | bytes 8912896 | tf_op jit(solution)/shard_map/reduce_scatter | solution.py:1045
  366.9 1.0 copy-start.6
  376.8 12.6 %all-to-all-start.1 = ((bf16[128,2,1024]{2,0,1:T(8,128)(2,1)}), bf16[128,2,1024]{2,0,1:T(8,128)(2,1)}, u32[]{:S(2)}, u32[]{:S(2)}) async-start(bf16[128,2,1024]{2,0,1:T(8,128)(2,1)} %bitcast.143), calls=%async_computation.2 | async-start | bytes 1048576 | tf_op jit(solution)/shard_map/all_to_all | solution.py:1057
  387.3 10.3 %copy-start.7 = (f32[8,256,256]{1,2,0:T(8,128)S(1)}, f32[8,256,256]{1,2,0:T(8,128)}, u32[]{:S(2)}) copy-start(f32[8,256,256]{1,2,0:T(8,128)} %get-tuple-element.124) | copy-start | bytes 6291460
  389.3 33.4 %all-to-all-start.2 = ((bf16[128,2,1024]{2,0,1:T(8,128)(2,1)}), bf16[128,2,1024]{2,0,1:T(8,128)(2,1)}, u32[]{:S(2)}, u32[]{:S(2)}) async-start(bf16[128,2,1024]{2,0,1:T(8,128)(2,1)} %bitcast.166), calls=%async_computation.3 | async-start | bytes 1048576 | tf_op jit(solution)/shard_map/all_to_all | solution.py:1060
  399.5 1.0 copy-start.10
  399.5 1.2 copy-start.11
  400.7 1.0 copy-start.8
  400.7 1.2 copy-start.9
  402.5 1.9 copy-start.1
  402.5 1.9 copy-start.17
  402.5 1.9 copy-start.18
  402.5 1.9 copy-start.20
  402.5 1.9 copy-start.22
  403.5 1.8 copy-start.2
  403.5 1.8 copy-start.3
  410.3 153.1 %collective-permute-start = (bf16[1024,1024]{1,0:T(8,128)(2,1)}, bf16[1024,1024]{1,0:T(8,128)(2,1)}, u32[]{:S(2)}, u32[]{:S(2)}) collective-permute-start(bf16[1024,1024]{1,0:T(8,128)(2,1)} %get-tuple-element.75), channel_id=1, source_target_pairs={{0,16},{16,0},{1,17},{17,1},{2,18},{18,2},{3,19},{19,3},{4,20},{20... | collective-permute-start | bytes 6291464 | tf_op jit(solution)/shard_map/ppermute | solution.py:1083
  418.2 3.3 copy-start.13
  423.4 135.4 %copy-start.15 = (bf16[1024,1024]{1,0:T(8,128)(2,1)S(1)}, bf16[1024,1024]{1,0:T(8,128)(2,1)}, u32[]{:S(2)}) copy-start(bf16[1024,1024]{1,0:T(8,128)(2,1)} %get-tuple-element.76) | copy-start | bytes 6291460
  558.8 4.7 copy-start.14
  568.0 5.7 copy-start.16
Sparse Core Ops, SparseCore 0:
  9.5 23.9 all-gather.8
  95.2 72.5 all-gather.4
  169.3 19.8 all-gather.6
  367.1 123.0 reduce-scatter.1
